TPU v7x, 256 devices: a whole 4x4x8 slice. The times are simulated.
256 devices in a mesh: visit: 32 (over x, y, core), ccd: 8 (over z).
Axes of the slice: x: 4, y: 4, z: 8, core: 2. Of those that a mesh axis runs over, the one named last changes fastest.
Arguments:
- raw_rows: bfloat16 [128, 8192, 128], P('visit', 'ccd')
- resample: bfloat16 [128, 128, 128], P('visit')
- slot_row: int32 [32, 8, 32, 128], P('visit', 'ccd'), may hold values from 0 to 4092, as said below
- tap_weight: float32 [4, 32, 8, 32, 128], P(None, 'visit', 'ccd'), may hold values from 0 to 1
- patch_id: int32 [32, 8, 32, 128], P('visit', 'ccd'), may hold values from 0 to 15
- live_mask: int32 [32, 8, 32, 128], P('visit', 'ccd'), may hold values 0 or 1
Outputs:
- offsets: float32 [128, 64], P('visit')
- background: float32 [4096, 128], P(('visit', 'ccd'))
Inputs may be any that keep to these rules, and one draw needn't show every extreme that they name: `slot_row`: each value is v * 1024 + b with v below 4 and b at most 1020.
All inputs are finite; a program needn't handle non-finite values. No bound on the sum of `live_mask` on one device may be relied on, other than what follows from the above.
Results may differ from a plain program's by a relative error of at most 0.0041.
Values may be sent and summed in bfloat16 or wider, within the bound.
No kernel may reach another device: no remote copies, remote signals or barrier semaphores. Data moves between devices by JAX's collectives and lax.ppermute only.
A program may use at most 64 MiB of HBM per device.

v0:
```python
import jax
import jax.numpy as jnp
from jax import lax
from jax.sharding import PartitionSpec as P

ORDER = 8
TAPS = 4
ITERS = 2
P_DEV = 16


ridge_weight = 1.0


def chebyshev(coords):
    series = [jnp.ones_like(coords), coords]
    for degree in range(2, ORDER):
        series.append(2.0 * coords * series[-1] - series[-2])
    return jnp.stack(series[:ORDER])


def model_of(coef_rows, cheb_rows, cheb_x):
    shaped = coef_rows.reshape(coef_rows.shape[:-1] + (ORDER, ORDER))
    reduced = jnp.sum(shaped * cheb_rows[..., None, :], axis=-1)
    return jnp.einsum("...i,ip->...p", reduced, cheb_x, precision=lax.Precision.HIGHEST)


def solve_offsets(gram_x, design, moments):
    design_sq = design.reshape(-1, ORDER, ORDER)
    gram = jnp.einsum("ac,vbd->vabcd", gram_x, design_sq).reshape(-1, ORDER * ORDER, ORDER * ORDER)
    gram = gram + ridge_weight * jnp.eye(ORDER * ORDER, dtype=jnp.float32)
    factor = jnp.linalg.cholesky(gram)
    return jax.scipy.linalg.cho_solve((factor, True), moments[..., None])[..., 0]


def consensus(arrived, sweep_codes):
    patch_hot = (sweep_codes[..., None] == jnp.arange(P_DEV, dtype=jnp.int32)).astype(jnp.bfloat16)
    counts = jnp.sum(patch_hot.astype(jnp.float32), axis=(0, 1))
    sums = jnp.einsum("nsk,nsq->kq", patch_hot, arrived, preferred_element_type=jnp.float32)
    background = sums / (counts + 1.0)[:, None]
    returned = jnp.einsum(
        "nsk,kq->nsq",
        patch_hot,
        background.astype(jnp.bfloat16),
        preferred_element_type=jnp.float32,
    ).astype(jnp.bfloat16)
    return (background, returned)


def per_device(raw_rows, resample, slot_row, tap_weight, patch_id, live_mask):
    f32 = jnp.float32
    visit_devs = lax.axis_size("visit")
    ccd_devs = lax.axis_size("ccd")
    ccd_index = lax.axis_index("ccd")
    vis_local, rows_local, pixels = raw_rows.shape
    slots = slot_row.shape[3]
    resampled = jnp.einsum("vrp,vpq->vrq", raw_rows, resample, preferred_element_type=f32)
    resampled = resampled.reshape(vis_local * rows_local, pixels)
    starts = slot_row[0, 0]
    weights = tap_weight[:, 0, 0]
    blended = jnp.zeros((visit_devs, slots, pixels), f32)
    for tap_index in range(TAPS):
        blended = blended + weights[tap_index][..., None] * jnp.take(
            resampled, starts + tap_index, axis=0
        )
    warped = blended.astype(jnp.bfloat16)
    local_visit = starts // rows_local
    row_pos = ccd_index * rows_local + starts % rows_local
    coord_y = (2 * row_pos + TAPS).astype(f32) / float(rows_local * ccd_devs) - 1.0
    cheb_y = jnp.moveaxis(chebyshev(coord_y), 0, -1)
    cheb_x = chebyshev((2 * jnp.arange(pixels) + 1).astype(f32) / float(pixels) - 1.0)
    gram_x = jnp.dot(cheb_x, cheb_x.T, precision=lax.Precision.HIGHEST)
    live_float = live_mask[0, 0].astype(f32)
    codes = patch_id[0, 0] + P_DEV * (1 - live_mask[0, 0])
    visit_hot = (local_visit[..., None] == jnp.arange(vis_local, dtype=jnp.int32)).astype(f32)
    visit_hot = visit_hot.reshape(-1, vis_local)
    outer_y = cheb_y[..., :, None] * cheb_y[..., None, :] * live_float[..., None, None]
    design_local = jnp.dot(
        visit_hot.T, outer_y.reshape(-1, ORDER * ORDER), precision=lax.Precision.HIGHEST
    )
    offset_coefs = jnp.zeros((vis_local, ORDER * ORDER), f32)
    background = jnp.zeros((P_DEV, pixels), f32)
    for sweep in range(ITERS):
        model = model_of(jnp.take(offset_coefs, local_visit, axis=0), cheb_y, cheb_x)
        corrected = (warped.astype(f32) - model).astype(jnp.bfloat16)
        arrived, sweep_codes = (
            lax.all_to_all(corrected, "visit", split_axis=0, concat_axis=0, tiled=True),
            lax.all_to_all(codes, "visit", split_axis=0, concat_axis=0, tiled=True),
        )
        background, returned = consensus(arrived, sweep_codes)
        matched = lax.all_to_all(returned, "visit", split_axis=0, concat_axis=0, tiled=True)
        resid = (warped.astype(f32) - matched.astype(f32)) * live_float[..., None]
        projected = jnp.einsum("nsp,ip->nsi", resid, cheb_x, precision=lax.Precision.HIGHEST)
        moment_rows = (projected[..., :, None] * cheb_y[..., None, :]).reshape(-1, ORDER * ORDER)
        moments_local = jnp.dot(visit_hot.T, moment_rows, precision=lax.Precision.HIGHEST)
        design_total, moments = lax.psum((design_local, moments_local), "ccd")
        offset_coefs = solve_offsets(gram_x, design_total, moments)
    return (offset_coefs, background)


def solution(mesh):
    in_specs = (
        P("visit", "ccd", None),
        P("visit", None, None),
        P("visit", "ccd", None, None),
        P(None, "visit", "ccd", None, None),
        P("visit", "ccd", None, None),
        P("visit", "ccd", None, None),
    )
    out_specs = (P("visit", None), P(("visit", "ccd"), None))
    return jax.shard_map(
        per_device, mesh=mesh, in_specs=in_specs, out_specs=out_specs, check_vma=False
    )
```

profile of v0, /device:TPU:1, one launch (start us, length us, event | category | flops | bytes accessed | tf_op | source)
XLA Modules:
  0.0 310.0 jit_solution(6960566433343756577)
XLA Ops:
  0.6 1.4 convert_bitcast_fusion.1
  2.1 8.6 %all-to-all-start = ((s32[32,1,128]{2,1,0:T(1,128)}), s32[32,1,128]{2,1,0:T(1,128)S(1)}, u32[]{:S(2)}, u32[]{:S(2)}) async-start(s32[32,1,128]{2,1,0:T(1,128)} %bitcast.23), calls=%async_computation | async-start | bytes 32768 | tf_op jit(solution)/shard_map/all_to_all | solution.py:88
  11.4 1.3 compare_and_fusion
  15.1 1.3 fusion.74
  16.4 14.2 %gather_fusion = f32[4096,128]{1,0:T(8,128)} fusion(f32[4096,128]{1,0:T(8,128)S(1)} %bitcast.249, s32[4096]{0:T(1024)S(1)} %get-tuple-element.22), kind=kCustom, calls=%fused_computation.clone | custom fusion | bytes 4210688 | tf_op jit(solution)/shard_map/jit(_take)/gather | solution.py:63
  30.6 14.2 %gather_fusion.1 = f32[4096,128]{1,0:T(8,128)} fusion(f32[4096,128]{1,0:T(8,128)S(1)} %bitcast.250, s32[4096]{0:T(1024)S(1)} %get-tuple-element.18), kind=kCustom, calls=%fused_computation.2.clone | custom fusion | bytes 4210688 | tf_op jit(solution)/shard_map/jit(_take)/gather | solution.py:63
  44.8 14.2 %gather_fusion.2 = f32[4096,128]{1,0:T(8,128)} fusion(f32[4096,128]{1,0:T(8,128)S(1)} %bitcast.251, s32[4096]{0:T(1024)S(1)} %get-tuple-element.21), kind=kCustom, calls=%fused_computation.3.clone | custom fusion | bytes 4210688 | tf_op jit(solution)/shard_map/jit(_take)/gather | solution.py:63
  59.0 14.1 %gather_fusion.3 = f32[4096,128]{1,0:T(8,128)} fusion(f32[4096,128]{1,0:T(8,128)S(1)} %bitcast.252, s32[4096]{0:T(1024)S(1)} %get-tuple-element.19), kind=kCustom, calls=%fused_computation.4.clone | custom fusion | bytes 4210688 | tf_op jit(solution)/shard_map/jit(_take)/gather | solution.py:63
  74.1 10.8 %gather_fusion.4 = f32[4096,64]{1,0:T(8,128)S(1)} fusion(f32[4,64]{1,0:T(4,128)S(1)} %broadcast_in_dim.26, s32[4096]{0:T(1024)S(1)} %get-tuple-element.20), kind=kCustom, calls=%fused_computation.1.clone | custom fusion | bytes 2113536 | tf_op jit(solution)/shard_map/jit(_take)/gather | solution.py:84
  84.8 1.7 copy.45
  86.5 1.6 fusion.25
  88.9 7.6 %fusion.9 = bf16[32,128,128]{2,1,0:T(8,128)(2,1)S(1)} fusion(f32[32,128,128]{2,1,0:T(8,128)} %bitcast.258, f32[32,128,128]{2,1,0:T(8,128)} %bitcast.257, f32[32,128,128]{2,1,0:T(8,128)} %bitcast.256, f32[32,128,128]{2,1,0:T(8,128)} %bitcast.255, f32[32,128]{1,0:T(8,128)S(1)} %get-tuple-element.12, f32[32,128]{1,0:T(8,128)} %get-tuple-element.13, ...), kind=kLoop, calls=%fused_computation.18 | loop fusion | flops 6291456 | bytes 9519104 | tf_op jit(solution)/shard_map/convert_element_type | solution.py:66
  96.4 4.4 %fusion = bf16[32,128,128]{2,1,0:T(8,128)(2,1)} fusion(bf16[32,128,128]{2,1,0:T(8,128)(2,1)S(1)} %fusion.9, f32[32,128,8]{1,2,0:T(8,128)S(1)} %fusion.25, f32[8,128]{1,0:T(8,128)S(1)} %stack.5), kind=kOutput, calls=%fused_computation.10 | convolution fusion | flops 51904512 | bytes 2232320 | tf_op jit(solution)/shard_map/...i,ip->...p/dot_general | solution.py:25
  100.9 7.4 %all-to-all-start.1 = ((bf16[32,128,128]{2,1,0:T(8,128)(2,1)}), bf16[32,128,128]{2,1,0:T(8,128)(2,1)S(1)}, u32[]{:S(2)}, u32[]{:S(2)}) async-start(bf16[32,128,128]{2,1,0:T(8,128)(2,1)} %fusion), calls=%async_computation.1 | async-start | bytes 2097152 | tf_op jit(solution)/shard_map/all_to_all | solution.py:87
  108.4 16.7 %all-to-all-done.1 = bf16[32,128,128]{2,1,0:T(8,128)(2,1)S(1)} async-done(((bf16[32,128,128]{2,1,0:T(8,128)(2,1)}), bf16[32,128,128]{2,1,0:T(8,128)(2,1)S(1)}, u32[]{:S(2)}, u32[]{:S(2)}) %all-to-all-start.1) | async-done | bytes 1048608 | tf_op jit(solution)/shard_map/all_to_all | solution.py:87
  125.2 1.8 convolution_convert_fusion.1
  127.0 3.9 %all-to-all-start.2 = ((bf16[32,128,128]{2,1,0:T(8,128)(2,1)}), bf16[32,128,128]{2,1,0:T(8,128)(2,1)S(1)}, u32[]{:S(2)}, u32[]{:S(2)}) async-start(bf16[32,128,128]{2,1,0:T(8,128)(2,1)} %convolution_convert_fusion.1), calls=%async_computation.2 | async-start | bytes 2097152 | tf_op jit(solution)/shard_map/all_to_all | solution.py:91
  131.1 16.7 %all-to-all-done.2 = bf16[32,128,128]{2,1,0:T(8,128)(2,1)S(1)} async-done(((bf16[32,128,128]{2,1,0:T(8,128)(2,1)}), bf16[32,128,128]{2,1,0:T(8,128)(2,1)S(1)}, u32[]{:S(2)}, u32[]{:S(2)}) %all-to-all-start.2) | async-done | bytes 1048608 | tf_op jit(solution)/shard_map/all_to_all | solution.py:91
  147.8 2.3 fusion.2
  150.9 1.2 fusion.22
  152.8 1.2 convolution_bitcast_fusion.5
  154.0 25.7 %all-reduce = (f32[4,64,1]{1,0,2:T(4,128)S(1)}, f32[4,8,8]{2,1,0:T(8,128)S(1)}) all-reduce(f32[4,64,1]{1,0,2:T(4,128)S(1)} %convolution_bitcast_fusion.5, f32[4,8,8]{2,1,0:T(8,128)S(1)} %reshape.398), channel_id=1, replica_groups=mesh['visit'=32,'ccd'=8] {'ccd'}, use_global_device_ids=true, to_apply=%region_5.9 | all-reduce | flops 512 | bytes 4096 | tf_op jit(solution)/shard_map/psum | solution.py:96
  180.4 23.5 %custom-call.9 = f32[4,64,64]{2,1,0:T(8,128)S(1)} custom-call(f32[4,64,64]{2,1,0:T(8,128)S(1)} %fusion.36), custom_call_target="Cholesky" | custom-call | tf_op jit(solution)/shard_map/jit(cholesky)/cholesky | solution.py:32
  204.1 19.7 %custom-call.11 = f32[4,1,64,64]{2,3,1,0:T(8,128)S(1)} custom-call(f32[4,1,64,64]{3,2,1,0:T(8,128)S(1)} %select_bitcast_fusion), custom_call_target="InvertDiagBlocksLowerTriangular" | custom-call | tf_op jit(solution)/shard_map/jit(_cho_solve)/vmap()/triangular_solve | solution.py:33
  224.4 14.2 %gather_fusion.5 = f32[4096,64]{1,0:T(8,128)} fusion(f32[4,64]{1,0:T(4,128)S(1)} %bitcast.248, s32[4096]{0:T(1024)S(1)} %get-tuple-element.20), kind=kCustom, calls=%fused_computation.5.clone | custom fusion | bytes 2113536 | tf_op jit(solution)/shard_map/jit(_take)/gather | solution.py:84
  238.5 2.2 copy.47
  241.1 3.4 %fusion.4 = bf16[32,128,128]{2,1,0:T(8,128)(2,1)S(1)} fusion(bf16[32,128,128]{2,1,0:T(8,128)(2,1)S(1)} %fusion.9, f32[32,128,8]{1,2,0:T(8,128)S(1)} %fusion.24, f32[8,128]{1,0:T(8,128)S(1)} %stack.5), kind=kOutput, calls=%fused_computation.13 | convolution fusion | flops 51904512 | bytes 2232320 | tf_op jit(solution)/shard_map/...i,ip->...p/dot_general | solution.py:25
  244.6 27.7 %all_to_all.27 = bf16[32,128,128]{2,1,0:T(8,128)(2,1)S(1)} all-to-all(bf16[32,128,128]{2,1,0:T(8,128)(2,1)S(1)} %fusion.4), channel_id=1, replica_groups=mesh['visit'=32,'ccd'=8] {'visit'}, dimensions={0} | all-to-all | bytes 2097152 | tf_op jit(solution)/shard_map/all_to_all | solution.py:87
  273.2 20.6 %all_to_all.28 = bf16[32,128,128]{2,1,0:T(8,128)(2,1)S(1)} all-to-all(bf16[32,128,128]{2,1,0:T(8,128)(2,1)S(1)} %convolution_convert_fusion), channel_id=1, replica_groups=mesh['visit'=32,'ccd'=8] {'visit'}, dimensions={0} | all-to-all | bytes 2097152 | tf_op jit(solution)/shard_map/all_to_all | solution.py:91
  293.9 2.3 fusion.6
  297.0 1.2 convolution_bitcast_fusion.3
  298.1 10.7 %psum.26 = f32[4,64,1]{1,0,2:T(4,128)S(1)} all-reduce(f32[4,64,1]{1,0,2:T(4,128)S(1)} %convolution_bitcast_fusion.3), channel_id=1, replica_groups=mesh['visit'=32,'ccd'=8] {'ccd'}, use_global_device_ids=true, to_apply=%region_7.12 | all-reduce | flops 256 | bytes 2048 | tf_op jit(solution)/shard_map/psum | solution.py:96
  (59 shorter events, 11.2 us)
Async XLA Ops:
  0.6 14.5 %copy-start = (bf16[4,1024,128]{2,1,0:T(8,128)(2,1)S(1)}, bf16[4,1024,128]{2,1,0:T(8,128)(2,1)}, u32[]{:S(2)}) copy-start(bf16[4,1024,128]{2,1,0:T(8,128)(2,1)} %param.13) | copy-start | bytes 3145732
  2.1 98.8 %all-to-all-start = ((s32[32,1,128]{2,1,0:T(1,128)}), s32[32,1,128]{2,1,0:T(1,128)S(1)}, u32[]{:S(2)}, u32[]{:S(2)}) async-start(s32[32,1,128]{2,1,0:T(1,128)} %bitcast.23), calls=%async_computation | async-start | bytes 32768 | tf_op jit(solution)/shard_map/all_to_all | solution.py:88
  59.0 14.2 %copy-start.2 = (f32[4,1,1,32,128]{4,3,2,1,0:T(8,128)S(1)}, f32[4,1,1,32,128]{4,3,2,1,0:T(8,128)}, u32[]{:S(2)}) copy-start(f32[4,1,1,32,128]{4,3,2,1,0:T(8,128)} %param.16) | copy-start | bytes 196612
  59.0 14.8 %copy-start.1 = (s32[1,1,32,128]{3,2,1,0:T(8,128)S(1)}, s32[1,1,32,128]{3,2,1,0:T(8,128)}, u32[]{:S(2)}) copy-start(s32[1,1,32,128]{3,2,1,0:T(8,128)} %param.15) | copy-start | bytes 49156
  100.9 24.3 %all-to-all-start.1 = ((bf16[32,128,128]{2,1,0:T(8,128)(2,1)}), bf16[32,128,128]{2,1,0:T(8,128)(2,1)S(1)}, u32[]{:S(2)}, u32[]{:S(2)}) async-start(bf16[32,128,128]{2,1,0:T(8,128)(2,1)} %fusion), calls=%async_computation.1 | async-start | bytes 2097152 | tf_op jit(solution)/shard_map/all_to_all | solution.py:87
  108.4 18.5 %copy-start.4 = (f32[16]{0:T(128)}, f32[16]{0:T(128)S(1)}, u32[]{:S(2)}) copy-start(f32[16]{0:T(128)S(1)} %broadcast_add_fusion.1) | copy-start | bytes 196
  127.0 20.8 %all-to-all-start.2 = ((bf16[32,128,128]{2,1,0:T(8,128)(2,1)}), bf16[32,128,128]{2,1,0:T(8,128)(2,1)S(1)}, u32[]{:S(2)}, u32[]{:S(2)}) async-start(bf16[32,128,128]{2,1,0:T(8,128)(2,1)} %convolution_convert_fusion.1), calls=%async_computation.2 | async-start | bytes 2097152 | tf_op jit(solution)/shard_map/all_to_all | solution.py:91
  241.1 31.1 %copy-start.5 = (f32[16]{0:T(128)S(1)}, f32[16]{0:T(128)}, u32[]{:S(2)}) copy-start(f32[16]{0:T(128)} %copy-done.4) | copy-start | bytes 196
  272.5 23.7 %copy-start.3 = (f32[16,128]{1,0:T(8,128)}, f32[16,128]{1,0:T(8,128)S(1)}, u32[]{:S(2)}) copy-start(f32[16,128]{1,0:T(8,128)S(1)} %fusion.14) | copy-start | bytes 24580
where the time goes:
time: 313 us; the launch traced here: 310 us
  local copies, waits for them, and re-layouts  89.3 us (29%)
  blocking collectives  84.7 us (27%)
  other arithmetic  59.7 us (19%)
  waiting for transfers between devices  33.5 us (11%)
  matrix products  21.9 us (7%)
  starting transfers between devices  19.9 us (6%)
    gather x4, local copies, waits for them, and re-layouts, per_device(): jnp.take(resampled, starts + tap_index, axis=0)  56.7 us
    psum x2, blocking collectives, per_device(): design_total, moments = lax.psum((design_local, moments_local), 'ccd')  36.4 us
    gather x4, local copies, waits for them, and re-layouts, per_device(): jnp.take(offset_coefs, local_visit, axis=0)  28.8 us
    all_to_all x1, blocking collectives, per_device(): lax.all_to_all(corrected, 'visit', split_axis=0, concat_axis=0, tiled=True)  27.7 us
    another operation x4, other arithmetic, solve_offsets(): factor = jnp.linalg.cholesky(gram)  23.6 us
    all_to_all x1, blocking collectives, per_device(): lax.all_to_all(returned, 'visit', split_axis=0, concat_axis=0, tiled=True)  20.6 us
    another operation x3, other arithmetic, solve_offsets(): jax.scipy.linalg.cho_solve((factor, True), moments[..., None])[..., 0]  19.8 us
    all_to_all x1, waiting for transfers between devices, per_device(): lax.all_to_all(corrected, 'visit', split_axis=0, concat_axis=0, tiled=True)  16.7 us
  transfers between devices with their start and end apart: 3, of which 2 were waited for; matrix products, arithmetic and copies ran while one was open for 29% of the time, Pallas kernels for 0%

commit v1 on v0

v1 whole, which is shorter than its diff:
```python
import functools

import jax
import jax.numpy as jnp
import numpy as np
from jax import lax
from jax.experimental import pallas as pl
from jax.experimental.pallas import tpu as pltpu
from jax.sharding import PartitionSpec as P

ORDER = 8
TAPS = 4
P_DEV = 16
RIDGE = 1.0
HI = lax.Precision.HIGHEST
F32 = jnp.float32
BF16 = jnp.bfloat16
VMEM = pl.BlockSpec(memory_space=pltpu.VMEM)
SMEM = pl.BlockSpec(memory_space=pltpu.SMEM)


def constants(pixels):
    x = (2 * np.arange(pixels) + 1) / pixels - 1.0
    cx = [np.ones_like(x), x]
    for _ in range(2, ORDER):
        cx.append(2 * x * cx[-1] - cx[-2])
    cx = np.stack(cx)
    lam, rot = np.linalg.eigh(cx @ cx.T)
    return lam, rot, rot.T @ cx


def dot(a, b, precision=None):
    return lax.dot_general(
        a, b, (((1,), (0,)), ((), ())), precision=precision, preferred_element_type=F32
    )


def dot_t(a, b, precision=None):
    return lax.dot_general(
        a, b, (((1,), (1,)), ((), ())), precision=precision, preferred_element_type=F32
    )


def iota(shape, dim):
    return lax.broadcasted_iota(jnp.int32, shape, dim)


def cheb_rows(y, count):
    sub = iota(y.shape, 0)
    prev, cur = jnp.ones_like(y), y
    out = jnp.where(sub == 0, prev, cur)
    for k in range(2, count):
        prev, cur = cur, 2.0 * y * cur - prev
        out = jnp.where(sub == k, cur, out)
    return out


def coord(b_pos, ccd, rows_local, ccd_devs):
    base = (ccd * rows_local).astype(F32)
    return (2.0 * (base + b_pos) + float(TAPS)) / float(rows_local * ccd_devs) - 1.0


def gather_kernel(
    ccd_devs, rows_smem, raw_ref, res_ref, srow_ref, w_ref, pid_ref, live_ref, cxt_ref,
    pay_ref, t_ref, q_ref, res_sc, row_sc, code_sc, wi_sc, h_sc,
):
    vis, rows, pix = raw_ref.shape
    owners, slots = srow_ref.shape
    wide = slots * TAPS
    ccd = lax.axis_index("ccd")
    for v in range(vis):
        res_sc[pl.ds(8 + v * rows, rows), :] = dot(raw_ref[v], res_ref[v])
    off = iota((slots, wide), 1) - TAPS * iota((slots, wide), 0)
    rep = jnp.where((off >= 0) & (off < TAPS), 1.0, 0.0).astype(BF16)
    srow = srow_ref[...]
    code = pid_ref[...] + P_DEV * (1 - live_ref[...])
    high, low = srow >> 8, srow & 255
    row_sc[...] = 256.0 * dot(high.astype(F32).astype(BF16), rep) + dot(
        low.astype(F32).astype(BF16), rep
    )
    code_sc[...] = dot(code.astype(F32).astype(BF16), rep)
    wi = None
    for t in range(TAPS):
        pick = jnp.where(off == t, 1.0, 0.0).astype(BF16)
        part = dot(w_ref[t].astype(BF16), pick)
        wi = part if wi is None else wi + part
    wi_sc[...] = wi
    q_ref[...] = jnp.zeros_like(q_ref)
    half = iota((8, pix), 0) < TAPS
    kid = iota((P_DEV, wide), 0).astype(F32)
    kid_s = iota((P_DEV, slots), 0)

    def body(j, carry):
        pieces = []
        for g in range(slots // 4):
            pair = []
            for h in range(2):
                s = 4 * g + 2 * h
                first = res_sc[pl.ds(rows_smem[j, s] + 8, 8), :]
                second = res_sc[pl.ds(rows_smem[j, s + 1] + 4, 8), :]
                pair.append(jnp.where(half, first, second))
            pieces.append(jnp.concatenate(pair, axis=0).astype(BF16))
        taps = jnp.concatenate(pieces, axis=0)
        row = row_sc[pl.ds(j, 1), :]
        cod = code_sc[pl.ds(j, 1), :]
        wgt = wi_sc[pl.ds(j, 1), :]
        visit = jnp.floor(row * (1.0 / rows))
        y = coord(row - visit * rows, ccd, rows, ccd_devs)
        ty = cheb_rows(jnp.broadcast_to(y, (ORDER, wide)), ORDER)
        ty = ty * jnp.where(cod < float(P_DEV), wgt, 0.0)
        lhs = [jnp.where(cod == kid, wgt, 0.0)]
        for v in range(vis):
            lhs.append(jnp.where(visit == float(v), ty, 0.0))
        lhs = jnp.concatenate(lhs, axis=0).astype(BF16)
        sums = dot(lhs, taps)
        t_ref[pl.ds(pl.multiple_of(j * P_DEV, P_DEV), P_DEV), :] = sums[:P_DEV]
        q_ref[...] += sums[P_DEV:]
        live = live_ref[pl.ds(j, 1), :]
        member = jnp.where((pid_ref[pl.ds(j, 1), :] == kid_s) & (live > 0), 1.0, 0.0)
        h_sc[pl.ds(pl.multiple_of(j * P_DEV, P_DEV), P_DEV), :] = member
        return carry

    lax.fori_loop(0, owners, body, 0)
    proj = dot_t(cxt_ref[...], t_ref[...], HI)
    counts = dot_t(jnp.ones((8, slots), BF16), h_sc[...].astype(BF16))
    blocks = owners * P_DEV // 128
    sub = iota((16, 128), 0)
    rows_out = [proj[:, 128 * q : 128 * (q + 1)] for q in range(blocks)]
    tail = jnp.zeros((16, 128), F32)
    for q in range(blocks):
        tail = jnp.where(sub == q, counts[0:1, 128 * q : 128 * (q + 1)], tail)
    block = jnp.concatenate(rows_out + [tail], axis=0).astype(BF16)
    for i in range(owners):
        pay_ref[i] = block


def design_kernel(
    ccd_devs, rows, srow_ref, pid_ref, live_ref, q_ref, cxt_ref, mt_ref, qb_ref, sy_ref, m_sc
):
    owners, slots = srow_ref.shape
    vis = q_ref.shape[0] // ORDER
    ccd = lax.axis_index("ccd")
    kid = iota((P_DEV, slots), 0)
    m_sc[...] = jnp.zeros_like(m_sc)

    def body(j, acc):
        srow = srow_ref[pl.ds(j, 1), :]
        live = live_ref[pl.ds(j, 1), :]
        pid = pid_ref[pl.ds(j, 1), :]
        visit = srow // rows
        y = coord((srow - visit * rows).astype(F32), ccd, rows, ccd_devs)
        ty = cheb_rows(jnp.broadcast_to(y, (ORDER, slots)), ORDER)
        member = jnp.where((pid == kid) & (live > 0), 1.0, 0.0)
        vt = jnp.concatenate(
            [jnp.where((visit == v) & (live > 0), ty, 0.0) for v in range(vis)], axis=0
        )
        both = dot_t(jnp.concatenate([member, ty], axis=0), vt, HI)
        m_sc[pl.ds(pl.multiple_of(j * P_DEV, P_DEV), P_DEV), 0 : vis * ORDER] = both[:P_DEV]
        return acc + both[P_DEV:]

    sy = lax.fori_loop(0, owners, body, jnp.zeros((ORDER, vis * ORDER), F32))
    sy_ref[...] = jnp.concatenate([sy, jnp.zeros((ORDER, 128 - vis * ORDER), F32)], axis=1)
    mt_ref[...] = m_sc[...].T[: vis * ORDER]
    qb_ref[...] = blocks_of(dot_t(q_ref[...], tile_rows(cxt_ref[...], 128 // ORDER), HI), vis)


def tile_rows(x, times):
    return jnp.concatenate([x] * times, axis=0)


def blocks_of(full, vis):
    lane = iota((ORDER, full.shape[1]), 1) // ORDER
    out = jnp.zeros((ORDER, full.shape[1]), F32)
    for v in range(vis):
        out = out + jnp.where(lane == v, full[v * ORDER : (v + 1) * ORDER], 0.0)
    return out


def moments_block(mt, back, q, vis):
    full = None
    for i, piece in enumerate(back):
        part = dot_t(mt[:, 128 * i : 128 * (i + 1)], tile_rows(piece, 128 // ORDER), HI)
        full = part if full is None else full + part
    return q - blocks_of(full, vis)


def senders_sum(ref, lo, hi):
    total = ref[0, lo:hi].astype(F32)
    for i in range(1, ref.shape[0]):
        total = total + ref[i, lo:hi].astype(F32)
    return total


def first_kernel(arr_ref, mt_ref, qb_ref, sy_ref, b_ref, den_ref, pay_ref):
    blocks = b_ref.shape[1] // 128
    vis = mt_ref.shape[0] // ORDER
    total = senders_sum(arr_ref, 0, arr_ref.shape[1])
    back = []
    for q in range(blocks):
        den = total[ORDER * blocks + q : ORDER * blocks + q + 1] + 1.0
        den = jnp.broadcast_to(den, (ORDER, 128))
        piece = total[ORDER * q : ORDER * (q + 1)] / den
        den_ref[:, 128 * q : 128 * (q + 1)] = den
        b_ref[:, 128 * q : 128 * (q + 1)] = piece
        back.append(piece)
    mom = moments_block(mt_ref[...], back, qb_ref[...], vis)
    block = jnp.concatenate([mom, sy_ref[...]], axis=0)
    for i in range(pay_ref.shape[0]):
        pay_ref[i] = block


def solve(mom, sy, lam, vis):
    n = vis * ORDER
    rows, lanes = iota((n, ORDER * 128), 0), iota((n, ORDER * 128), 1)
    pos = lanes % 128
    pick = (rows // ORDER == pos // ORDER) & (rows % ORDER == lanes // 128)
    spread = dot(sy[:, :n], jnp.where(pick, 1.0, 0.0), HI)
    sub = iota((ORDER, 128), 0)
    mat = [
        spread[:, 128 * b : 128 * (b + 1)] * lam + jnp.where(sub == b, RIDGE, 0.0)
        for b in range(ORDER)
    ]
    rhs = [mom[b : b + 1] for b in range(ORDER)]
    for p in range(ORDER):
        inv = 1.0 / mat[p][p : p + 1]
        mat[p] = mat[p] * inv
        rhs[p] = rhs[p] * inv
        for b in range(ORDER):
            if b != p:
                factor = mat[b][p : p + 1]
                mat[b] = mat[b] - factor * mat[p]
                rhs[b] = rhs[b] - factor * rhs[p]
    out = jnp.zeros((ORDER, 128), F32)
    for b in range(ORDER):
        out = jnp.where(sub == b, rhs[b], out)
    return jnp.where(iota((ORDER, 128), 1) < n, out, 0.0)


def block_diag_t(z, vis):
    n = vis * ORDER
    tiled = tile_rows(z, vis)
    keep = iota((n, 128), 0) // ORDER == iota((n, 128), 1) // ORDER
    return jnp.where(keep, tiled, 0.0).T[:n]


def model_kernel(arr_ref, lam_ref, mt_ref, m_ref, t_ref, cxt_ref, sy_ref, pay_ref):
    vis = mt_ref.shape[0] // ORDER
    total = arr_ref[0]
    for i in range(1, arr_ref.shape[0]):
        total = total + arr_ref[i]
    sy_ref[...] = total[ORDER:]
    z = solve(total[:ORDER], total[ORDER:], lam_ref[0:1], vis)
    diag = block_diag_t(z, vis)
    weights = diag[:ORDER]
    for v in range(1, vis):
        weights = weights + diag[v * ORDER : (v + 1) * ORDER]
    model = dot(weights, mt_ref[...], HI)
    surface = lax.dot_general(
        weights, cxt_ref[...], (((0,), (0,)), ((), ())), precision=HI, preferred_element_type=F32
    )
    surface = jnp.concatenate([surface, jnp.zeros((128 - vis * ORDER, 128), F32)], axis=0)
    corrected = t_ref[...] - dot(m_ref[...], surface, HI)
    blocks = model.shape[1] // 128
    block = jnp.concatenate(
        [model[:, 128 * q : 128 * (q + 1)] for q in range(blocks)], axis=0
    ).astype(BF16)
    rows = ORDER * blocks
    for i in range(pay_ref.shape[0]):
        pay_ref[i, 0:rows] = block
        pay_ref[i, rows : rows + P_DEV] = corrected[P_DEV * i : P_DEV * (i + 1)].astype(BF16)


def second_kernel(arr_ref, b_ref, den_ref, mt_ref, qb_ref, lam_ref, pay_ref):
    blocks = b_ref.shape[1] // 128
    vis = mt_ref.shape[0] // ORDER
    total = senders_sum(arr_ref, 0, ORDER * blocks)
    lam = lam_ref[:, 0:1]
    back = []
    for q in range(blocks):
        cols = slice(128 * q, 128 * (q + 1))
        model = total[ORDER * q : ORDER * (q + 1)]
        back.append(b_ref[:, cols] - lam * model / den_ref[:, cols])
    mom = moments_block(mt_ref[...], back, qb_ref[...], vis)
    for i in range(pay_ref.shape[0]):
        pay_ref[i] = mom


def background_kernel(arr_ref, den_ref, out_ref):
    rows = arr_ref.shape[1] - P_DEV
    sums = senders_sum(arr_ref, rows, rows + P_DEV)
    own = lax.axis_index("visit") * P_DEV
    width = den_ref.shape[1]
    pick = iota((P_DEV, width), 1) == iota((P_DEV, width), 0) + own
    den = dot_t(jnp.where(pick, 1.0, 0.0), den_ref[...], HI)
    out_ref[...] = sums / den[:, 0:1]


def final_kernel(arr_ref, sy_ref, lam_ref, rot_ref, out_ref):
    vis = out_ref.shape[0]
    n = vis * ORDER
    total = arr_ref[0]
    for i in range(1, arr_ref.shape[0]):
        total = total + arr_ref[i]
    z = solve(total, sy_ref[...], lam_ref[0:1], vis)
    zt = z.T[:n]
    coef = jnp.concatenate(
        [dot(rot_ref[...], zt[v * ORDER : (v + 1) * ORDER], HI) for v in range(vis)], axis=0
    )
    wide = ORDER * ORDER
    spread = jnp.where(iota((ORDER, wide), 1) % ORDER == iota((ORDER, wide), 0), 1.0, 0.0)
    flat = dot(coef, spread, HI)
    keep = iota((n, wide), 1) // ORDER == iota((n, wide), 0) % ORDER
    flat = jnp.where(keep, flat, 0.0)
    for v in range(vis):
        out_ref[v : v + 1] = jnp.sum(flat[v * ORDER : (v + 1) * ORDER], axis=0, keepdims=True)


def call(kernel, out_shape, scratch=(), n_in=1, smem=()):
    return pl.pallas_call(
        kernel,
        out_shape=out_shape,
        in_specs=[SMEM if i in smem else VMEM for i in range(n_in)],
        out_specs=jax.tree.map(lambda _: VMEM, out_shape),
        scratch_shapes=list(scratch),
    )


def shape(dims, dtype=F32):
    return jax.ShapeDtypeStruct(dims, dtype)


def exchange(x, axis):
    return lax.all_to_all(x, axis, split_axis=0, concat_axis=0, tiled=True)


def per_device(raw_rows, resample, slot_row, tap_weight, patch_id, live_mask):
    owners = lax.axis_size("visit")
    ccd_devs = lax.axis_size("ccd")
    vis, rows, pix = raw_rows.shape
    slots = slot_row.shape[3]
    patches = owners * P_DEV
    blocks = patches // 128
    nvb = vis * ORDER
    lam, rot, cxt = constants(pix)
    lam_lane = np.zeros((8, 128))
    lam_lane[0, :nvb] = np.tile(lam, vis)
    lam_sub = np.broadcast_to(lam[:, None], (8, 128))
    lam_lane, lam_sub = jnp.asarray(lam_lane, F32), jnp.asarray(lam_sub, F32)
    cxt, rot = jnp.asarray(cxt, F32), jnp.asarray(rot, F32)
    srow, pid, live = slot_row[0, 0], patch_id[0, 0], live_mask[0, 0]
    weights = tap_weight[:, 0, 0]
    pay_rows = ORDER * blocks + P_DEV

    pay1, tsum, qsum = call(
        functools.partial(gather_kernel, ccd_devs),
        (
            shape((owners, pay_rows, 128), BF16),
            shape((patches, pix)),
            shape((nvb, pix)),
        ),
        scratch=(
            pltpu.VMEM((vis * rows + 16, pix), F32),
            pltpu.VMEM((owners, slots * TAPS), F32),
            pltpu.VMEM((owners, slots * TAPS), F32),
            pltpu.VMEM((owners, slots * TAPS), F32),
            pltpu.VMEM((patches, slots), F32),
        ),
        n_in=8,
        smem=(0,),
    )(srow, raw_rows, resample, srow, weights, pid, live, cxt)
    arr1 = exchange(pay1, "visit")
    mt, qb, sy, m = call(
        functools.partial(design_kernel, ccd_devs, rows),
        (
            shape((nvb, patches)),
            shape((ORDER, 128)),
            shape((ORDER, 128)),
            shape((patches, 128)),
        ),
        n_in=5,
    )(srow, pid, live, qsum, cxt)
    back, den, pay2 = call(
        first_kernel,
        (
            shape((ORDER, patches)),
            shape((ORDER, patches)),
            shape((ccd_devs, 2 * ORDER, 128)),
        ),
        n_in=4,
    )(arr1, mt, qb, sy)
    arr2 = exchange(pay2, "ccd")
    sy_all, pay3 = call(
        model_kernel,
        (shape((ORDER, 128)), shape((owners, pay_rows, 128), BF16)),
        n_in=6,
    )(arr2, lam_lane, mt, m, tsum, cxt)
    arr3 = exchange(pay3, "visit")
    pay4 = call(
        second_kernel,
        shape((ccd_devs, ORDER, 128)),
        n_in=6,
    )(arr3, back, den, mt, qb, lam_sub)
    arr4 = exchange(pay4, "ccd")
    background = call(background_kernel, shape((P_DEV, pix)), n_in=2)(arr3, den)
    offsets = call(final_kernel, shape((vis, ORDER * ORDER)), n_in=4)(
        arr4, sy_all, lam_lane, rot
    )
    return offsets, background


def solution(mesh):
    in_specs = (
        P("visit", "ccd", None),
        P("visit", None, None),
        P("visit", "ccd", None, None),
        P(None, "visit", "ccd", None, None),
        P("visit", "ccd", None, None),
        P("visit", "ccd", None, None),
    )
    out_specs = (P("visit", None), P(("visit", "ccd"), None))
    return jax.shard_map(
        per_device, mesh=mesh, in_specs=in_specs, out_specs=out_specs, check_vma=False
    )
```

time: 313 us -> 84 us (0.27)
  local copies, waits for them, and re-layouts: 89.3 us -> 1.37 us
  other arithmetic: 59.7 us -> 0 us
  blocking collectives: 84.7 us -> 32.1 us
  Pallas kernels: 0 us -> 29.8 us
  waiting for transfers between devices: 33.5 us -> 7.6 us
  matrix products: 21.9 us -> 0 us
  starting transfers between devices: 19.9 us -> 11.9 us
    gather x8 -> x0, local copies, waits for them, and re-layouts: 85.5 us -> none  [the longest x4 56.7 us: per_device(): jnp.take(resampled, starts + tap_index, axis=0)]
    another operation x8 -> x0, other arithmetic: 43.4 us -> none  [the longest x4 23.6 us: solve_offsets(): factor = jnp.linalg.cholesky(gram)]
    psum x2 -> x0, blocking collectives: 36.4 us -> none  [per_device(): design_total, moments = lax.psum((design_local, moments_local), 'ccd')]
    pallas_call x0 -> x7, Pallas kernels: none -> 29.8 us  [the longest x1 11 us: per_device(): call(functools.partial(gather_kernel, ccd_devs), (shape((owners, pay_rows...]
    all_to_all x3 -> x2, waiting for transfers between devices: 33.5 us -> 7.6 us  [exchange(): return lax.all_to_all(x, axis, split_axis=0, concat_axis=0, tiled=True)]
    dot_general x12 -> x0, matrix products: 20.2 us -> none  [the longest x2 7.86 us: model_of(): jnp.einsum('...i,ip->...p', reduced, cheb_x, precision=lax.Precision.HIGH...]
    all_to_all x2, blocking collectives: 48.3 us -> 32.1 us  [exchange(): return lax.all_to_all(x, axis, split_axis=0, concat_axis=0, tiled=True)]
    convert_element_type x3 -> x0, other arithmetic: 9.04 us -> none  [the longest x1 7.58 us: per_device(): warped = blended.astype(jnp.bfloat16)]
  transfers between devices with their start and end apart: 3 -> 2, of which waited for: 2 -> 2; matrix products, arithmetic and copies ran while one was open for 29% -> 0% of each run, Pallas kernels for 0% -> 11%
where the time goes in v1:
time: 84 us; the launch traced here: 83.4 us
  blocking collectives  32.1 us (38%)
  Pallas kernels  29.8 us (35%)
  starting transfers between devices  11.9 us (14%)
  waiting for transfers between devices  7.6 us (9%)
  local copies, waits for them, and re-layouts  1.37 us (2%)
    all_to_all x2, blocking collectives, exchange(): return lax.all_to_all(x, axis, split_axis=0, concat_axis=0, tiled=True)  32.1 us
    all_to_all x2, starting transfers between devices, exchange(): return lax.all_to_all(x, axis, split_axis=0, concat_axis=0, tiled=True)  11.9 us
    pallas_call x1, Pallas kernels, per_device(): call(functools.partial(gather_kernel, ccd_devs), (shape((owners, pay_rows...  11 us
    pallas_call x1, Pallas kernels, per_device(): call(functools.partial(design_kernel, ccd_devs, rows), (shape((nvb, patch...  7.62 us
    all_to_all x2, waiting for transfers between devices, exchange(): return lax.all_to_all(x, axis, split_axis=0, concat_axis=0, tiled=True)  7.6 us
    pallas_call x1, Pallas kernels, per_device(): call(model_kernel, (shape((ORDER, 128)), shape((owners, pay_rows, 128), B...  2.79 us
    pallas_call x1, Pallas kernels, per_device(): call(second_kernel, shape((ccd_devs, ORDER, 128)), n_in=6)  2.26 us
    pallas_call x1, Pallas kernels, per_device(): call(first_kernel, (shape((ORDER, patches)), shape((ORDER, patches)), sha...  2.24 us
  transfers between devices with their start and end apart: 2, of which 2 were waited for; matrix products, arithmetic and copies ran while one was open for 0% of the time, Pallas kernels for 11%

profile of v1, /device:TPU:1, one launch (start us, length us, event | category | flops | bytes accessed | tf_op | source)
XLA Modules:
  0.0 83.4 jit_solution(159738617830837911)
XLA Ops:
  0.6 11.0 %shard_map.113 = (bf16[32,48,128]{2,1,0:T(8,128)(2,1)}, f32[512,128]{1,0:T(8,128)}, f32[32,128]{1,0:T(8,128)}) custom-call(s32[32,128]{1,0:T(8,128)} %bitcast.4, bf16[4,1024,128]{2,1,0:T(8,128)(2,1)} %raw_ref.1, bf16[4,128,128]{2,1,0:T(8,128)(2,1)} %res_ref.1, s32[32,128]{1,0:T(8,128)} %bitcast.5, f32[4,32,128]{2,1,0:T(8,128)} %bitcast.11, ...), custom_call_target="tpu_custom_call" | custom-call | tf_op jit(solution)/shard_map/pallas_call | solution.py:354
  11.7 8.6 %all-to-all-start = ((bf16[32,48,128]{2,1,0:T(8,128)(2,1)}), bf16[32,48,128]{2,1,0:T(8,128)(2,1)S(1)}, u32[]{:S(2)}, u32[]{:S(2)}) async-start(bf16[32,48,128]{2,1,0:T(8,128)(2,1)} %get-tuple-element.14), calls=%async_computation | async-start | bytes 786432 | tf_op jit(solution)/shard_map/all_to_all | solution.py:333
  20.2 7.6 %shard_map.114 = (f32[32,512]{1,0:T(8,128)}, f32[8,128]{1,0:T(8,128)}, f32[8,128]{1,0:T(8,128)}, f32[512,128]{1,0:T(8,128)}) custom-call(s32[32,128]{1,0:T(8,128)} %bitcast.6, s32[32,128]{1,0:T(8,128)} %bitcast.8, s32[32,128]{1,0:T(8,128)} %bitcast.10, f32[32,128]{1,0:T(8,128)} %get-tuple-element.15.q_ref, f32[8,128]{1,0:T(8,128)} %constant.10.clone.cxt_ref), custom_call_target="tpu_custom_call" | custom-call | tf_op jit(solution)/shard_map/pallas_call | solution.py:372
  27.9 2.7 %all-to-all-done.arr_ref = bf16[32,48,128]{2,1,0:T(8,128)(2,1)S(1)} async-done(((bf16[32,48,128]{2,1,0:T(8,128)(2,1)}), bf16[32,48,128]{2,1,0:T(8,128)(2,1)S(1)}, u32[]{:S(2)}, u32[]{:S(2)}) %all-to-all-start) | async-done | bytes 393248 | tf_op jit(solution)/shard_map/all_to_all | solution.py:333
  30.5 0.0 copy-start
  30.5 0.8 copy-done
  31.3 2.2 %shard_map.115 = (f32[8,512]{1,0:T(8,128)}, f32[8,512]{1,0:T(8,128)}, f32[8,16,128]{2,1,0:T(8,128)}) custom-call(bf16[32,48,128]{2,1,0:T(8,128)(2,1)} %copy-done, f32[32,512]{1,0:T(8,128)} %get-tuple-element.16.mt_ref, f32[8,128]{1,0:T(8,128)} %get-tuple-element.17.qb_ref, f32[8,128]{1,0:T(8,128)} %get-tuple-element.18.sy_ref), custom_call_target="tpu_custom_call" | custom-call | tf_op jit(solution)/shard_map/pallas_call | solution.py:382
  33.5 15.4 %all_to_all.20.arr_ref = f32[8,16,128]{2,1,0:T(8,128)} all-to-all(f32[8,16,128]{2,1,0:T(8,128)} %get-tuple-element.19), channel_id=1, replica_groups=mesh['visit'=32,'ccd'=8] {'ccd'}, dimensions={0} | all-to-all | bytes 131072 | tf_op jit(solution)/shard_map/all_to_all | solution.py:333
  48.9 2.8 %shard_map.116 = (f32[8,128]{1,0:T(8,128)}, bf16[32,48,128]{2,1,0:T(8,128)(2,1)}) custom-call(f32[8,16,128]{2,1,0:T(8,128)} %all_to_all.20.arr_ref, f32[8,128]{1,0:T(8,128)} %constant.8.clone.lam_ref, f32[32,512]{1,0:T(8,128)} %get-tuple-element.16.mt_ref, f32[512,128]{1,0:T(8,128)} %get-tuple-element.20.m_ref, f32[512,128]{1,0:T(8,128)} %get-tuple-element.21.t_ref, ...), custom_call_target="tpu_custom_call" | custom-call | tf_op jit(solution)/shard_map/pallas_call | solution.py:392
  51.7 16.6 %all_to_all.21.arr_ref = bf16[32,48,128]{2,1,0:T(8,128)(2,1)} all-to-all(bf16[32,48,128]{2,1,0:T(8,128)(2,1)} %get-tuple-element.22), channel_id=1, replica_groups=mesh['visit'=32,'ccd'=8] {'visit'}, dimensions={0} | all-to-all | bytes 786432 | tf_op jit(solution)/shard_map/all_to_all | solution.py:333
  68.4 2.3 %shard_map.117 = f32[8,8,128]{2,1,0:T(8,128)} custom-call(bf16[32,48,128]{2,1,0:T(8,128)(2,1)} %all_to_all.21.arr_ref, f32[8,512]{1,0:T(8,128)} %get-tuple-element.23.b_ref, f32[8,512]{1,0:T(8,128)} %get-tuple-element.24.den_ref, f32[32,512]{1,0:T(8,128)} %get-tuple-element.16.mt_ref, f32[8,128]{1,0:T(8,128)} %get-tuple-element.17.qb_ref, ...), custom_call_target="tpu_custom_call" | custom-call | tf_op jit(solution)/shard_map/pallas_call | solution.py:398
  70.6 3.3 %all-to-all-start.3 = ((f32[8,8,128]{2,1,0:T(8,128)}), f32[8,8,128]{2,1,0:T(8,128)S(1)}, u32[]{:S(2)}, u32[]{:S(2)}) async-start(f32[8,8,128]{2,1,0:T(8,128)} %shard_map.117), calls=%async_computation.3 | async-start | bytes 65536 | tf_op jit(solution)/shard_map/all_to_all | solution.py:333
  74.0 1.8 %shard_map.119 = f32[16,128]{1,0:T(8,128)} custom-call(bf16[32,48,128]{2,1,0:T(8,128)(2,1)} %all_to_all.21.arr_ref, f32[8,512]{1,0:T(8,128)} %get-tuple-element.24.den_ref), custom_call_target="tpu_custom_call" | custom-call | tf_op jit(solution)/shard_map/pallas_call | solution.py:404
  75.8 4.9 %all-to-all-done.3.arr_ref = f32[8,8,128]{2,1,0:T(8,128)S(1)} async-done(((f32[8,8,128]{2,1,0:T(8,128)}), f32[8,8,128]{2,1,0:T(8,128)S(1)}, u32[]{:S(2)}, u32[]{:S(2)}) %all-to-all-start.3) | async-done | bytes 32800 | tf_op jit(solution)/shard_map/all_to_all | solution.py:333
  80.7 0.0 copy-start.1
  80.7 0.6 copy-done.1
  81.4 2.0 %shard_map.118 = f32[4,64]{1,0:T(4,128)} custom-call(f32[8,8,128]{2,1,0:T(8,128)} %copy-done.1, f32[8,128]{1,0:T(8,128)} %get-tuple-element.25.sy_ref, f32[8,128]{1,0:T(8,128)} %constant.8.clone.lam_ref, f32[8,8]{1,0:T(8,128)} %constant.11.clone.rot_ref), custom_call_target="tpu_custom_call" | custom-call | tf_op jit(solution)/shard_map/pallas_call | solution.py:405
Async XLA Ops:
  11.7 18.9 %all-to-all-start = ((bf16[32,48,128]{2,1,0:T(8,128)(2,1)}), bf16[32,48,128]{2,1,0:T(8,128)(2,1)S(1)}, u32[]{:S(2)}, u32[]{:S(2)}) async-start(bf16[32,48,128]{2,1,0:T(8,128)(2,1)} %get-tuple-element.14), calls=%async_computation | async-start | bytes 786432 | tf_op jit(solution)/shard_map/all_to_all | solution.py:333
  30.5 0.8 copy-start
  70.6 10.1 %all-to-all-start.3 = ((f32[8,8,128]{2,1,0:T(8,128)}), f32[8,8,128]{2,1,0:T(8,128)S(1)}, u32[]{:S(2)}, u32[]{:S(2)}) async-start(f32[8,8,128]{2,1,0:T(8,128)} %shard_map.117), calls=%async_computation.3 | async-start | bytes 65536 | tf_op jit(solution)/shard_map/all_to_all | solution.py:333
  80.7 0.6 copy-start.1

commit v2 on v1

--- a/solution.py
+++ b/solution.py
@@ -91,13 +91,17 @@
     kid_s = iota((P_DEV, slots), 0)
 
     def body(j, carry):
+        start = pl.multiple_of(j * slots, slots)
+        row_at = [
+            rows_smem.at[pl.ds(i, (owners - 1) * slots + 1)][start] for i in range(slots)
+        ]
         pieces = []
         for g in range(slots // 4):
             pair = []
             for h in range(2):
                 s = 4 * g + 2 * h
-                first = res_sc[pl.ds(rows_smem[j, s] + 8, 8), :]
-                second = res_sc[pl.ds(rows_smem[j, s + 1] + 4, 8), :]
+                first = res_sc[pl.ds(row_at[s] + 8, 8), :]
+                second = res_sc[pl.ds(row_at[s + 1] + 4, 8), :]
                 pair.append(jnp.where(half, first, second))
             pieces.append(jnp.concatenate(pair, axis=0).astype(BF16))
         taps = jnp.concatenate(pieces, axis=0)
@@ -120,7 +124,7 @@
         h_sc[pl.ds(pl.multiple_of(j * P_DEV, P_DEV), P_DEV), :] = member
         return carry
 
-    lax.fori_loop(0, owners, body, 0)
+    lax.fori_loop(0, owners, body, 0, unroll=4)
     proj = dot_t(cxt_ref[...], t_ref[...], HI)
     counts = dot_t(jnp.ones((8, slots), BF16), h_sc[...].astype(BF16))
     blocks = owners * P_DEV // 128
@@ -315,8 +319,8 @@
         out_ref[v : v + 1] = jnp.sum(flat[v * ORDER : (v + 1) * ORDER], axis=0, keepdims=True)
 
 
-def call(kernel, out_shape, scratch=(), n_in=1, smem=()):
-    return pl.pallas_call(
+def call(kernel, out_shape, scratch=(), n_in=1, smem=(), plain=()):
+    fn = pl.pallas_call(
         kernel,
         out_shape=out_shape,
         in_specs=[SMEM if i in smem else VMEM for i in range(n_in)],
@@ -324,8 +328,22 @@
         scratch_shapes=list(scratch),
     )
 
+    def run(*args):
+        return fn(
+            *(
+                x if i in plain or i in smem else pltpu.with_memory_space_constraint(x, pltpu.VMEM)
+                for i, x in enumerate(args)
+            )
+        )
+
+    return run
+
 
 def shape(dims, dtype=F32):
+    return pltpu.VMEM(dims, dtype)
+
+
+def result(dims, dtype=F32):
     return jax.ShapeDtypeStruct(dims, dtype)
 
 
@@ -367,7 +385,8 @@
         ),
         n_in=8,
         smem=(0,),
-    )(srow, raw_rows, resample, srow, weights, pid, live, cxt)
+        plain=range(8),
+    )(srow.reshape(-1), raw_rows, resample, srow, weights, pid, live, cxt)
     arr1 = exchange(pay1, "visit")
     mt, qb, sy, m = call(
         functools.partial(design_kernel, ccd_devs, rows),
@@ -378,6 +397,7 @@
             shape((patches, 128)),
         ),
         n_in=5,
+        plain=(0, 1, 2, 4),
     )(srow, pid, live, qsum, cxt)
     back, den, pay2 = call(
         first_kernel,
@@ -401,8 +421,8 @@
         n_in=6,
     )(arr3, back, den, mt, qb, lam_sub)
     arr4 = exchange(pay4, "ccd")
-    background = call(background_kernel, shape((P_DEV, pix)), n_in=2)(arr3, den)
-    offsets = call(final_kernel, shape((vis, ORDER * ORDER)), n_in=4)(
+    background = call(background_kernel, result((P_DEV, pix)), n_in=2)(arr3, den)
+    offsets = call(final_kernel, result((vis, ORDER * ORDER)), n_in=4)(
         arr4, sy_all, lam_lane, rot
     )
     return offsets, background

time: 84 us -> 71.8 us (0.85)
  Pallas kernels: 29.8 us -> 18.6 us
  waiting for transfers between devices: 7.6 us -> 9.19 us
  local copies, waits for them, and re-layouts: 1.37 us -> 0.03 us
  blocking collectives: 32.1 us -> 31 us
    pallas_call x7, Pallas kernels: 29.8 us -> 18.6 us  [run(): fn(*(x if i in plain or i in smem else pltpu.with_memory_space_constraint...]
    all_to_all x2, waiting for transfers between devices: 7.6 us -> 9.19 us  [exchange(): return lax.all_to_all(x, axis, split_axis=0, concat_axis=0, tiled=True)]
    unnamed x4 -> x8, local copies, waits for them, and re-layouts: 1.37 us -> 0.03 us
    all_to_all x2, blocking collectives: 32.1 us -> 31 us  [exchange(): return lax.all_to_all(x, axis, split_axis=0, concat_axis=0, tiled=True)]
where the time goes in v2:
time: 71.8 us; the launch traced here: 71.4 us
  blocking collectives  31 us (43%)
  Pallas kernels  18.6 us (26%)
  starting transfers between devices  11.9 us (17%)
  waiting for transfers between devices  9.19 us (13%)
    all_to_all x2, blocking collectives, exchange(): return lax.all_to_all(x, axis, split_axis=0, concat_axis=0, tiled=True)  31 us
    pallas_call x7, Pallas kernels, run(): fn(*(x if i in plain or i in smem else pltpu.with_memory_space_constraint...  18.6 us
    all_to_all x2, starting transfers between devices, exchange(): return lax.all_to_all(x, axis, split_axis=0, concat_axis=0, tiled=True)  11.9 us
    all_to_all x2, waiting for transfers between devices, exchange(): return lax.all_to_all(x, axis, split_axis=0, concat_axis=0, tiled=True)  9.19 us
  transfers between devices with their start and end apart: 2, of which 2 were waited for; matrix products, arithmetic and copies ran while one was open for 0% of the time, Pallas kernels for 11%

profile of v2, /device:TPU:1, one launch (start us, length us, event | category | flops | bytes accessed | tf_op | source)
XLA Modules:
  0.0 71.4 jit_solution(9626092315282245931)
XLA Ops:
  0.6 6.8 %shard_map.113 = (bf16[32,48,128]{2,1,0:T(8,128)(2,1)}, f32[512,128]{1,0:T(8,128)S(1)}, f32[32,128]{1,0:T(8,128)S(1)}) custom-call(s32[4096]{0:T(1024)} %bitcast.5, bf16[4,1024,128]{2,1,0:T(8,128)(2,1)} %raw_ref.1, bf16[4,128,128]{2,1,0:T(8,128)(2,1)} %res_ref.1, s32[32,128]{1,0:T(8,128)} %bitcast.6, f32[4,32,128]{2,1,0:T(8,128)} %bitcast.12, ...), custom_call_target="tpu_custom_call" | custom-call | tf_op jit(solution)/shard_map/pallas_call | solution.py:332
  7.4 8.6 %all-to-all-start = ((bf16[32,48,128]{2,1,0:T(8,128)(2,1)}), bf16[32,48,128]{2,1,0:T(8,128)(2,1)S(1)}, u32[]{:S(2)}, u32[]{:S(2)}) async-start(bf16[32,48,128]{2,1,0:T(8,128)(2,1)} %get-tuple-element.14), calls=%async_computation | async-start | bytes 786432 | tf_op jit(solution)/shard_map/all_to_all | solution.py:351
  16.0 7.0 %shard_map.114 = (f32[32,512]{1,0:T(8,128)S(1)}, f32[8,128]{1,0:T(8,128)S(1)}, f32[8,128]{1,0:T(8,128)S(1)}, f32[512,128]{1,0:T(8,128)S(1)}) custom-call(s32[32,128]{1,0:T(8,128)} %bitcast.7, s32[32,128]{1,0:T(8,128)} %bitcast.9, s32[32,128]{1,0:T(8,128)} %bitcast.11, f32[32,128]{1,0:T(8,128)S(1)} %get-tuple-element.15.q_ref, f32[8,128]{1,0:T(8,128)} %constant.10.clone.cxt_ref), custom_call_target="tpu_custom_call" | custom-call | tf_op jit(solution)/shard_map/pallas_call | solution.py:332
  23.0 3.3 %all-to-all-done.arr_ref = bf16[32,48,128]{2,1,0:T(8,128)(2,1)S(1)} async-done(((bf16[32,48,128]{2,1,0:T(8,128)(2,1)}), bf16[32,48,128]{2,1,0:T(8,128)(2,1)S(1)}, u32[]{:S(2)}, u32[]{:S(2)}) %all-to-all-start) | async-done | bytes 393248 | tf_op jit(solution)/shard_map/all_to_all | solution.py:351
  26.2 0.6 shard_map.115
  26.8 0.0 copy-start
  26.8 0.0 copy-start.1
  26.8 15.3 %all_to_all.20.arr_ref = f32[8,16,128]{2,1,0:T(8,128)S(1)} all-to-all(f32[8,16,128]{2,1,0:T(8,128)S(1)} %get-tuple-element.19), channel_id=1, replica_groups=mesh['visit'=32,'ccd'=8] {'ccd'}, dimensions={0} | all-to-all | bytes 131072 | tf_op jit(solution)/shard_map/all_to_all | solution.py:351
  42.1 0.0 copy-done
  42.1 0.0 copy-done.1
  42.1 0.9 %shard_map.116 = (f32[8,128]{1,0:T(8,128)S(1)}, bf16[32,48,128]{2,1,0:T(8,128)(2,1)S(1)}) custom-call(f32[8,16,128]{2,1,0:T(8,128)S(1)} %all_to_all.20.arr_ref, f32[8,128]{1,0:T(8,128)S(1)} %copy-done.1, f32[32,512]{1,0:T(8,128)S(1)} %get-tuple-element.16.mt_ref, f32[512,128]{1,0:T(8,128)S(1)} %get-tuple-element.20.m_ref, ...), custom_call_target="tpu_custom_call" | custom-call | tf_op jit(solution)/shard_map/pallas_call | solution.py:332
  43.0 0.0 copy-start.2
  43.1 15.7 %all_to_all.21.arr_ref = bf16[32,48,128]{2,1,0:T(8,128)(2,1)S(1)} all-to-all(bf16[32,48,128]{2,1,0:T(8,128)(2,1)S(1)} %get-tuple-element.22), channel_id=1, replica_groups=mesh['visit'=32,'ccd'=8] {'visit'}, dimensions={0} | all-to-all | bytes 786432 | tf_op jit(solution)/shard_map/all_to_all | solution.py:351
  58.8 0.0 copy-done.2
  58.8 1.2 %shard_map.117 = f32[8,8,128]{2,1,0:T(8,128)} custom-call(bf16[32,48,128]{2,1,0:T(8,128)(2,1)S(1)} %all_to_all.21.arr_ref, f32[8,512]{1,0:T(8,128)S(1)} %get-tuple-element.23.b_ref, f32[8,512]{1,0:T(8,128)S(1)} %get-tuple-element.24.den_ref, f32[32,512]{1,0:T(8,128)S(1)} %get-tuple-element.16.mt_ref, f32[8,128]{1,0:T(8,128)S(1)} %get-tuple-element.17.qb_ref, ...), custom_call_target="tpu_custom_call" | custom-call | tf_op jit(solution)/shard_map/pallas_call | solution.py:332
  60.0 3.3 %all-to-all-start.3 = ((f32[8,8,128]{2,1,0:T(8,128)}), f32[8,8,128]{2,1,0:T(8,128)S(1)}, u32[]{:S(2)}, u32[]{:S(2)}) async-start(f32[8,8,128]{2,1,0:T(8,128)} %shard_map.117), calls=%async_computation.3 | async-start | bytes 65536 | tf_op jit(solution)/shard_map/all_to_all | solution.py:351
  63.3 0.0 copy-start.3
  63.3 0.8 %shard_map.119 = f32[16,128]{1,0:T(8,128)} custom-call(bf16[32,48,128]{2,1,0:T(8,128)(2,1)S(1)} %all_to_all.21.arr_ref, f32[8,512]{1,0:T(8,128)S(1)} %get-tuple-element.24.den_ref), custom_call_target="tpu_custom_call" | custom-call | tf_op jit(solution)/shard_map/pallas_call | solution.py:332
  64.2 5.9 %all-to-all-done.3.arr_ref = f32[8,8,128]{2,1,0:T(8,128)S(1)} async-done(((f32[8,8,128]{2,1,0:T(8,128)}), f32[8,8,128]{2,1,0:T(8,128)S(1)}, u32[]{:S(2)}, u32[]{:S(2)}) %all-to-all-start.3) | async-done | bytes 32800 | tf_op jit(solution)/shard_map/all_to_all | solution.py:351
  70.1 0.0 copy-done.3
  70.1 1.2 %shard_map.118 = f32[4,64]{1,0:T(4,128)} custom-call(f32[8,8,128]{2,1,0:T(8,128)S(1)} %all-to-all-done.3.arr_ref, f32[8,128]{1,0:T(8,128)S(1)} %get-tuple-element.25.sy_ref, f32[8,128]{1,0:T(8,128)S(1)} %copy-done.1, f32[8,8]{1,0:T(8,128)S(1)} %copy-done.3), custom_call_target="tpu_custom_call" | custom-call | tf_op jit(solution)/shard_map/pallas_call | solution.py:332
Async XLA Ops:
  7.4 18.9 %all-to-all-start = ((bf16[32,48,128]{2,1,0:T(8,128)(2,1)}), bf16[32,48,128]{2,1,0:T(8,128)(2,1)S(1)}, u32[]{:S(2)}, u32[]{:S(2)}) async-start(bf16[32,48,128]{2,1,0:T(8,128)(2,1)} %get-tuple-element.14), calls=%async_computation | async-start | bytes 786432 | tf_op jit(solution)/shard_map/all_to_all | solution.py:351
  26.8 15.3 %copy-start = (f32[8,128]{1,0:T(8,128)S(1)}, f32[8,128]{1,0:T(8,128)}, u32[]{:S(2)}) copy-start(f32[8,128]{1,0:T(8,128)} %constant.10.clone.cxt_ref) | copy-start | bytes 12292
  26.8 15.3 %copy-start.1 = (f32[8,128]{1,0:T(8,128)S(1)}, f32[8,128]{1,0:T(8,128)}, u32[]{:S(2)}) copy-start(f32[8,128]{1,0:T(8,128)} %constant.8.clone.lam_ref) | copy-start | bytes 12292
  43.0 15.7 %copy-start.2 = (f32[8,128]{1,0:T(8,128)S(1)}, f32[8,128]{1,0:T(8,128)}, u32[]{:S(2)}) copy-start(f32[8,128]{1,0:T(8,128)} %constant.9.clone.lam_ref) | copy-start | bytes 12292
  60.0 10.1 %all-to-all-start.3 = ((f32[8,8,128]{2,1,0:T(8,128)}), f32[8,8,128]{2,1,0:T(8,128)S(1)}, u32[]{:S(2)}, u32[]{:S(2)}) async-start(f32[8,8,128]{2,1,0:T(8,128)} %shard_map.117), calls=%async_computation.3 | async-start | bytes 65536 | tf_op jit(solution)/shard_map/all_to_all | solution.py:351
  63.3 6.8 %copy-start.3 = (f32[8,8]{1,0:T(8,128)S(1)}, f32[8,8]{1,0:T(8,128)}, u32[]{:S(2)}) copy-start(f32[8,8]{1,0:T(8,128)} %constant.11.clone.rot_ref) | copy-start | bytes 772

commit v3 on v2

--- a/solution.py
+++ b/solution.py
@@ -12,11 +12,12 @@
 TAPS = 4
 P_DEV = 16
 RIDGE = 1.0
+UNROLL = 8
 HI = lax.Precision.HIGHEST
 F32 = jnp.float32
 BF16 = jnp.bfloat16
 VMEM = pl.BlockSpec(memory_space=pltpu.VMEM)
-SMEM = pl.BlockSpec(memory_space=pltpu.SMEM)
+HBM = pl.BlockSpec(memory_space=pl.ANY)
 
 
 def constants(pixels):
@@ -41,6 +42,14 @@
     )
 
 
+def split(x, parts):
+    out = []
+    for _ in range(parts):
+        out.append(x.astype(BF16))
+        x = x - out[-1].astype(F32)
+    return out
+
+
 def iota(shape, dim):
     return lax.broadcasted_iota(jnp.int32, shape, dim)
 
@@ -61,24 +70,39 @@
 
 
 def gather_kernel(
-    ccd_devs, rows_smem, raw_ref, res_ref, srow_ref, w_ref, pid_ref, live_ref, cxt_ref,
+    ccd_devs, rows_hbm, raw_hbm, res_hbm, srow_hbm, w_hbm, pid_hbm, live_hbm, cxt_hbm,
     pay_ref, t_ref, q_ref, res_sc, row_sc, code_sc, wi_sc, h_sc,
+    rows_smem, raw_ref, res_ref, srow_ref, w_ref, pid_ref, live_ref, cxt_ref, sems,
 ):
     vis, rows, pix = raw_ref.shape
     owners, slots = srow_ref.shape
     wide = slots * TAPS
     ccd = lax.axis_index("ccd")
-    for v in range(vis):
-        res_sc[pl.ds(8 + v * rows, rows), :] = dot(raw_ref[v], res_ref[v])
+    small = [
+        pltpu.make_async_copy(src, dst, sems.at[n])
+        for n, (src, dst) in enumerate(
+            ((srow_hbm, srow_ref), (pid_hbm, pid_ref), (live_hbm, live_ref), (w_hbm, w_ref))
+        )
+    ]
+    index = pltpu.make_async_copy(rows_hbm, rows_smem, sems.at[4])
+    warp = pltpu.make_async_copy(res_hbm, res_ref, sems.at[5])
+    proj_copy = pltpu.make_async_copy(cxt_hbm, cxt_ref, sems.at[6 + vis])
+    raw = [
+        pltpu.make_async_copy(raw_hbm.at[v], raw_ref.at[v], sems.at[6 + v]) for v in range(vis)
+    ]
+    for copy in small + [warp] + raw + [index, proj_copy]:
+        copy.start()
+    for copy in small:
+        copy.wait()
     off = iota((slots, wide), 1) - TAPS * iota((slots, wide), 0)
     rep = jnp.where((off >= 0) & (off < TAPS), 1.0, 0.0).astype(BF16)
     srow = srow_ref[...]
     code = pid_ref[...] + P_DEV * (1 - live_ref[...])
     high, low = srow >> 8, srow & 255
-    row_sc[...] = 256.0 * dot(high.astype(F32).astype(BF16), rep) + dot(
-        low.astype(F32).astype(BF16), rep
-    )
-    code_sc[...] = dot(code.astype(F32).astype(BF16), rep)
+    whole = jnp.concatenate([high, low, code], axis=0).astype(F32).astype(BF16)
+    whole = dot(whole, rep)
+    row_sc[...] = 256.0 * whole[:owners] + whole[owners : 2 * owners]
+    code_sc[...] = whole[2 * owners :]
     wi = None
     for t in range(TAPS):
         pick = jnp.where(off == t, 1.0, 0.0).astype(BF16)
@@ -89,6 +113,21 @@
     half = iota((8, pix), 0) < TAPS
     kid = iota((P_DEV, wide), 0).astype(F32)
     kid_s = iota((P_DEV, slots), 0)
+    for copy in [warp] + raw + [index, proj_copy]:
+        copy.wait()
+    zero = jnp.zeros((pix, pix), BF16)
+    for v in range(0, vis, 2):
+        pair = jnp.concatenate([raw_ref[v], raw_ref[v + 1]], axis=1)
+        diag = jnp.concatenate(
+            [
+                jnp.concatenate([res_ref[v], zero], axis=1),
+                jnp.concatenate([zero, res_ref[v + 1]], axis=1),
+            ],
+            axis=0,
+        )
+        both = dot(pair, diag)
+        res_sc[pl.ds(8 + v * rows, rows), :] = both[:, :pix]
+        res_sc[pl.ds(8 + (v + 1) * rows, rows), :] = both[:, pix:]
 
     def body(j, carry):
         start = pl.multiple_of(j * slots, slots)
@@ -121,16 +160,19 @@
         q_ref[...] += sums[P_DEV:]
         live = live_ref[pl.ds(j, 1), :]
         member = jnp.where((pid_ref[pl.ds(j, 1), :] == kid_s) & (live > 0), 1.0, 0.0)
-        h_sc[pl.ds(pl.multiple_of(j * P_DEV, P_DEV), P_DEV), :] = member
+        h_sc[pl.ds(pl.multiple_of(j * P_DEV, P_DEV), P_DEV), :] = member.astype(BF16)
         return carry
 
-    lax.fori_loop(0, owners, body, 0, unroll=4)
-    proj = dot_t(cxt_ref[...], t_ref[...], HI)
-    counts = dot_t(jnp.ones((8, slots), BF16), h_sc[...].astype(BF16))
+    lax.fori_loop(0, owners, body, 0, unroll=UNROLL)
+    c_hi, c_lo = split(cxt_ref[...], 2)
+    t_hi, t_lo = split(t_ref[...], 2)
+    proj = dot_t(jnp.concatenate([c_hi, c_lo], axis=0), t_hi)
+    proj = proj[:ORDER] + proj[ORDER:] + dot_t(c_hi, t_lo)
+    counts = dot_t(jnp.ones((8, slots), BF16), h_sc[...])
     blocks = owners * P_DEV // 128
-    sub = iota((16, 128), 0)
+    sub = iota((8, 128), 0)
     rows_out = [proj[:, 128 * q : 128 * (q + 1)] for q in range(blocks)]
-    tail = jnp.zeros((16, 128), F32)
+    tail = jnp.zeros((8, 128), F32)
     for q in range(blocks):
         tail = jnp.where(sub == q, counts[0:1, 128 * q : 128 * (q + 1)], tail)
     block = jnp.concatenate(rows_out + [tail], axis=0).astype(BF16)
@@ -139,10 +181,12 @@
 
 
 def design_kernel(
-    ccd_devs, rows, srow_ref, pid_ref, live_ref, q_ref, cxt_ref, mt_ref, qb_ref, sy_ref, m_sc
+    ccd_devs, rows, srow_ref, pid_ref, live_ref, q_ref, cxt_ref,
+    mt_ref, qb_ref, sy_ref, mw_ref, mtw_ref, m_sc,
 ):
     owners, slots = srow_ref.shape
     vis = q_ref.shape[0] // ORDER
+    n = vis * ORDER
     ccd = lax.axis_index("ccd")
     kid = iota((P_DEV, slots), 0)
     m_sc[...] = jnp.zeros_like(m_sc)
@@ -154,17 +198,29 @@
         visit = srow // rows
         y = coord((srow - visit * rows).astype(F32), ccd, rows, ccd_devs)
         ty = cheb_rows(jnp.broadcast_to(y, (ORDER, slots)), ORDER)
-        member = jnp.where((pid == kid) & (live > 0), 1.0, 0.0)
+        member = jnp.where((pid == kid) & (live > 0), 1.0, 0.0).astype(BF16)
         vt = jnp.concatenate(
             [jnp.where((visit == v) & (live > 0), ty, 0.0) for v in range(vis)], axis=0
         )
-        both = dot_t(jnp.concatenate([member, ty], axis=0), vt, HI)
-        m_sc[pl.ds(pl.multiple_of(j * P_DEV, P_DEV), P_DEV), 0 : vis * ORDER] = both[:P_DEV]
+        parts = jnp.concatenate([p.astype(F32) for p in split(ty, 3)] + [jnp.zeros_like(ty)], axis=0)
+        left = jnp.concatenate([member, parts.astype(BF16)], axis=0)
+        both = None
+        for piece in split(vt, 3):
+            part = dot_t(left, piece)
+            both = part if both is None else both + part
+        m_sc[pl.ds(pl.multiple_of(j * P_DEV, P_DEV), P_DEV), 0:n] = both[:P_DEV]
         return acc + both[P_DEV:]
 
-    sy = lax.fori_loop(0, owners, body, jnp.zeros((ORDER, vis * ORDER), F32))
-    sy_ref[...] = jnp.concatenate([sy, jnp.zeros((ORDER, 128 - vis * ORDER), F32)], axis=1)
-    mt_ref[...] = m_sc[...].T[: vis * ORDER]
+    sy = lax.fori_loop(0, owners, body, jnp.zeros((4 * ORDER, n), F32), unroll=4)
+    sy = sy[:ORDER] + sy[ORDER : 2 * ORDER] + sy[2 * ORDER : 3 * ORDER]
+    sy_ref[...] = jnp.concatenate([sy, jnp.zeros((ORDER, 128 - n), F32)], axis=1)
+    m_hi, m_lo = split(m_sc[...], 2)
+    mt = m_sc[...].T[:n]
+    mt_ref[...] = mt
+    mt_hi, mt_lo = split(mt, 2)
+    mtw_ref[...] = jnp.concatenate([mt_hi, mt_hi, mt_lo, jnp.zeros_like(mt_hi)], axis=0)
+    mw_ref[0] = m_hi
+    mw_ref[1] = m_lo
     qb_ref[...] = blocks_of(dot_t(q_ref[...], tile_rows(cxt_ref[...], 128 // ORDER), HI), vis)
 
 
@@ -247,8 +303,9 @@
     return jnp.where(keep, tiled, 0.0).T[:n]
 
 
-def model_kernel(arr_ref, lam_ref, mt_ref, m_ref, t_ref, cxt_ref, sy_ref, pay_ref):
-    vis = mt_ref.shape[0] // ORDER
+def model_kernel(arr_ref, lam_ref, mtw_ref, mw_ref, t_ref, cxt_ref, sy_ref, pay_ref):
+    vis = mtw_ref.shape[0] // (4 * ORDER)
+    n = vis * ORDER
     total = arr_ref[0]
     for i in range(1, arr_ref.shape[0]):
         total = total + arr_ref[i]
@@ -258,12 +315,18 @@
     weights = diag[:ORDER]
     for v in range(1, vis):
         weights = weights + diag[v * ORDER : (v + 1) * ORDER]
-    model = dot(weights, mt_ref[...], HI)
+    w_hi, w_lo = split(weights, 2)
+    model = (
+        dot(w_hi, mtw_ref[0:n])
+        + dot(w_lo, mtw_ref[n : 2 * n])
+        + dot(w_hi, mtw_ref[2 * n : 3 * n])
+    )
     surface = lax.dot_general(
         weights, cxt_ref[...], (((0,), (0,)), ((), ())), precision=HI, preferred_element_type=F32
     )
-    surface = jnp.concatenate([surface, jnp.zeros((128 - vis * ORDER, 128), F32)], axis=0)
-    corrected = t_ref[...] - dot(m_ref[...], surface, HI)
+    surface = jnp.concatenate([surface, jnp.zeros((128 - n, 128), F32)], axis=0)
+    s_hi, s_lo = split(surface, 2)
+    corrected = t_ref[...] - (dot(mw_ref[0], s_hi) + dot(mw_ref[0], s_lo) + dot(mw_ref[1], s_hi))
     blocks = model.shape[1] // 128
     block = jnp.concatenate(
         [model[:, 128 * q : 128 * (q + 1)] for q in range(blocks)], axis=0
@@ -306,24 +369,16 @@
     for i in range(1, arr_ref.shape[0]):
         total = total + arr_ref[i]
     z = solve(total, sy_ref[...], lam_ref[0:1], vis)
-    zt = z.T[:n]
-    coef = jnp.concatenate(
-        [dot(rot_ref[...], zt[v * ORDER : (v + 1) * ORDER], HI) for v in range(vis)], axis=0
-    )
-    wide = ORDER * ORDER
-    spread = jnp.where(iota((ORDER, wide), 1) % ORDER == iota((ORDER, wide), 0), 1.0, 0.0)
-    flat = dot(coef, spread, HI)
-    keep = iota((n, wide), 1) // ORDER == iota((n, wide), 0) % ORDER
-    flat = jnp.where(keep, flat, 0.0)
+    flat = tile_rows(z, ORDER).T[:n] * tile_rows(rot_ref[...], vis)
     for v in range(vis):
         out_ref[v : v + 1] = jnp.sum(flat[v * ORDER : (v + 1) * ORDER], axis=0, keepdims=True)
 
 
-def call(kernel, out_shape, scratch=(), n_in=1, smem=(), plain=()):
+def call(kernel, out_shape, scratch=(), n_in=1, hbm=(), plain=()):
     fn = pl.pallas_call(
         kernel,
         out_shape=out_shape,
-        in_specs=[SMEM if i in smem else VMEM for i in range(n_in)],
+        in_specs=[HBM if i in hbm else VMEM for i in range(n_in)],
         out_specs=jax.tree.map(lambda _: VMEM, out_shape),
         scratch_shapes=list(scratch),
     )
@@ -331,7 +386,7 @@
     def run(*args):
         return fn(
             *(
-                x if i in plain or i in smem else pltpu.with_memory_space_constraint(x, pltpu.VMEM)
+                x if i in plain or i in hbm else pltpu.with_memory_space_constraint(x, pltpu.VMEM)
                 for i, x in enumerate(args)
             )
         )
@@ -364,7 +419,8 @@
     lam_lane[0, :nvb] = np.tile(lam, vis)
     lam_sub = np.broadcast_to(lam[:, None], (8, 128))
     lam_lane, lam_sub = jnp.asarray(lam_lane, F32), jnp.asarray(lam_sub, F32)
-    cxt, rot = jnp.asarray(cxt, F32), jnp.asarray(rot, F32)
+    cxt = jnp.asarray(cxt, F32)
+    rot = jnp.asarray(np.repeat(rot.T, ORDER, axis=1), F32)
     srow, pid, live = slot_row[0, 0], patch_id[0, 0], live_mask[0, 0]
     weights = tap_weight[:, 0, 0]
     pay_rows = ORDER * blocks + P_DEV
@@ -372,7 +428,7 @@
     pay1, tsum, qsum = call(
         functools.partial(gather_kernel, ccd_devs),
         (
-            shape((owners, pay_rows, 128), BF16),
+            shape((owners, ORDER * blocks + 8, 128), BF16),
             shape((patches, pix)),
             shape((nvb, pix)),
         ),
@@ -381,21 +437,31 @@
             pltpu.VMEM((owners, slots * TAPS), F32),
             pltpu.VMEM((owners, slots * TAPS), F32),
             pltpu.VMEM((owners, slots * TAPS), F32),
-            pltpu.VMEM((patches, slots), F32),
+            pltpu.VMEM((patches, slots), BF16),
+            pltpu.SMEM((owners * slots,), jnp.int32),
+            pltpu.VMEM(raw_rows.shape, BF16),
+            pltpu.VMEM(resample.shape, BF16),
+            pltpu.VMEM((owners, slots), jnp.int32),
+            pltpu.VMEM((TAPS, owners, slots), F32),
+            pltpu.VMEM((owners, slots), jnp.int32),
+            pltpu.VMEM((owners, slots), jnp.int32),
+            pltpu.VMEM((ORDER, pix), F32),
+            pltpu.SemaphoreType.DMA((7 + vis,)),
         ),
         n_in=8,
-        smem=(0,),
-        plain=range(8),
+        hbm=range(8),
     )(srow.reshape(-1), raw_rows, resample, srow, weights, pid, live, cxt)
     arr1 = exchange(pay1, "visit")
-    mt, qb, sy, m = call(
+    mt, qb, sy, mw, mtw = call(
         functools.partial(design_kernel, ccd_devs, rows),
         (
             shape((nvb, patches)),
             shape((ORDER, 128)),
             shape((ORDER, 128)),
-            shape((patches, 128)),
+            shape((2, patches, 128), BF16),
+            shape((4 * nvb, patches), BF16),
         ),
+        scratch=(pltpu.VMEM((patches, 128), F32),),
         n_in=5,
         plain=(0, 1, 2, 4),
     )(srow, pid, live, qsum, cxt)
@@ -413,7 +479,7 @@
         model_kernel,
         (shape((ORDER, 128)), shape((owners, pay_rows, 128), BF16)),
         n_in=6,
-    )(arr2, lam_lane, mt, m, tsum, cxt)
+    )(arr2, lam_lane, mtw, mw, tsum, cxt)
     arr3 = exchange(pay3, "visit")
     pay4 = call(
         second_kernel,

time: 71.8 us -> 70.1 us (0.976)
  Pallas kernels: 18.6 us -> 13.3 us
  waiting for transfers between devices: 9.19 us -> 12.6 us
    pallas_call x7, Pallas kernels: 18.6 us -> 13.3 us  [run(): fn(*(x if i in plain or i in hbm else pltpu.with_memory_space_constraint(...]
    all_to_all x2, waiting for transfers between devices: 9.19 us -> 12.6 us  [exchange(): return lax.all_to_all(x, axis, split_axis=0, concat_axis=0, tiled=True)]
  transfers between devices with their start and end apart: 2 -> 2, of which waited for: 2 -> 2; matrix products, arithmetic and copies ran while one was open for 0% -> 0% of each run, Pallas kernels for 11% -> 6%
where the time goes in v3:
time: 70.1 us; the launch traced here: 69.5 us
  blocking collectives  30.3 us (43%)
  Pallas kernels  13.3 us (19%)
  waiting for transfers between devices  12.6 us (18%)
  starting transfers between devices  11.9 us (17%)
  local copies, waits for them, and re-layouts  0.71 us (1%)
    all_to_all x2, blocking collectives, exchange(): return lax.all_to_all(x, axis, split_axis=0, concat_axis=0, tiled=True)  30.3 us
    pallas_call x7, Pallas kernels, run(): fn(*(x if i in plain or i in hbm else pltpu.with_memory_space_constraint(...  13.3 us
    all_to_all x2, waiting for transfers between devices, exchange(): return lax.all_to_all(x, axis, split_axis=0, concat_axis=0, tiled=True)  12.6 us
    all_to_all x2, starting transfers between devices, exchange(): return lax.all_to_all(x, axis, split_axis=0, concat_axis=0, tiled=True)  11.9 us
  transfers between devices with their start and end apart: 2, of which 2 were waited for; matrix products, arithmetic and copies ran while one was open for 0% of the time, Pallas kernels for 6%

profile of v3, /device:TPU:1, one launch (start us, length us, event | category | flops | bytes accessed | tf_op | source)
XLA Modules:
  0.0 69.5 jit_solution(10926007587823056334)
XLA Ops:
  0.6 6.0 %shard_map.113 = (bf16[32,40,128]{2,1,0:T(8,128)(2,1)}, f32[512,128]{1,0:T(8,128)S(1)}, f32[32,128]{1,0:T(8,128)S(1)}) custom-call(s32[4096]{0:T(1024)} %bitcast.5, bf16[4,1024,128]{2,1,0:T(8,128)(2,1)} %raw_hbm.1, bf16[4,128,128]{2,1,0:T(8,128)(2,1)} %res_hbm.1, s32[32,128]{1,0:T(8,128)} %bitcast.6, f32[4,32,128]{2,1,0:T(8,128)} %bitcast.12, ...), custom_call_target="tpu_custom_call" | custom-call | tf_op jit(solution)/shard_map/pallas_call | solution.py:387
  6.6 8.6 %all-to-all-start = ((bf16[32,40,128]{2,1,0:T(8,128)(2,1)}), bf16[32,40,128]{2,1,0:T(8,128)(2,1)S(1)}, u32[]{:S(2)}, u32[]{:S(2)}) async-start(bf16[32,40,128]{2,1,0:T(8,128)(2,1)} %get-tuple-element.15), calls=%async_computation | async-start | bytes 655360 | tf_op jit(solution)/shard_map/all_to_all | solution.py:406
  15.2 3.0 %shard_map.114 = (f32[32,512]{1,0:T(8,128)S(1)}, f32[8,128]{1,0:T(8,128)S(1)}, f32[8,128]{1,0:T(8,128)S(1)}, bf16[2,512,128]{2,1,0:T(8,128)(2,1)S(1)}, bf16[128,512]{1,0:T(8,128)(2,1)S(1)}) custom-call(s32[32,128]{1,0:T(8,128)} %bitcast.7, s32[32,128]{1,0:T(8,128)} %bitcast.9, s32[32,128]{1,0:T(8,128)} %bitcast.11, f32[32,128]{1,0:T(8,128)S(1)} %get-tuple-element.16.q_ref, ...), custom_call_target="tpu_custom_call" | custom-call | tf_op jit(solution)/shard_map/pallas_call | solution.py:387
  18.2 6.6 %all-to-all-done.arr_ref = bf16[32,40,128]{2,1,0:T(8,128)(2,1)S(1)} async-done(((bf16[32,40,128]{2,1,0:T(8,128)(2,1)}), bf16[32,40,128]{2,1,0:T(8,128)(2,1)S(1)}, u32[]{:S(2)}, u32[]{:S(2)}) %all-to-all-start) | async-done | bytes 327712 | tf_op jit(solution)/shard_map/all_to_all | solution.py:406
  24.8 0.6 shard_map.115
  25.4 0.0 copy-start.1
  25.4 15.1 %all_to_all.20.arr_ref = f32[8,16,128]{2,1,0:T(8,128)S(1)} all-to-all(f32[8,16,128]{2,1,0:T(8,128)S(1)} %get-tuple-element.20), channel_id=1, replica_groups=mesh['visit'=32,'ccd'=8] {'ccd'}, dimensions={0} | all-to-all | bytes 131072 | tf_op jit(solution)/shard_map/all_to_all | solution.py:406
  40.5 0.0 copy-start
  40.5 0.0 copy-done.1
  40.6 0.7 copy-done
  41.2 0.8 %shard_map.116 = (f32[8,128]{1,0:T(8,128)S(1)}, bf16[32,48,128]{2,1,0:T(8,128)(2,1)S(1)}) custom-call(f32[8,16,128]{2,1,0:T(8,128)S(1)} %all_to_all.20.arr_ref, f32[8,128]{1,0:T(8,128)S(1)} %copy-done.1, bf16[128,512]{1,0:T(8,128)(2,1)S(1)} %get-tuple-element.21.mtw_ref, bf16[2,512,128]{2,1,0:T(8,128)(2,1)S(1)} %get-tuple-element.22.mw_ref, ...), custom_call_target="tpu_custom_call" | custom-call | tf_op jit(solution)/shard_map/pallas_call | solution.py:387
  42.1 0.0 copy-start.2
  42.1 15.2 %all_to_all.21.arr_ref = bf16[32,48,128]{2,1,0:T(8,128)(2,1)S(1)} all-to-all(bf16[32,48,128]{2,1,0:T(8,128)(2,1)S(1)} %get-tuple-element.24), channel_id=1, replica_groups=mesh['visit'=32,'ccd'=8] {'visit'}, dimensions={0} | all-to-all | bytes 786432 | tf_op jit(solution)/shard_map/all_to_all | solution.py:406
  57.3 0.0 copy-done.2
  57.3 1.2 %shard_map.117 = f32[8,8,128]{2,1,0:T(8,128)} custom-call(bf16[32,48,128]{2,1,0:T(8,128)(2,1)S(1)} %all_to_all.21.arr_ref, f32[8,512]{1,0:T(8,128)S(1)} %get-tuple-element.25.b_ref, f32[8,512]{1,0:T(8,128)S(1)} %get-tuple-element.26.den_ref, f32[32,512]{1,0:T(8,128)S(1)} %get-tuple-element.17.mt_ref, f32[8,128]{1,0:T(8,128)S(1)} %get-tuple-element.18.qb_ref, ...), custom_call_target="tpu_custom_call" | custom-call | tf_op jit(solution)/shard_map/pallas_call | solution.py:387
  58.5 3.3 %all-to-all-start.3 = ((f32[8,8,128]{2,1,0:T(8,128)}), f32[8,8,128]{2,1,0:T(8,128)S(1)}, u32[]{:S(2)}, u32[]{:S(2)}) async-start(f32[8,8,128]{2,1,0:T(8,128)} %shard_map.117), calls=%async_computation.3 | async-start | bytes 65536 | tf_op jit(solution)/shard_map/all_to_all | solution.py:406
  61.8 0.0 copy-start.3
  61.8 0.8 %shard_map.119 = f32[16,128]{1,0:T(8,128)} custom-call(bf16[32,48,128]{2,1,0:T(8,128)(2,1)S(1)} %all_to_all.21.arr_ref, f32[8,512]{1,0:T(8,128)S(1)} %get-tuple-element.26.den_ref), custom_call_target="tpu_custom_call" | custom-call | tf_op jit(solution)/shard_map/pallas_call | solution.py:387
  62.7 5.9 %all-to-all-done.3.arr_ref = f32[8,8,128]{2,1,0:T(8,128)S(1)} async-done(((f32[8,8,128]{2,1,0:T(8,128)}), f32[8,8,128]{2,1,0:T(8,128)S(1)}, u32[]{:S(2)}, u32[]{:S(2)}) %all-to-all-start.3) | async-done | bytes 32800 | tf_op jit(solution)/shard_map/all_to_all | solution.py:406
  68.6 0.0 copy-done.3
  68.6 0.9 %shard_map.118 = f32[4,64]{1,0:T(4,128)} custom-call(f32[8,8,128]{2,1,0:T(8,128)S(1)} %all-to-all-done.3.arr_ref, f32[8,128]{1,0:T(8,128)S(1)} %get-tuple-element.27.sy_ref, f32[8,128]{1,0:T(8,128)S(1)} %copy-done.1, f32[8,64]{1,0:T(8,128)S(1)} %copy-done.3), custom_call_target="tpu_custom_call" | custom-call | tf_op jit(solution)/shard_map/pallas_call | solution.py:387
Async XLA Ops:
  6.6 18.2 %all-to-all-start = ((bf16[32,40,128]{2,1,0:T(8,128)(2,1)}), bf16[32,40,128]{2,1,0:T(8,128)(2,1)S(1)}, u32[]{:S(2)}, u32[]{:S(2)}) async-start(bf16[32,40,128]{2,1,0:T(8,128)(2,1)} %get-tuple-element.15), calls=%async_computation | async-start | bytes 655360 | tf_op jit(solution)/shard_map/all_to_all | solution.py:406
  25.4 15.1 %copy-start.1 = (f32[8,128]{1,0:T(8,128)S(1)}, f32[8,128]{1,0:T(8,128)}, u32[]{:S(2)}) copy-start(f32[8,128]{1,0:T(8,128)} %constant.8.clone.lam_ref) | copy-start | bytes 12292
  40.5 0.7 copy-start
  42.1 15.2 %copy-start.2 = (f32[8,128]{1,0:T(8,128)S(1)}, f32[8,128]{1,0:T(8,128)}, u32[]{:S(2)}) copy-start(f32[8,128]{1,0:T(8,128)} %constant.9.clone.lam_ref) | copy-start | bytes 12292
  58.5 10.1 %all-to-all-start.3 = ((f32[8,8,128]{2,1,0:T(8,128)}), f32[8,8,128]{2,1,0:T(8,128)S(1)}, u32[]{:S(2)}, u32[]{:S(2)}) async-start(f32[8,8,128]{2,1,0:T(8,128)} %shard_map.117), calls=%async_computation.3 | async-start | bytes 65536 | tf_op jit(solution)/shard_map/all_to_all | solution.py:406
  61.8 6.8 %copy-start.3 = (f32[8,64]{1,0:T(8,128)S(1)}, f32[8,64]{1,0:T(8,128)}, u32[]{:S(2)}) copy-start(f32[8,64]{1,0:T(8,128)} %constant.11.clone.rot_ref) | copy-start | bytes 6148

commit v4 on v3

--- a/solution.py
+++ b/solution.py
@@ -13,6 +13,7 @@
 P_DEV = 16
 RIDGE = 1.0
 UNROLL = 8
+CXT, LAM_LANE, LAM_SUB, ROT = (slice(8 * i, 8 * (i + 1)) for i in range(4))
 HI = lax.Precision.HIGHEST
 F32 = jnp.float32
 BF16 = jnp.bfloat16
@@ -86,7 +87,7 @@
     ]
     index = pltpu.make_async_copy(rows_hbm, rows_smem, sems.at[4])
     warp = pltpu.make_async_copy(res_hbm, res_ref, sems.at[5])
-    proj_copy = pltpu.make_async_copy(cxt_hbm, cxt_ref, sems.at[6 + vis])
+    proj_copy = pltpu.make_async_copy(cxt_hbm.at[CXT], cxt_ref, sems.at[6 + vis])
     raw = [
         pltpu.make_async_copy(raw_hbm.at[v], raw_ref.at[v], sems.at[6 + v]) for v in range(vis)
     ]
@@ -181,8 +182,8 @@
 
 
 def design_kernel(
-    ccd_devs, rows, srow_ref, pid_ref, live_ref, q_ref, cxt_ref,
-    mt_ref, qb_ref, sy_ref, mw_ref, mtw_ref, m_sc,
+    ccd_devs, rows, srow_ref, pid_ref, live_ref, q_ref, const_ref,
+    qb_ref, sy_ref, mw_ref, mtw_ref, keep_ref, m_sc,
 ):
     owners, slots = srow_ref.shape
     vis = q_ref.shape[0] // ORDER
@@ -213,15 +214,14 @@
 
     sy = lax.fori_loop(0, owners, body, jnp.zeros((4 * ORDER, n), F32), unroll=4)
     sy = sy[:ORDER] + sy[ORDER : 2 * ORDER] + sy[2 * ORDER : 3 * ORDER]
-    sy_ref[...] = jnp.concatenate([sy, jnp.zeros((ORDER, 128 - n), F32)], axis=1)
+    sy_ref[...] = widen(sy)
     m_hi, m_lo = split(m_sc[...], 2)
-    mt = m_sc[...].T[:n]
-    mt_ref[...] = mt
-    mt_hi, mt_lo = split(mt, 2)
-    mtw_ref[...] = jnp.concatenate([mt_hi, mt_hi, mt_lo, jnp.zeros_like(mt_hi)], axis=0)
+    mtw_ref[...] = jnp.concatenate(split(m_sc[...].T[:n], 2), axis=0)
+    keep_ref[...] = const_ref[...]
     mw_ref[0] = m_hi
     mw_ref[1] = m_lo
-    qb_ref[...] = blocks_of(dot_t(q_ref[...], tile_rows(cxt_ref[...], 128 // ORDER), HI), vis)
+    full = dot_t(q_ref[...], tile_rows(const_ref[CXT], vis), HI)
+    qb_ref[...] = widen(blocks_of(full, vis))
 
 
 def tile_rows(x, times):
@@ -236,12 +236,18 @@
     return out
 
 
-def moments_block(mt, back, q, vis):
-    full = None
-    for i, piece in enumerate(back):
-        part = dot_t(mt[:, 128 * i : 128 * (i + 1)], tile_rows(piece, 128 // ORDER), HI)
-        full = part if full is None else full + part
-    return q - blocks_of(full, vis)
+def widen(x):
+    return jnp.concatenate([x, jnp.zeros((x.shape[0], 128 - x.shape[1]), F32)], axis=1)
+
+
+def moments_block(mtw_ref, back, q):
+    n = mtw_ref.shape[0] // 2
+    vis = n // ORDER
+    b_hi, b_lo = split(back, 2)
+    b_hi, b_lo = (tile_rows(x.astype(F32), vis).astype(BF16) for x in (b_hi, b_lo))
+    full = dot_t(mtw_ref[...], b_hi)
+    full = full[:n] + full[n:] + dot_t(mtw_ref[0:n], b_lo)
+    return q - widen(blocks_of(full, vis))
 
 
 def senders_sum(ref, lo, hi):
@@ -251,36 +257,38 @@
     return total
 
 
-def first_kernel(arr_ref, mt_ref, qb_ref, sy_ref, b_ref, den_ref, pay_ref):
+def first_kernel(arr_ref, mtw_ref, qb_ref, sy_ref, b_ref, den_ref, pay_ref):
     blocks = b_ref.shape[1] // 128
-    vis = mt_ref.shape[0] // ORDER
     total = senders_sum(arr_ref, 0, arr_ref.shape[1])
-    back = []
+    back, dens = [], []
     for q in range(blocks):
         den = total[ORDER * blocks + q : ORDER * blocks + q + 1] + 1.0
-        den = jnp.broadcast_to(den, (ORDER, 128))
-        piece = total[ORDER * q : ORDER * (q + 1)] / den
-        den_ref[:, 128 * q : 128 * (q + 1)] = den
-        b_ref[:, 128 * q : 128 * (q + 1)] = piece
-        back.append(piece)
-    mom = moments_block(mt_ref[...], back, qb_ref[...], vis)
+        dens.append(jnp.broadcast_to(den, (ORDER, 128)))
+        back.append(total[ORDER * q : ORDER * (q + 1)] / dens[-1])
+    back = jnp.concatenate(back, axis=1)
+    den_ref[...] = jnp.concatenate(dens, axis=1)
+    b_ref[...] = back
+    mom = moments_block(mtw_ref, back, qb_ref[...])
     block = jnp.concatenate([mom, sy_ref[...]], axis=0)
     for i in range(pay_ref.shape[0]):
         pay_ref[i] = block
 
 
-def solve(mom, sy, lam, vis):
+def systems(sy, lam, vis):
     n = vis * ORDER
     rows, lanes = iota((n, ORDER * 128), 0), iota((n, ORDER * 128), 1)
     pos = lanes % 128
     pick = (rows // ORDER == pos // ORDER) & (rows % ORDER == lanes // 128)
     spread = dot(sy[:, :n], jnp.where(pick, 1.0, 0.0), HI)
     sub = iota((ORDER, 128), 0)
-    mat = [
+    return [
         spread[:, 128 * b : 128 * (b + 1)] * lam + jnp.where(sub == b, RIDGE, 0.0)
         for b in range(ORDER)
     ]
-    rhs = [mom[b : b + 1] for b in range(ORDER)]
+
+
+def eliminate(mat, rhs):
+    mat, rhs = list(mat), list(rhs)
     for p in range(ORDER):
         inv = 1.0 / mat[p][p : p + 1]
         mat[p] = mat[p] * inv
@@ -290,10 +298,16 @@
                 factor = mat[b][p : p + 1]
                 mat[b] = mat[b] - factor * mat[p]
                 rhs[b] = rhs[b] - factor * rhs[p]
+    return rhs
+
+
+def solve(mom, sy, lam, vis):
+    rhs = eliminate(systems(sy, lam, vis), [mom[b : b + 1] for b in range(ORDER)])
+    sub = iota((ORDER, 128), 0)
     out = jnp.zeros((ORDER, 128), F32)
     for b in range(ORDER):
         out = jnp.where(sub == b, rhs[b], out)
-    return jnp.where(iota((ORDER, 128), 1) < n, out, 0.0)
+    return jnp.where(iota((ORDER, 128), 1) < vis * ORDER, out, 0.0)
 
 
 def block_diag_t(z, vis):
@@ -303,26 +317,24 @@
     return jnp.where(keep, tiled, 0.0).T[:n]
 
 
-def model_kernel(arr_ref, lam_ref, mtw_ref, mw_ref, t_ref, cxt_ref, sy_ref, pay_ref):
-    vis = mtw_ref.shape[0] // (4 * ORDER)
+def model_kernel(arr_ref, const_ref, mtw_ref, mw_ref, t_ref, sy_ref, pay_ref):
+    vis = mtw_ref.shape[0] // (2 * ORDER)
     n = vis * ORDER
     total = arr_ref[0]
     for i in range(1, arr_ref.shape[0]):
         total = total + arr_ref[i]
     sy_ref[...] = total[ORDER:]
-    z = solve(total[:ORDER], total[ORDER:], lam_ref[0:1], vis)
+    z = solve(total[:ORDER], total[ORDER:], const_ref[LAM_LANE], vis)
     diag = block_diag_t(z, vis)
     weights = diag[:ORDER]
     for v in range(1, vis):
         weights = weights + diag[v * ORDER : (v + 1) * ORDER]
     w_hi, w_lo = split(weights, 2)
     model = (
-        dot(w_hi, mtw_ref[0:n])
-        + dot(w_lo, mtw_ref[n : 2 * n])
-        + dot(w_hi, mtw_ref[2 * n : 3 * n])
+        dot(w_hi, mtw_ref[0:n]) + dot(w_lo, mtw_ref[0:n]) + dot(w_hi, mtw_ref[n : 2 * n])
     )
     surface = lax.dot_general(
-        weights, cxt_ref[...], (((0,), (0,)), ((), ())), precision=HI, preferred_element_type=F32
+        weights, const_ref[CXT], (((0,), (0,)), ((), ())), precision=HI, preferred_element_type=F32
     )
     surface = jnp.concatenate([surface, jnp.zeros((128 - n, 128), F32)], axis=0)
     s_hi, s_lo = split(surface, 2)
@@ -337,22 +349,19 @@
         pay_ref[i, rows : rows + P_DEV] = corrected[P_DEV * i : P_DEV * (i + 1)].astype(BF16)
 
 
-def second_kernel(arr_ref, b_ref, den_ref, mt_ref, qb_ref, lam_ref, pay_ref):
+def second_kernel(arr_ref, b_ref, den_ref, mtw_ref, qb_ref, const_ref, pay_ref):
     blocks = b_ref.shape[1] // 128
-    vis = mt_ref.shape[0] // ORDER
     total = senders_sum(arr_ref, 0, ORDER * blocks)
-    lam = lam_ref[:, 0:1]
-    back = []
-    for q in range(blocks):
-        cols = slice(128 * q, 128 * (q + 1))
-        model = total[ORDER * q : ORDER * (q + 1)]
-        back.append(b_ref[:, cols] - lam * model / den_ref[:, cols])
-    mom = moments_block(mt_ref[...], back, qb_ref[...], vis)
+    model = jnp.concatenate(
+        [total[ORDER * q : ORDER * (q + 1)] for q in range(blocks)], axis=1
+    )
+    lam = const_ref[LAM_SUB][:, 0:1]
+    mom = moments_block(mtw_ref, b_ref[...] - lam * model / den_ref[...], qb_ref[...])
     for i in range(pay_ref.shape[0]):
         pay_ref[i] = mom
 
 
-def background_kernel(arr_ref, den_ref, out_ref):
+def background_kernel(vis, arr_ref, den_ref, sy_ref, const_ref, out_ref, inv_ref):
     rows = arr_ref.shape[1] - P_DEV
     sums = senders_sum(arr_ref, rows, rows + P_DEV)
     own = lax.axis_index("visit") * P_DEV
@@ -360,16 +369,23 @@
     pick = iota((P_DEV, width), 1) == iota((P_DEV, width), 0) + own
     den = dot_t(jnp.where(pick, 1.0, 0.0), den_ref[...], HI)
     out_ref[...] = sums / den[:, 0:1]
-
-
-def final_kernel(arr_ref, sy_ref, lam_ref, rot_ref, out_ref):
+    sub = iota((ORDER, 128), 0)
+    unit = [jnp.where(sub == b, 1.0, 0.0) for b in range(ORDER)]
+    inverse = eliminate(systems(sy_ref[...], const_ref[LAM_LANE], vis), unit)
+    for b in range(ORDER):
+        inv_ref[b] = inverse[b]
+
+
+def final_kernel(arr_ref, inv_ref, const_ref, out_ref):
     vis = out_ref.shape[0]
     n = vis * ORDER
     total = arr_ref[0]
     for i in range(1, arr_ref.shape[0]):
         total = total + arr_ref[i]
-    z = solve(total, sy_ref[...], lam_ref[0:1], vis)
-    flat = tile_rows(z, ORDER).T[:n] * tile_rows(rot_ref[...], vis)
+    z = inv_ref[0] * total[0:1]
+    for d in range(1, ORDER):
+        z = z + inv_ref[d] * total[d : d + 1]
+    flat = tile_rows(z, ORDER).T[:n] * tile_rows(const_ref[ROT][:, : ORDER * ORDER], vis)
     for v in range(vis):
         out_ref[v : v + 1] = jnp.sum(flat[v * ORDER : (v + 1) * ORDER], axis=0, keepdims=True)
 
@@ -415,12 +431,12 @@
     blocks = patches // 128
     nvb = vis * ORDER
     lam, rot, cxt = constants(pix)
-    lam_lane = np.zeros((8, 128))
-    lam_lane[0, :nvb] = np.tile(lam, vis)
-    lam_sub = np.broadcast_to(lam[:, None], (8, 128))
-    lam_lane, lam_sub = jnp.asarray(lam_lane, F32), jnp.asarray(lam_sub, F32)
-    cxt = jnp.asarray(cxt, F32)
-    rot = jnp.asarray(np.repeat(rot.T, ORDER, axis=1), F32)
+    const = np.zeros((32, 128))
+    const[CXT] = cxt
+    const[LAM_LANE, :nvb] = np.tile(lam, vis)
+    const[LAM_SUB] = lam[:, None]
+    const[ROT, : ORDER * ORDER] = np.repeat(rot.T, ORDER, axis=1)
+    const = jnp.asarray(const, F32)
     srow, pid, live = slot_row[0, 0], patch_id[0, 0], live_mask[0, 0]
     weights = tap_weight[:, 0, 0]
     pay_rows = ORDER * blocks + P_DEV
@@ -450,21 +466,21 @@
         ),
         n_in=8,
         hbm=range(8),
-    )(srow.reshape(-1), raw_rows, resample, srow, weights, pid, live, cxt)
+    )(srow.reshape(-1), raw_rows, resample, srow, weights, pid, live, const)
     arr1 = exchange(pay1, "visit")
-    mt, qb, sy, mw, mtw = call(
+    qb, sy, mw, mtw, const = call(
         functools.partial(design_kernel, ccd_devs, rows),
         (
-            shape((nvb, patches)),
             shape((ORDER, 128)),
             shape((ORDER, 128)),
             shape((2, patches, 128), BF16),
-            shape((4 * nvb, patches), BF16),
+            shape((2 * nvb, patches), BF16),
+            shape(const.shape),
         ),
         scratch=(pltpu.VMEM((patches, 128), F32),),
         n_in=5,
         plain=(0, 1, 2, 4),
-    )(srow, pid, live, qsum, cxt)
+    )(srow, pid, live, qsum, const)
     back, den, pay2 = call(
         first_kernel,
         (
@@ -473,24 +489,24 @@
             shape((ccd_devs, 2 * ORDER, 128)),
         ),
         n_in=4,
-    )(arr1, mt, qb, sy)
+    )(arr1, mtw, qb, sy)
     arr2 = exchange(pay2, "ccd")
     sy_all, pay3 = call(
         model_kernel,
         (shape((ORDER, 128)), shape((owners, pay_rows, 128), BF16)),
-        n_in=6,
-    )(arr2, lam_lane, mtw, mw, tsum, cxt)
+        n_in=5,
+    )(arr2, const, mtw, mw, tsum)
     arr3 = exchange(pay3, "visit")
-    pay4 = call(
-        second_kernel,
-        shape((ccd_devs, ORDER, 128)),
-        n_in=6,
-    )(arr3, back, den, mt, qb, lam_sub)
+    pay4 = call(second_kernel, shape((ccd_devs, ORDER, 128)), n_in=6)(
+        arr3, back, den, mtw, qb, const
+    )
     arr4 = exchange(pay4, "ccd")
-    background = call(background_kernel, result((P_DEV, pix)), n_in=2)(arr3, den)
-    offsets = call(final_kernel, result((vis, ORDER * ORDER)), n_in=4)(
-        arr4, sy_all, lam_lane, rot
-    )
+    background, inverse = call(
+        functools.partial(background_kernel, vis),
+        (result((P_DEV, pix)), shape((ORDER, ORDER, 128))),
+        n_in=4,
+    )(arr3, den, sy_all, const)
+    offsets = call(final_kernel, result((vis, ORDER * ORDER)), n_in=3)(arr4, inverse, const)
     return offsets, background
 
 

time: 70.1 us -> 68.5 us (0.977)
  Pallas kernels: 13.3 us -> 12.4 us
  local copies, waits for them, and re-layouts: 0.71 us -> 0 us
    pallas_call x7, Pallas kernels: 13.3 us -> 12.4 us  [run(): fn(*(x if i in plain or i in hbm else pltpu.with_memory_space_constraint(...]
    unnamed x8 -> x0, local copies, waits for them, and re-layouts: 0.71 us -> none
where the time goes in v4:
time: 68.5 us; the launch traced here: 67.9 us
  blocking collectives  30.3 us (44%)
  waiting for transfers between devices  12.6 us (18%)
  Pallas kernels  12.4 us (18%)
  starting transfers between devices  11.9 us (17%)
    all_to_all x2, blocking collectives, exchange(): return lax.all_to_all(x, axis, split_axis=0, concat_axis=0, tiled=True)  30.3 us
    all_to_all x2, waiting for transfers between devices, exchange(): return lax.all_to_all(x, axis, split_axis=0, concat_axis=0, tiled=True)  12.6 us
    pallas_call x7, Pallas kernels, run(): fn(*(x if i in plain or i in hbm else pltpu.with_memory_space_constraint(...  12.4 us
    all_to_all x2, starting transfers between devices, exchange(): return lax.all_to_all(x, axis, split_axis=0, concat_axis=0, tiled=True)  11.9 us
  transfers between devices with their start and end apart: 2, of which 2 were waited for; matrix products, arithmetic and copies ran while one was open for 0% of the time, Pallas kernels for 6%

profile of v4, /device:TPU:1, one launch (start us, length us, event | category | flops | bytes accessed | tf_op | source)
XLA Modules:
  0.0 67.9 jit_solution(9013919794710304700)
XLA Ops:
  0.6 6.0 %shard_map.86 = (bf16[32,40,128]{2,1,0:T(8,128)(2,1)}, f32[512,128]{1,0:T(8,128)S(1)}, f32[32,128]{1,0:T(8,128)S(1)}) custom-call(s32[4096]{0:T(1024)} %bitcast.5, bf16[4,1024,128]{2,1,0:T(8,128)(2,1)} %raw_hbm.1, bf16[4,128,128]{2,1,0:T(8,128)(2,1)} %res_hbm.1, s32[32,128]{1,0:T(8,128)} %bitcast.6, f32[4,32,128]{2,1,0:T(8,128)} %bitcast.8, ...), custom_call_target="tpu_custom_call" | custom-call | tf_op jit(solution)/shard_map/pallas_call | solution.py:403
  6.6 8.6 %all-to-all-start = ((bf16[32,40,128]{2,1,0:T(8,128)(2,1)}), bf16[32,40,128]{2,1,0:T(8,128)(2,1)S(1)}, u32[]{:S(2)}, u32[]{:S(2)}) async-start(bf16[32,40,128]{2,1,0:T(8,128)(2,1)} %get-tuple-element.17), calls=%async_computation | async-start | bytes 655360 | tf_op jit(solution)/shard_map/all_to_all | solution.py:422
  15.2 3.0 %shard_map.87 = (f32[8,128]{1,0:T(8,128)S(1)}, f32[8,128]{1,0:T(8,128)S(1)}, bf16[2,512,128]{2,1,0:T(8,128)(2,1)S(1)}, bf16[64,512]{1,0:T(8,128)(2,1)S(1)}, f32[32,128]{1,0:T(8,128)S(1)}) custom-call(s32[32,128]{1,0:T(8,128)} %bitcast.7, s32[32,128]{1,0:T(8,128)} %bitcast.10, s32[32,128]{1,0:T(8,128)} %bitcast.12, f32[32,128]{1,0:T(8,128)S(1)} %get-tuple-element.18.q_ref, ...), custom_call_target="tpu_custom_call" | custom-call | tf_op jit(solution)/shard_map/pallas_call | solution.py:403
  18.2 6.7 %all-to-all-done.arr_ref = bf16[32,40,128]{2,1,0:T(8,128)(2,1)S(1)} async-done(((bf16[32,40,128]{2,1,0:T(8,128)(2,1)}), bf16[32,40,128]{2,1,0:T(8,128)(2,1)S(1)}, u32[]{:S(2)}, u32[]{:S(2)}) %all-to-all-start) | async-done | bytes 327712 | tf_op jit(solution)/shard_map/all_to_all | solution.py:422
  24.8 0.2 shard_map.88
  25.1 15.1 %all_to_all.20.arr_ref = f32[8,16,128]{2,1,0:T(8,128)S(1)} all-to-all(f32[8,16,128]{2,1,0:T(8,128)S(1)} %get-tuple-element.22), channel_id=1, replica_groups=mesh['visit'=32,'ccd'=8] {'ccd'}, dimensions={0} | all-to-all | bytes 131072 | tf_op jit(solution)/shard_map/all_to_all | solution.py:422
  40.2 0.8 %shard_map.89 = (f32[8,128]{1,0:T(8,128)S(1)}, bf16[32,48,128]{2,1,0:T(8,128)(2,1)S(1)}) custom-call(f32[8,16,128]{2,1,0:T(8,128)S(1)} %all_to_all.20.arr_ref, f32[32,128]{1,0:T(8,128)S(1)} %get-tuple-element.23.const_ref, bf16[64,512]{1,0:T(8,128)(2,1)S(1)} %get-tuple-element.19.mtw_ref, bf16[2,512,128]{2,1,0:T(8,128)(2,1)S(1)} %get-tuple-element.24.mw_ref, ...), custom_call_target="tpu_custom_call" | custom-call | tf_op jit(solution)/shard_map/pallas_call | solution.py:403
  41.0 15.2 %all_to_all.21.arr_ref = bf16[32,48,128]{2,1,0:T(8,128)(2,1)S(1)} all-to-all(bf16[32,48,128]{2,1,0:T(8,128)(2,1)S(1)} %get-tuple-element.26), channel_id=1, replica_groups=mesh['visit'=32,'ccd'=8] {'visit'}, dimensions={0} | all-to-all | bytes 786432 | tf_op jit(solution)/shard_map/all_to_all | solution.py:422
  56.2 0.8 %shard_map.90 = f32[8,8,128]{2,1,0:T(8,128)} custom-call(bf16[32,48,128]{2,1,0:T(8,128)(2,1)S(1)} %all_to_all.21.arr_ref, f32[8,512]{1,0:T(8,128)S(1)} %get-tuple-element.27.b_ref, f32[8,512]{1,0:T(8,128)S(1)} %get-tuple-element.28.den_ref, bf16[64,512]{1,0:T(8,128)(2,1)S(1)} %get-tuple-element.19.mtw_ref, f32[8,128]{1,0:T(8,128)S(1)} %get-tuple-element.20.qb_ref, ...), custom_call_target="tpu_custom_call" | custom-call | tf_op jit(solution)/shard_map/pallas_call | solution.py:403
  57.1 3.3 %all-to-all-start.3 = ((f32[8,8,128]{2,1,0:T(8,128)}), f32[8,8,128]{2,1,0:T(8,128)S(1)}, u32[]{:S(2)}, u32[]{:S(2)}) async-start(f32[8,8,128]{2,1,0:T(8,128)} %shard_map.90), calls=%async_computation.3 | async-start | bytes 65536 | tf_op jit(solution)/shard_map/all_to_all | solution.py:422
  60.4 0.9 %shard_map.91 = (f32[16,128]{1,0:T(8,128)}, f32[8,8,128]{2,1,0:T(8,128)S(1)}) custom-call(bf16[32,48,128]{2,1,0:T(8,128)(2,1)S(1)} %all_to_all.21.arr_ref, f32[8,512]{1,0:T(8,128)S(1)} %get-tuple-element.28.den_ref, f32[8,128]{1,0:T(8,128)S(1)} %get-tuple-element.29.sy_ref, f32[32,128]{1,0:T(8,128)S(1)} %get-tuple-element.23.const_ref), custom_call_target="tpu_custom_call" | custom-call | tf_op jit(solution)/shard_map/pallas_call | solution.py:403
  61.3 5.9 %all-to-all-done.3.arr_ref = f32[8,8,128]{2,1,0:T(8,128)S(1)} async-done(((f32[8,8,128]{2,1,0:T(8,128)}), f32[8,8,128]{2,1,0:T(8,128)S(1)}, u32[]{:S(2)}, u32[]{:S(2)}) %all-to-all-start.3) | async-done | bytes 32800 | tf_op jit(solution)/shard_map/all_to_all | solution.py:422
  67.2 0.7 shard_map.92
Async XLA Ops:
  6.6 18.2 %all-to-all-start = ((bf16[32,40,128]{2,1,0:T(8,128)(2,1)}), bf16[32,40,128]{2,1,0:T(8,128)(2,1)S(1)}, u32[]{:S(2)}, u32[]{:S(2)}) async-start(bf16[32,40,128]{2,1,0:T(8,128)(2,1)} %get-tuple-element.17), calls=%async_computation | async-start | bytes 655360 | tf_op jit(solution)/shard_map/all_to_all | solution.py:422
  57.1 10.1 %all-to-all-start.3 = ((f32[8,8,128]{2,1,0:T(8,128)}), f32[8,8,128]{2,1,0:T(8,128)S(1)}, u32[]{:S(2)}, u32[]{:S(2)}) async-start(f32[8,8,128]{2,1,0:T(8,128)} %shard_map.90), calls=%async_computation.3 | async-start | bytes 65536 | tf_op jit(solution)/shard_map/all_to_all | solution.py:422

commit v5 on v4

--- a/solution.py
+++ b/solution.py
@@ -12,7 +12,7 @@
 TAPS = 4
 P_DEV = 16
 RIDGE = 1.0
-UNROLL = 8
+UNROLL = 16
 CXT, LAM_LANE, LAM_SUB, ROT = (slice(8 * i, 8 * (i + 1)) for i in range(4))
 HI = lax.Precision.HIGHEST
 F32 = jnp.float32
@@ -218,8 +218,9 @@
     m_hi, m_lo = split(m_sc[...], 2)
     mtw_ref[...] = jnp.concatenate(split(m_sc[...].T[:n], 2), axis=0)
     keep_ref[...] = const_ref[...]
-    mw_ref[0] = m_hi
-    mw_ref[1] = m_lo
+    m_hi, m_lo = m_hi.astype(F32), m_lo.astype(F32)
+    wide = m_hi + pltpu.roll(m_hi, n, 1) + pltpu.roll(m_lo, 2 * n, 1)
+    mw_ref[...] = wide.astype(BF16)
     full = dot_t(q_ref[...], tile_rows(const_ref[CXT], vis), HI)
     qb_ref[...] = widen(blocks_of(full, vis))
 
@@ -238,6 +239,35 @@
 
 def widen(x):
     return jnp.concatenate([x, jnp.zeros((x.shape[0], 128 - x.shape[1]), F32)], axis=1)
+
+
+def pack(x):
+    turned = [x] + [pltpu.roll(x, 32 * g, 1) for g in range(1, 4)]
+    out = []
+    for r in range(ORDER // 4):
+        row = turned[0][4 * r : 4 * r + 1]
+        for g in range(1, 4):
+            row = row + turned[g][4 * r + g : 4 * r + g + 1]
+        out.append(row)
+    return out
+
+
+def unpack(x):
+    out = []
+    for row in x:
+        row = jnp.broadcast_to(row, (ORDER, 128))
+        out.append(row[0:1])
+        for g in range(1, 4):
+            out.append(pltpu.roll(row, 128 - 32 * g, 1)[0:1])
+    return out
+
+
+def stack(rows):
+    sub = iota((8, 128), 0)
+    out = jnp.broadcast_to(rows[0], (8, 128))
+    for i in range(1, len(rows)):
+        out = jnp.where(sub == i, rows[i], out)
+    return out
 
 
 def moments_block(mtw_ref, back, q):
@@ -269,7 +299,7 @@
     den_ref[...] = jnp.concatenate(dens, axis=1)
     b_ref[...] = back
     mom = moments_block(mtw_ref, back, qb_ref[...])
-    block = jnp.concatenate([mom, sy_ref[...]], axis=0)
+    block = stack(pack(mom) + pack(sy_ref[...]))[: pay_ref.shape[1]]
     for i in range(pay_ref.shape[0]):
         pay_ref[i] = block
 
@@ -302,11 +332,7 @@
 
 
 def solve(mom, sy, lam, vis):
-    rhs = eliminate(systems(sy, lam, vis), [mom[b : b + 1] for b in range(ORDER)])
-    sub = iota((ORDER, 128), 0)
-    out = jnp.zeros((ORDER, 128), F32)
-    for b in range(ORDER):
-        out = jnp.where(sub == b, rhs[b], out)
+    out = stack(eliminate(systems(sy, lam, vis), mom))
     return jnp.where(iota((ORDER, 128), 1) < vis * ORDER, out, 0.0)
 
 
@@ -323,8 +349,11 @@
     total = arr_ref[0]
     for i in range(1, arr_ref.shape[0]):
         total = total + arr_ref[i]
-    sy_ref[...] = total[ORDER:]
-    z = solve(total[:ORDER], total[ORDER:], const_ref[LAM_LANE], vis)
+    rows = ORDER // 4
+    sy = stack(unpack([total[i : i + 1] for i in range(rows, 2 * rows)]))
+    sy_ref[...] = sy
+    mom = unpack([total[i : i + 1] for i in range(rows)])
+    z = solve(mom, sy, const_ref[LAM_LANE], vis)
     diag = block_diag_t(z, vis)
     weights = diag[:ORDER]
     for v in range(1, vis):
@@ -336,9 +365,9 @@
     surface = lax.dot_general(
         weights, const_ref[CXT], (((0,), (0,)), ((), ())), precision=HI, preferred_element_type=F32
     )
-    surface = jnp.concatenate([surface, jnp.zeros((128 - n, 128), F32)], axis=0)
     s_hi, s_lo = split(surface, 2)
-    corrected = t_ref[...] - (dot(mw_ref[0], s_hi) + dot(mw_ref[0], s_lo) + dot(mw_ref[1], s_hi))
+    surface = jnp.concatenate([s_hi, s_lo, s_hi, jnp.zeros((128 - 3 * n, 128), BF16)], axis=0)
+    corrected = t_ref[...] - dot(mw_ref[...], surface)
     blocks = model.shape[1] // 128
     block = jnp.concatenate(
         [model[:, 128 * q : 128 * (q + 1)] for q in range(blocks)], axis=0
@@ -357,8 +386,9 @@
     )
     lam = const_ref[LAM_SUB][:, 0:1]
     mom = moments_block(mtw_ref, b_ref[...] - lam * model / den_ref[...], qb_ref[...])
+    block = stack(pack(mom))[: pay_ref.shape[1]]
     for i in range(pay_ref.shape[0]):
-        pay_ref[i] = mom
+        pay_ref[i] = block
 
 
 def background_kernel(vis, arr_ref, den_ref, sy_ref, const_ref, out_ref, inv_ref):
@@ -382,9 +412,10 @@
     total = arr_ref[0]
     for i in range(1, arr_ref.shape[0]):
         total = total + arr_ref[i]
-    z = inv_ref[0] * total[0:1]
+    mom = unpack([total[i : i + 1] for i in range(ORDER // 4)])
+    z = inv_ref[0] * mom[0]
     for d in range(1, ORDER):
-        z = z + inv_ref[d] * total[d : d + 1]
+        z = z + inv_ref[d] * mom[d]
     flat = tile_rows(z, ORDER).T[:n] * tile_rows(const_ref[ROT][:, : ORDER * ORDER], vis)
     for v in range(vis):
         out_ref[v : v + 1] = jnp.sum(flat[v * ORDER : (v + 1) * ORDER], axis=0, keepdims=True)
@@ -473,7 +504,7 @@
         (
             shape((ORDER, 128)),
             shape((ORDER, 128)),
-            shape((2, patches, 128), BF16),
+            shape((patches, 128), BF16),
             shape((2 * nvb, patches), BF16),
             shape(const.shape),
         ),
@@ -486,7 +517,7 @@
         (
             shape((ORDER, patches)),
             shape((ORDER, patches)),
-            shape((ccd_devs, 2 * ORDER, 128)),
+            shape((ccd_devs, ORDER // 2, 128)),
         ),
         n_in=4,
     )(arr1, mtw, qb, sy)
@@ -497,7 +528,7 @@
         n_in=5,
     )(arr2, const, mtw, mw, tsum)
     arr3 = exchange(pay3, "visit")
-    pay4 = call(second_kernel, shape((ccd_devs, ORDER, 128)), n_in=6)(
+    pay4 = call(second_kernel, shape((ccd_devs, ORDER // 4, 128)), n_in=6)(
         arr3, back, den, mtw, qb, const
     )
     arr4 = exchange(pay4, "ccd")

time: 68.5 us -> 67.5 us (0.985)
  no operation moved by 1% of the time
where the time goes in v5:
time: 67.5 us; the launch traced here: 66.9 us
  blocking collectives  29.7 us (44%)
  Pallas kernels  12.4 us (18%)
  waiting for transfers between devices  12.2 us (18%)
  starting transfers between devices  11.9 us (18%)
    all_to_all x2, blocking collectives, exchange(): return lax.all_to_all(x, axis, split_axis=0, concat_axis=0, tiled=True)  29.7 us
    pallas_call x7, Pallas kernels, run(): fn(*(x if i in plain or i in hbm else pltpu.with_memory_space_constraint(...  12.4 us
    all_to_all x2, waiting for transfers between devices, exchange(): return lax.all_to_all(x, axis, split_axis=0, concat_axis=0, tiled=True)  12.2 us
    all_to_all x2, starting transfers between devices, exchange(): return lax.all_to_all(x, axis, split_axis=0, concat_axis=0, tiled=True)  11.9 us
  transfers between devices with their start and end apart: 2, of which 2 were waited for; matrix products, arithmetic and copies ran while one was open for 0% of the time, Pallas kernels for 6%

profile of v5, /device:TPU:1, one launch (start us, length us, event | category | flops | bytes accessed | tf_op | source)
XLA Modules:
  0.0 66.9 jit_solution(16288224419917871082)
XLA Ops:
  0.6 5.7 %shard_map.86 = (bf16[32,40,128]{2,1,0:T(8,128)(2,1)}, f32[512,128]{1,0:T(8,128)S(1)}, f32[32,128]{1,0:T(8,128)S(1)}) custom-call(s32[4096]{0:T(1024)} %bitcast.5, bf16[4,1024,128]{2,1,0:T(8,128)(2,1)} %raw_hbm.1, bf16[4,128,128]{2,1,0:T(8,128)(2,1)} %res_hbm.1, s32[32,128]{1,0:T(8,128)} %bitcast.6, f32[4,32,128]{2,1,0:T(8,128)} %bitcast.8, ...), custom_call_target="tpu_custom_call" | custom-call | tf_op jit(solution)/shard_map/pallas_call | solution.py:434
  6.4 8.6 %all-to-all-start = ((bf16[32,40,128]{2,1,0:T(8,128)(2,1)}), bf16[32,40,128]{2,1,0:T(8,128)(2,1)S(1)}, u32[]{:S(2)}, u32[]{:S(2)}) async-start(bf16[32,40,128]{2,1,0:T(8,128)(2,1)} %get-tuple-element.17), calls=%async_computation | async-start | bytes 655360 | tf_op jit(solution)/shard_map/all_to_all | solution.py:453
  15.0 3.0 %shard_map.87 = (f32[8,128]{1,0:T(8,128)S(1)}, f32[8,128]{1,0:T(8,128)S(1)}, bf16[512,128]{1,0:T(8,128)(2,1)S(1)}, bf16[64,512]{1,0:T(8,128)(2,1)S(1)}, f32[32,128]{1,0:T(8,128)S(1)}) custom-call(s32[32,128]{1,0:T(8,128)} %bitcast.7, s32[32,128]{1,0:T(8,128)} %bitcast.10, s32[32,128]{1,0:T(8,128)} %bitcast.12, f32[32,128]{1,0:T(8,128)S(1)} %get-tuple-element.18.q_ref, ...), custom_call_target="tpu_custom_call" | custom-call | tf_op jit(solution)/shard_map/pallas_call | solution.py:434
  18.0 6.6 %all-to-all-done.arr_ref = bf16[32,40,128]{2,1,0:T(8,128)(2,1)S(1)} async-done(((bf16[32,40,128]{2,1,0:T(8,128)(2,1)}), bf16[32,40,128]{2,1,0:T(8,128)(2,1)S(1)}, u32[]{:S(2)}, u32[]{:S(2)}) %all-to-all-start) | async-done | bytes 327712 | tf_op jit(solution)/shard_map/all_to_all | solution.py:453
  24.6 0.3 shard_map.88
  24.9 14.6 %all_to_all.20.arr_ref = f32[8,4,128]{2,1,0:T(4,128)S(1)} all-to-all(f32[8,4,128]{2,1,0:T(4,128)S(1)} %get-tuple-element.22), channel_id=1, replica_groups=mesh['visit'=32,'ccd'=8] {'ccd'}, dimensions={0} | all-to-all | bytes 32768 | tf_op jit(solution)/shard_map/all_to_all | solution.py:453
  39.5 0.8 %shard_map.89 = (f32[8,128]{1,0:T(8,128)S(1)}, bf16[32,48,128]{2,1,0:T(8,128)(2,1)S(1)}) custom-call(f32[8,4,128]{2,1,0:T(4,128)S(1)} %all_to_all.20.arr_ref, f32[32,128]{1,0:T(8,128)S(1)} %get-tuple-element.23.const_ref, bf16[64,512]{1,0:T(8,128)(2,1)S(1)} %get-tuple-element.19.mtw_ref, bf16[512,128]{1,0:T(8,128)(2,1)S(1)} %get-tuple-element.24.mw_ref, ...), custom_call_target="tpu_custom_call" | custom-call | tf_op jit(solution)/shard_map/pallas_call | solution.py:434
  40.3 15.1 %all_to_all.21.arr_ref = bf16[32,48,128]{2,1,0:T(8,128)(2,1)S(1)} all-to-all(bf16[32,48,128]{2,1,0:T(8,128)(2,1)S(1)} %get-tuple-element.26), channel_id=1, replica_groups=mesh['visit'=32,'ccd'=8] {'visit'}, dimensions={0} | all-to-all | bytes 786432 | tf_op jit(solution)/shard_map/all_to_all | solution.py:453
  55.4 0.9 %shard_map.90 = f32[8,2,128]{2,1,0:T(2,128)} custom-call(bf16[32,48,128]{2,1,0:T(8,128)(2,1)S(1)} %all_to_all.21.arr_ref, f32[8,512]{1,0:T(8,128)S(1)} %get-tuple-element.27.b_ref, f32[8,512]{1,0:T(8,128)S(1)} %get-tuple-element.28.den_ref, bf16[64,512]{1,0:T(8,128)(2,1)S(1)} %get-tuple-element.19.mtw_ref, f32[8,128]{1,0:T(8,128)S(1)} %get-tuple-element.20.qb_ref, ...), custom_call_target="tpu_custom_call" | custom-call | tf_op jit(solution)/shard_map/pallas_call | solution.py:434
  56.3 3.3 %all-to-all-start.3 = ((f32[8,2,128]{2,1,0:T(2,128)}), f32[8,2,128]{2,1,0:T(2,128)S(1)}, u32[]{:S(2)}, u32[]{:S(2)}) async-start(f32[8,2,128]{2,1,0:T(2,128)} %shard_map.90), calls=%async_computation.3 | async-start | bytes 16384 | tf_op jit(solution)/shard_map/all_to_all | solution.py:453
  59.6 0.9 %shard_map.91 = (f32[16,128]{1,0:T(8,128)}, f32[8,8,128]{2,1,0:T(8,128)S(1)}) custom-call(bf16[32,48,128]{2,1,0:T(8,128)(2,1)S(1)} %all_to_all.21.arr_ref, f32[8,512]{1,0:T(8,128)S(1)} %get-tuple-element.28.den_ref, f32[8,128]{1,0:T(8,128)S(1)} %get-tuple-element.29.sy_ref, f32[32,128]{1,0:T(8,128)S(1)} %get-tuple-element.23.const_ref), custom_call_target="tpu_custom_call" | custom-call | tf_op jit(solution)/shard_map/pallas_call | solution.py:434
  60.5 5.6 %all-to-all-done.3.arr_ref = f32[8,2,128]{2,1,0:T(2,128)S(1)} async-done(((f32[8,2,128]{2,1,0:T(2,128)}), f32[8,2,128]{2,1,0:T(2,128)S(1)}, u32[]{:S(2)}, u32[]{:S(2)}) %all-to-all-start.3) | async-done | bytes 8224 | tf_op jit(solution)/shard_map/all_to_all | solution.py:453
  66.2 0.7 %shard_map.92 = f32[4,64]{1,0:T(4,128)} custom-call(f32[8,2,128]{2,1,0:T(2,128)S(1)} %all-to-all-done.3.arr_ref, f32[8,8,128]{2,1,0:T(8,128)S(1)} %get-tuple-element.30.inv_ref, f32[32,128]{1,0:T(8,128)S(1)} %get-tuple-element.23.const_ref), custom_call_target="tpu_custom_call" | custom-call | tf_op jit(solution)/shard_map/pallas_call | solution.py:434
Async XLA Ops:
  6.4 18.2 %all-to-all-start = ((bf16[32,40,128]{2,1,0:T(8,128)(2,1)}), bf16[32,40,128]{2,1,0:T(8,128)(2,1)S(1)}, u32[]{:S(2)}, u32[]{:S(2)}) async-start(bf16[32,40,128]{2,1,0:T(8,128)(2,1)} %get-tuple-element.17), calls=%async_computation | async-start | bytes 655360 | tf_op jit(solution)/shard_map/all_to_all | solution.py:453
  56.3 9.8 %all-to-all-start.3 = ((f32[8,2,128]{2,1,0:T(2,128)}), f32[8,2,128]{2,1,0:T(2,128)S(1)}, u32[]{:S(2)}, u32[]{:S(2)}) async-start(f32[8,2,128]{2,1,0:T(2,128)} %shard_map.90), calls=%async_computation.3 | async-start | bytes 16384 | tf_op jit(solution)/shard_map/all_to_all | solution.py:453

commit v6 on v5

--- a/solution.py
+++ b/solution.py
@@ -12,13 +12,14 @@
 TAPS = 4
 P_DEV = 16
 RIDGE = 1.0
-UNROLL = 16
+UNROLL = 8
 CXT, LAM_LANE, LAM_SUB, ROT = (slice(8 * i, 8 * (i + 1)) for i in range(4))
 HI = lax.Precision.HIGHEST
 F32 = jnp.float32
 BF16 = jnp.bfloat16
 VMEM = pl.BlockSpec(memory_space=pltpu.VMEM)
 HBM = pl.BlockSpec(memory_space=pl.ANY)
+SMEM = pl.BlockSpec(memory_space=pltpu.SMEM)
 
 
 def constants(pixels):
@@ -70,31 +71,117 @@
     return (2.0 * (base + b_pos) + float(TAPS)) / float(rows_local * ccd_devs) - 1.0
 
 
+def project_kernel(
+    srow_hbm, raw_hbm, res_hbm, w_hbm, pid_hbm, live_hbm, const_hbm,
+    pay_ref, srow_ref, raw_ref, res_ref, w_ref, pid_ref, live_ref, const_ref,
+    hi_sc, lo_sc, code_sc, acc_sc, sems,
+):
+    vis, rows, pix = raw_ref.shape
+    owners, slots = srow_ref.shape
+    blocks = owners * P_DEV // 128
+    group = owners // blocks
+    small = (
+        (srow_hbm, srow_ref), (w_hbm, w_ref), (pid_hbm, pid_ref), (live_hbm, live_ref),
+        (const_hbm, const_ref), (res_hbm, res_ref),
+    )
+    copies = [pltpu.make_async_copy(a, b, sems.at[n]) for n, (a, b) in enumerate(small)]
+    raw_copy = pltpu.make_async_copy(raw_hbm, raw_ref, sems.at[len(small)])
+    for copy in copies + [raw_copy]:
+        copy.start()
+    for copy in copies:
+        copy.wait()
+    span = 128 - TAPS + 1
+    srow = srow_ref[...].astype(F32)
+    high = jnp.floor((srow + 0.5) * (1.0 / span))
+    hi_sc[...] = high
+    lo_sc[...] = srow - span * high
+    place = P_DEV * (iota((owners, slots), 0) % group) + pid_ref[...]
+    code_sc[...] = jnp.where(live_ref[...] > 0, place, -1).astype(F32)
+    c_parts = jnp.concatenate(split(const_ref[CXT], 2), axis=0)
+    kernels = []
+    for v in range(vis):
+        both = dot_t(c_parts, res_ref[v])
+        kernels.append(jnp.concatenate(split(both[:ORDER] + both[ORDER:], 2), axis=0))
+    raw_copy.wait()
+    pieces = []
+    for v in range(vis):
+        both = dot_t(kernels[v], raw_ref[v])
+        pieces.append(both[:ORDER] + both[ORDER:])
+    table = jnp.concatenate(pieces, axis=1)
+    tiles = vis * rows // 128
+    lane = iota((ORDER, 128), 1)
+    windows = []
+    for k in range(-(-(vis * rows - TAPS + 1) // span)):
+        start = span * k
+        first, shift = start // 128, start % 128
+        a = table[:, 128 * first : 128 * (first + 1)]
+        if shift:
+            nxt = min(first + 1, tiles - 1)
+            b = table[:, 128 * nxt : 128 * (nxt + 1)]
+            a = jnp.where(
+                lane < 128 - shift, pltpu.roll(a, 128 - shift, 1), pltpu.roll(b, 128 - shift, 1)
+            )
+        windows.append(a)
+    if len(windows) % 2:
+        windows.append(jnp.zeros((ORDER, 128), F32))
+    left = jnp.concatenate(windows, axis=0).astype(BF16)
+    ids = iota((128, slots), 0).astype(F32).astype(BF16)
+    ones = jnp.ones((ORDER, slots), BF16)
+    unit = jnp.ones((128, slots), BF16)
+
+    def pair_sums(m):
+        taps, his = [], []
+        for h in range(2):
+            j = 2 * m + h
+            low = lo_sc[pl.ds(j, 1), :]
+            one = jnp.zeros((128, slots), BF16)
+            for t in range(TAPS):
+                hit = ids == (low + float(t)).astype(BF16)
+                one = jnp.where(hit, w_ref[t, pl.ds(j, 1), :].astype(BF16), one)
+            taps.append(one)
+            his.append(jnp.broadcast_to(hi_sc[pl.ds(j, 1), :], (ORDER, slots)))
+        vals = dot(left, jnp.concatenate(taps, axis=1))
+        left_sums, members = [], []
+        for h in range(2):
+            got = jnp.zeros((ORDER, slots), F32)
+            for k in range(len(windows)):
+                part = vals[ORDER * k : ORDER * (k + 1), slots * h : slots * (h + 1)]
+                got = jnp.where(his[h] == float(k), part, got)
+            left_sums.append(jnp.concatenate(split(got, 2) + [ones, ones], axis=0))
+            code = code_sc[pl.ds(2 * m + h, 1), :].astype(BF16)
+            members.append(jnp.where(ids == code, unit, jnp.zeros_like(unit)))
+        return dot_t(jnp.concatenate(left_sums, axis=1), jnp.concatenate(members, axis=1))
+
+    def body(q, carry):
+        pairs = group // 2
+        total = pair_sums(q * pairs)
+        for m in range(1, pairs):
+            total = total + pair_sums(q * pairs + m)
+        acc_sc[q] = total
+        return carry
+
+    lax.fori_loop(0, blocks, body, 0)
+    sub = iota((8, 128), 0)
+    tail = jnp.zeros((8, 128), F32)
+    rows_out = []
+    for q in range(blocks):
+        rows_out.append(acc_sc[q, 0:ORDER] + acc_sc[q, ORDER : 2 * ORDER])
+        tail = jnp.where(sub == q, acc_sc[q, 2 * ORDER : 3 * ORDER], tail)
+    block = jnp.concatenate(rows_out + [tail], axis=0).astype(BF16)
+    for i in range(owners):
+        pay_ref[i] = block
+
+
 def gather_kernel(
-    ccd_devs, rows_hbm, raw_hbm, res_hbm, srow_hbm, w_hbm, pid_hbm, live_hbm, cxt_hbm,
-    pay_ref, t_ref, q_ref, res_sc, row_sc, code_sc, wi_sc, h_sc,
-    rows_smem, raw_ref, res_ref, srow_ref, w_ref, pid_ref, live_ref, cxt_ref, sems,
+    ccd_devs, rows_smem, raw_ref, res_ref, srow_ref, w_ref, pid_ref, live_ref, const_ref,
+    t_ref, qb_ref, sy_ref, mw_ref, mtw_ref,
+    res_sc, row_sc, code_sc, wi_sc, q_sc, m_sc,
 ):
     vis, rows, pix = raw_ref.shape
     owners, slots = srow_ref.shape
     wide = slots * TAPS
+    n = vis * ORDER
     ccd = lax.axis_index("ccd")
-    small = [
-        pltpu.make_async_copy(src, dst, sems.at[n])
-        for n, (src, dst) in enumerate(
-            ((srow_hbm, srow_ref), (pid_hbm, pid_ref), (live_hbm, live_ref), (w_hbm, w_ref))
-        )
-    ]
-    index = pltpu.make_async_copy(rows_hbm, rows_smem, sems.at[4])
-    warp = pltpu.make_async_copy(res_hbm, res_ref, sems.at[5])
-    proj_copy = pltpu.make_async_copy(cxt_hbm.at[CXT], cxt_ref, sems.at[6 + vis])
-    raw = [
-        pltpu.make_async_copy(raw_hbm.at[v], raw_ref.at[v], sems.at[6 + v]) for v in range(vis)
-    ]
-    for copy in small + [warp] + raw + [index, proj_copy]:
-        copy.start()
-    for copy in small:
-        copy.wait()
     off = iota((slots, wide), 1) - TAPS * iota((slots, wide), 0)
     rep = jnp.where((off >= 0) & (off < TAPS), 1.0, 0.0).astype(BF16)
     srow = srow_ref[...]
@@ -110,12 +197,11 @@
         part = dot(w_ref[t].astype(BF16), pick)
         wi = part if wi is None else wi + part
     wi_sc[...] = wi
-    q_ref[...] = jnp.zeros_like(q_ref)
+    q_sc[...] = jnp.zeros_like(q_sc)
+    m_sc[...] = jnp.zeros_like(m_sc)
     half = iota((8, pix), 0) < TAPS
     kid = iota((P_DEV, wide), 0).astype(F32)
     kid_s = iota((P_DEV, slots), 0)
-    for copy in [warp] + raw + [index, proj_copy]:
-        copy.wait()
     zero = jnp.zeros((pix, pix), BF16)
     for v in range(0, vis, 2):
         pair = jnp.concatenate([raw_ref[v], raw_ref[v + 1]], axis=1)
@@ -130,7 +216,27 @@
         res_sc[pl.ds(8 + v * rows, rows), :] = both[:, :pix]
         res_sc[pl.ds(8 + (v + 1) * rows, rows), :] = both[:, pix:]
 
-    def body(j, carry):
+    def design(j):
+        srow = srow_ref[pl.ds(j, 1), :]
+        live = live_ref[pl.ds(j, 1), :]
+        pid = pid_ref[pl.ds(j, 1), :]
+        visit = srow // rows
+        y = coord((srow - visit * rows).astype(F32), ccd, rows, ccd_devs)
+        ty = cheb_rows(jnp.broadcast_to(y, (ORDER, slots)), ORDER)
+        member = jnp.where((pid == kid_s) & (live > 0), 1.0, 0.0).astype(BF16)
+        vt = jnp.concatenate(
+            [jnp.where((visit == v) & (live > 0), ty, 0.0) for v in range(vis)], axis=0
+        )
+        parts = jnp.concatenate([p.astype(F32) for p in split(ty, 3)] + [jnp.zeros_like(ty)], axis=0)
+        left = jnp.concatenate([member, parts.astype(BF16)], axis=0)
+        both = None
+        for piece in split(vt, 3):
+            part = dot_t(left, piece)
+            both = part if both is None else both + part
+        m_sc[pl.ds(pl.multiple_of(j * P_DEV, P_DEV), P_DEV), 0:n] = both[:P_DEV]
+        return both[P_DEV:]
+
+    def body(j, acc):
         start = pl.multiple_of(j * slots, slots)
         row_at = [
             rows_smem.at[pl.ds(i, (owners - 1) * slots + 1)][start] for i in range(slots)
@@ -158,70 +264,18 @@
         lhs = jnp.concatenate(lhs, axis=0).astype(BF16)
         sums = dot(lhs, taps)
         t_ref[pl.ds(pl.multiple_of(j * P_DEV, P_DEV), P_DEV), :] = sums[:P_DEV]
-        q_ref[...] += sums[P_DEV:]
-        live = live_ref[pl.ds(j, 1), :]
-        member = jnp.where((pid_ref[pl.ds(j, 1), :] == kid_s) & (live > 0), 1.0, 0.0)
-        h_sc[pl.ds(pl.multiple_of(j * P_DEV, P_DEV), P_DEV), :] = member.astype(BF16)
-        return carry
-
-    lax.fori_loop(0, owners, body, 0, unroll=UNROLL)
-    c_hi, c_lo = split(cxt_ref[...], 2)
-    t_hi, t_lo = split(t_ref[...], 2)
-    proj = dot_t(jnp.concatenate([c_hi, c_lo], axis=0), t_hi)
-    proj = proj[:ORDER] + proj[ORDER:] + dot_t(c_hi, t_lo)
-    counts = dot_t(jnp.ones((8, slots), BF16), h_sc[...])
-    blocks = owners * P_DEV // 128
-    sub = iota((8, 128), 0)
-    rows_out = [proj[:, 128 * q : 128 * (q + 1)] for q in range(blocks)]
-    tail = jnp.zeros((8, 128), F32)
-    for q in range(blocks):
-        tail = jnp.where(sub == q, counts[0:1, 128 * q : 128 * (q + 1)], tail)
-    block = jnp.concatenate(rows_out + [tail], axis=0).astype(BF16)
-    for i in range(owners):
-        pay_ref[i] = block
-
-
-def design_kernel(
-    ccd_devs, rows, srow_ref, pid_ref, live_ref, q_ref, const_ref,
-    qb_ref, sy_ref, mw_ref, mtw_ref, keep_ref, m_sc,
-):
-    owners, slots = srow_ref.shape
-    vis = q_ref.shape[0] // ORDER
-    n = vis * ORDER
-    ccd = lax.axis_index("ccd")
-    kid = iota((P_DEV, slots), 0)
-    m_sc[...] = jnp.zeros_like(m_sc)
-
-    def body(j, acc):
-        srow = srow_ref[pl.ds(j, 1), :]
-        live = live_ref[pl.ds(j, 1), :]
-        pid = pid_ref[pl.ds(j, 1), :]
-        visit = srow // rows
-        y = coord((srow - visit * rows).astype(F32), ccd, rows, ccd_devs)
-        ty = cheb_rows(jnp.broadcast_to(y, (ORDER, slots)), ORDER)
-        member = jnp.where((pid == kid) & (live > 0), 1.0, 0.0).astype(BF16)
-        vt = jnp.concatenate(
-            [jnp.where((visit == v) & (live > 0), ty, 0.0) for v in range(vis)], axis=0
-        )
-        parts = jnp.concatenate([p.astype(F32) for p in split(ty, 3)] + [jnp.zeros_like(ty)], axis=0)
-        left = jnp.concatenate([member, parts.astype(BF16)], axis=0)
-        both = None
-        for piece in split(vt, 3):
-            part = dot_t(left, piece)
-            both = part if both is None else both + part
-        m_sc[pl.ds(pl.multiple_of(j * P_DEV, P_DEV), P_DEV), 0:n] = both[:P_DEV]
-        return acc + both[P_DEV:]
-
-    sy = lax.fori_loop(0, owners, body, jnp.zeros((4 * ORDER, n), F32), unroll=4)
+        q_sc[...] += sums[P_DEV:]
+        return acc + design(j)
+
+    sy = lax.fori_loop(0, owners, body, jnp.zeros((4 * ORDER, n), F32), unroll=UNROLL)
     sy = sy[:ORDER] + sy[ORDER : 2 * ORDER] + sy[2 * ORDER : 3 * ORDER]
     sy_ref[...] = widen(sy)
     m_hi, m_lo = split(m_sc[...], 2)
     mtw_ref[...] = jnp.concatenate(split(m_sc[...].T[:n], 2), axis=0)
-    keep_ref[...] = const_ref[...]
     m_hi, m_lo = m_hi.astype(F32), m_lo.astype(F32)
-    wide = m_hi + pltpu.roll(m_hi, n, 1) + pltpu.roll(m_lo, 2 * n, 1)
-    mw_ref[...] = wide.astype(BF16)
-    full = dot_t(q_ref[...], tile_rows(const_ref[CXT], vis), HI)
+    wide_m = m_hi + pltpu.roll(m_hi, n, 1) + pltpu.roll(m_lo, 2 * n, 1)
+    mw_ref[...] = wide_m.astype(BF16)
+    full = dot_t(q_sc[...], tile_rows(const_ref[CXT], vis), HI)
     qb_ref[...] = widen(blocks_of(full, vis))
 
 
@@ -421,11 +475,12 @@
         out_ref[v : v + 1] = jnp.sum(flat[v * ORDER : (v + 1) * ORDER], axis=0, keepdims=True)
 
 
-def call(kernel, out_shape, scratch=(), n_in=1, hbm=(), plain=()):
+def call(kernel, out_shape, scratch=(), n_in=1, hbm=(), smem=()):
+    spec = {i: HBM for i in hbm} | {i: SMEM for i in smem}
     fn = pl.pallas_call(
         kernel,
         out_shape=out_shape,
-        in_specs=[HBM if i in hbm else VMEM for i in range(n_in)],
+        in_specs=[spec.get(i, VMEM) for i in range(n_in)],
         out_specs=jax.tree.map(lambda _: VMEM, out_shape),
         scratch_shapes=list(scratch),
     )
@@ -433,7 +488,7 @@
     def run(*args):
         return fn(
             *(
-                x if i in plain or i in hbm else pltpu.with_memory_space_constraint(x, pltpu.VMEM)
+                x if i in spec else pltpu.with_memory_space_constraint(x, pltpu.VMEM)
                 for i, x in enumerate(args)
             )
         )
@@ -472,46 +527,50 @@
     weights = tap_weight[:, 0, 0]
     pay_rows = ORDER * blocks + P_DEV
 
-    pay1, tsum, qsum = call(
+    ints = shape((owners, slots), jnp.int32)
+    pay1, srow_v, raw_v, res_v, w_v, pid_v, live_v, const = call(
+        project_kernel,
+        (
+            shape((owners, ORDER * blocks + 8, 128), BF16),
+            ints,
+            shape(raw_rows.shape, BF16),
+            shape(resample.shape, BF16),
+            shape((TAPS, owners, slots)),
+            ints,
+            ints,
+            shape(const.shape),
+        ),
+        scratch=(
+            pltpu.VMEM((owners, slots), F32),
+            pltpu.VMEM((owners, slots), F32),
+            pltpu.VMEM((owners, slots), F32),
+            pltpu.VMEM((blocks, 4 * ORDER, 128), F32),
+            pltpu.SemaphoreType.DMA((7,)),
+        ),
+        n_in=7,
+        hbm=range(7),
+    )(srow, raw_rows, resample, weights, pid, live, const)
+    arr1 = exchange(pay1, "visit")
+    tsum, qb, sy, mw, mtw = call(
         functools.partial(gather_kernel, ccd_devs),
         (
-            shape((owners, ORDER * blocks + 8, 128), BF16),
             shape((patches, pix)),
-            shape((nvb, pix)),
+            shape((ORDER, 128)),
+            shape((ORDER, 128)),
+            shape((patches, 128), BF16),
+            shape((2 * nvb, patches), BF16),
         ),
         scratch=(
             pltpu.VMEM((vis * rows + 16, pix), F32),
             pltpu.VMEM((owners, slots * TAPS), F32),
             pltpu.VMEM((owners, slots * TAPS), F32),
             pltpu.VMEM((owners, slots * TAPS), F32),
-            pltpu.VMEM((patches, slots), BF16),
-            pltpu.SMEM((owners * slots,), jnp.int32),
-            pltpu.VMEM(raw_rows.shape, BF16),
-            pltpu.VMEM(resample.shape, BF16),
-            pltpu.VMEM((owners, slots), jnp.int32),
-            pltpu.VMEM((TAPS, owners, slots), F32),
-            pltpu.VMEM((owners, slots), jnp.int32),
-            pltpu.VMEM((owners, slots), jnp.int32),
-            pltpu.VMEM((ORDER, pix), F32),
-            pltpu.SemaphoreType.DMA((7 + vis,)),
+            pltpu.VMEM((nvb, pix), F32),
+            pltpu.VMEM((patches, 128), F32),
         ),
         n_in=8,
-        hbm=range(8),
-    )(srow.reshape(-1), raw_rows, resample, srow, weights, pid, live, const)
-    arr1 = exchange(pay1, "visit")
-    qb, sy, mw, mtw, const = call(
-        functools.partial(design_kernel, ccd_devs, rows),
-        (
-            shape((ORDER, 128)),
-            shape((ORDER, 128)),
-            shape((patches, 128), BF16),
-            shape((2 * nvb, patches), BF16),
-            shape(const.shape),
-        ),
-        scratch=(pltpu.VMEM((patches, 128), F32),),
-        n_in=5,
-        plain=(0, 1, 2, 4),
-    )(srow, pid, live, qsum, const)
+        smem=(0,),
+    )(srow.reshape(-1), raw_v, res_v, srow_v, w_v, pid_v, live_v, const)
     back, den, pay2 = call(
         first_kernel,
         (

time: 67.5 us -> 66.4 us (0.984)
  waiting for transfers between devices: 12.2 us -> 10.3 us
  Pallas kernels: 12.4 us -> 13.2 us
    all_to_all x2, waiting for transfers between devices: 12.2 us -> 10.3 us  [exchange(): return lax.all_to_all(x, axis, split_axis=0, concat_axis=0, tiled=True)]
    pallas_call x7, Pallas kernels: 12.4 us -> 13.2 us  [run(): fn(*(x if i in spec else pltpu.with_memory_space_constraint(x, pltpu.VMEM...]
  transfers between devices with their start and end apart: 2 -> 2, of which waited for: 2 -> 2; matrix products, arithmetic and copies ran while one was open for 0% -> 0% of each run, Pallas kernels for 6% -> 9%
where the time goes in v6:
time: 66.4 us; the launch traced here: 65.8 us
  blocking collectives  29.7 us (45%)
  Pallas kernels  13.2 us (20%)
  starting transfers between devices  11.9 us (18%)
  waiting for transfers between devices  10.3 us (16%)
  between operations  0.67 us (1%)
    all_to_all x2, blocking collectives, exchange(): return lax.all_to_all(x, axis, split_axis=0, concat_axis=0, tiled=True)  29.7 us
    pallas_call x7, Pallas kernels, run(): fn(*(x if i in spec else pltpu.with_memory_space_constraint(x, pltpu.VMEM...  13.2 us
    all_to_all x2, starting transfers between devices, exchange(): return lax.all_to_all(x, axis, split_axis=0, concat_axis=0, tiled=True)  11.9 us
    all_to_all x2, waiting for transfers between devices, exchange(): return lax.all_to_all(x, axis, split_axis=0, concat_axis=0, tiled=True)  10.3 us
  transfers between devices with their start and end apart: 2, of which 2 were waited for; matrix products, arithmetic and copies ran while one was open for 0% of the time, Pallas kernels for 9%

profile of v6, /device:TPU:1, one launch (start us, length us, event | category | flops | bytes accessed | tf_op | source)
XLA Modules:
  0.0 65.8 jit_solution(5708938061425512062)
XLA Ops:
  0.6 4.7 %shard_map.86 = (bf16[32,40,128]{2,1,0:T(8,128)(2,1)}, s32[32,128]{1,0:T(8,128)S(1)}, bf16[4,1024,128]{2,1,0:T(8,128)(2,1)S(1)}, bf16[4,128,128]{2,1,0:T(8,128)(...) custom-call(s32[32,128]{1,0:T(8,128)} %bitcast.6, ...), custom_call_target="tpu_custom_call" | custom-call | tf_op jit(solution)/shard_map/pallas_call | solution.py:489
  5.3 8.6 %all-to-all-start = ((bf16[32,40,128]{2,1,0:T(8,128)(2,1)}), bf16[32,40,128]{2,1,0:T(8,128)(2,1)S(1)}, u32[]{:S(2)}, u32[]{:S(2)}) async-start(bf16[32,40,128]{2,1,0:T(8,128)(2,1)} %get-tuple-element.22), calls=%async_computation | async-start | bytes 655360 | tf_op jit(solution)/shard_map/all_to_all | solution.py:508
  13.9 4.9 %shard_map.87 = (f32[512,128]{1,0:T(8,128)S(1)}, f32[8,128]{1,0:T(8,128)S(1)}, f32[8,128]{1,0:T(8,128)S(1)}, bf16[512,128]{1,0:T(8,128)(2,1)S(1)}, bf16[64,512]{1,0:T(8,128)(2,1)S(1)}) custom-call(s32[4096]{0:T(1024)} %bitcast.7, bf16[4,1024,128]{2,1,0:T(8,128)(2,1)S(1)} %get-tuple-element.23.raw_ref, bf16[4,128,128]{2,1,0:T(8,128)(2,1)S(1)} %get-tuple-element.24.res_ref, ...), custom_call_target="tpu_custom_call" | custom-call | tf_op jit(solution)/shard_map/pallas_call | solution.py:489
  18.8 4.7 %all-to-all-done.arr_ref = bf16[32,40,128]{2,1,0:T(8,128)(2,1)S(1)} async-done(((bf16[32,40,128]{2,1,0:T(8,128)(2,1)}), bf16[32,40,128]{2,1,0:T(8,128)(2,1)S(1)}, u32[]{:S(2)}, u32[]{:S(2)}) %all-to-all-start) | async-done | bytes 327712 | tf_op jit(solution)/shard_map/all_to_all | solution.py:508
  23.5 0.3 shard_map.88
  23.8 14.6 %all_to_all.20.arr_ref = f32[8,4,128]{2,1,0:T(4,128)S(1)} all-to-all(f32[8,4,128]{2,1,0:T(4,128)S(1)} %get-tuple-element.33), channel_id=1, replica_groups=mesh['visit'=32,'ccd'=8] {'ccd'}, dimensions={0} | all-to-all | bytes 32768 | tf_op jit(solution)/shard_map/all_to_all | solution.py:508
  38.4 0.8 %shard_map.89 = (f32[8,128]{1,0:T(8,128)S(1)}, bf16[32,48,128]{2,1,0:T(8,128)(2,1)S(1)}) custom-call(f32[8,4,128]{2,1,0:T(4,128)S(1)} %all_to_all.20.arr_ref, f32[32,128]{1,0:T(8,128)S(1)} %get-tuple-element.29.const_ref, bf16[64,512]{1,0:T(8,128)(2,1)S(1)} %get-tuple-element.30.mtw_ref, bf16[512,128]{1,0:T(8,128)(2,1)S(1)} %get-tuple-element.34.mw_ref, ...), custom_call_target="tpu_custom_call" | custom-call | tf_op jit(solution)/shard_map/pallas_call | solution.py:489
  39.2 15.1 %all_to_all.21.arr_ref = bf16[32,48,128]{2,1,0:T(8,128)(2,1)S(1)} all-to-all(bf16[32,48,128]{2,1,0:T(8,128)(2,1)S(1)} %get-tuple-element.36), channel_id=1, replica_groups=mesh['visit'=32,'ccd'=8] {'visit'}, dimensions={0} | all-to-all | bytes 786432 | tf_op jit(solution)/shard_map/all_to_all | solution.py:508
  54.3 0.9 %shard_map.90 = f32[8,2,128]{2,1,0:T(2,128)} custom-call(bf16[32,48,128]{2,1,0:T(8,128)(2,1)S(1)} %all_to_all.21.arr_ref, f32[8,512]{1,0:T(8,128)S(1)} %get-tuple-element.37.b_ref, f32[8,512]{1,0:T(8,128)S(1)} %get-tuple-element.38.den_ref, bf16[64,512]{1,0:T(8,128)(2,1)S(1)} %get-tuple-element.30.mtw_ref, f32[8,128]{1,0:T(8,128)S(1)} %get-tuple-element.31.qb_ref, ...), custom_call_target="tpu_custom_call" | custom-call | tf_op jit(solution)/shard_map/pallas_call | solution.py:489
  55.2 3.3 %all-to-all-start.3 = ((f32[8,2,128]{2,1,0:T(2,128)}), f32[8,2,128]{2,1,0:T(2,128)S(1)}, u32[]{:S(2)}, u32[]{:S(2)}) async-start(f32[8,2,128]{2,1,0:T(2,128)} %shard_map.90), calls=%async_computation.3 | async-start | bytes 16384 | tf_op jit(solution)/shard_map/all_to_all | solution.py:508
  58.6 0.9 %shard_map.91 = (f32[16,128]{1,0:T(8,128)}, f32[8,8,128]{2,1,0:T(8,128)S(1)}) custom-call(bf16[32,48,128]{2,1,0:T(8,128)(2,1)S(1)} %all_to_all.21.arr_ref, f32[8,512]{1,0:T(8,128)S(1)} %get-tuple-element.38.den_ref, f32[8,128]{1,0:T(8,128)S(1)} %get-tuple-element.39.sy_ref, f32[32,128]{1,0:T(8,128)S(1)} %get-tuple-element.29.const_ref), custom_call_target="tpu_custom_call" | custom-call | tf_op jit(solution)/shard_map/pallas_call | solution.py:489
  59.5 5.6 %all-to-all-done.3.arr_ref = f32[8,2,128]{2,1,0:T(2,128)S(1)} async-done(((f32[8,2,128]{2,1,0:T(2,128)}), f32[8,2,128]{2,1,0:T(2,128)S(1)}, u32[]{:S(2)}, u32[]{:S(2)}) %all-to-all-start.3) | async-done | bytes 8224 | tf_op jit(solution)/shard_map/all_to_all | solution.py:508
  65.1 0.7 %shard_map.92 = f32[4,64]{1,0:T(4,128)} custom-call(f32[8,2,128]{2,1,0:T(2,128)S(1)} %all-to-all-done.3.arr_ref, f32[8,8,128]{2,1,0:T(8,128)S(1)} %get-tuple-element.40.inv_ref, f32[32,128]{1,0:T(8,128)S(1)} %get-tuple-element.29.const_ref), custom_call_target="tpu_custom_call" | custom-call | tf_op jit(solution)/shard_map/pallas_call | solution.py:489
Async XLA Ops:
  5.3 18.2 %all-to-all-start = ((bf16[32,40,128]{2,1,0:T(8,128)(2,1)}), bf16[32,40,128]{2,1,0:T(8,128)(2,1)S(1)}, u32[]{:S(2)}, u32[]{:S(2)}) async-start(bf16[32,40,128]{2,1,0:T(8,128)(2,1)} %get-tuple-element.22), calls=%async_computation | async-start | bytes 655360 | tf_op jit(solution)/shard_map/all_to_all | solution.py:508
  55.2 9.8 %all-to-all-start.3 = ((f32[8,2,128]{2,1,0:T(2,128)}), f32[8,2,128]{2,1,0:T(2,128)S(1)}, u32[]{:S(2)}, u32[]{:S(2)}) async-start(f32[8,2,128]{2,1,0:T(2,128)} %shard_map.90), calls=%async_computation.3 | async-start | bytes 16384 | tf_op jit(solution)/shard_map/all_to_all | solution.py:508

commit v7 on v6

--- a/solution.py
+++ b/solution.py
@@ -90,7 +90,8 @@
         copy.start()
     for copy in copies:
         copy.wait()
-    span = 128 - TAPS + 1
+    wide = 256
+    span = wide - TAPS + 1
     srow = srow_ref[...].astype(F32)
     high = jnp.floor((srow + 0.5) * (1.0 / span))
     hi_sc[...] = high
@@ -110,22 +111,27 @@
     table = jnp.concatenate(pieces, axis=1)
     tiles = vis * rows // 128
     lane = iota((ORDER, 128), 1)
+
+    def window(start):
+        first, shift = start // 128, start % 128
+        a, b = (
+            table[:, 128 * t : 128 * (t + 1)]
+            for t in (min(first, tiles - 1), min(first + 1, tiles - 1))
+        )
+        if not shift:
+            return a
+        a, b = pltpu.roll(a, 128 - shift, 1), pltpu.roll(b, 128 - shift, 1)
+        return jnp.where(lane < 128 - shift, a, b)
+
     windows = []
     for k in range(-(-(vis * rows - TAPS + 1) // span)):
-        start = span * k
-        first, shift = start // 128, start % 128
-        a = table[:, 128 * first : 128 * (first + 1)]
-        if shift:
-            nxt = min(first + 1, tiles - 1)
-            b = table[:, 128 * nxt : 128 * (nxt + 1)]
-            a = jnp.where(
-                lane < 128 - shift, pltpu.roll(a, 128 - shift, 1), pltpu.roll(b, 128 - shift, 1)
-            )
-        windows.append(a)
+        parts = [window(span * k + c) for c in range(0, wide, 128)]
+        windows.append(jnp.concatenate(parts, axis=1))
     if len(windows) % 2:
-        windows.append(jnp.zeros((ORDER, 128), F32))
+        windows.append(jnp.zeros((ORDER, wide), F32))
     left = jnp.concatenate(windows, axis=0).astype(BF16)
-    ids = iota((128, slots), 0).astype(F32).astype(BF16)
+    rid = iota((wide, slots), 0).astype(F32).astype(BF16)
+    ids = rid[:128]
     ones = jnp.ones((ORDER, slots), BF16)
     unit = jnp.ones((128, slots), BF16)
 
@@ -134,9 +140,9 @@
         for h in range(2):
             j = 2 * m + h
             low = lo_sc[pl.ds(j, 1), :]
-            one = jnp.zeros((128, slots), BF16)
+            one = jnp.zeros((wide, slots), BF16)
             for t in range(TAPS):
-                hit = ids == (low + float(t)).astype(BF16)
+                hit = rid == (low + float(t)).astype(BF16)
                 one = jnp.where(hit, w_ref[t, pl.ds(j, 1), :].astype(BF16), one)
             taps.append(one)
             his.append(jnp.broadcast_to(hi_sc[pl.ds(j, 1), :], (ORDER, slots)))
@@ -160,7 +166,7 @@
         acc_sc[q] = total
         return carry
 
-    lax.fori_loop(0, blocks, body, 0)
+    lax.fori_loop(0, blocks, body, 0, unroll=2)
     sub = iota((8, 128), 0)
     tail = jnp.zeros((8, 128), F32)
     rows_out = []
@@ -359,14 +365,11 @@
 
 
 def systems(sy, lam, vis):
-    n = vis * ORDER
-    rows, lanes = iota((n, ORDER * 128), 0), iota((n, ORDER * 128), 1)
-    pos = lanes % 128
-    pick = (rows // ORDER == pos // ORDER) & (rows % ORDER == lanes // 128)
-    spread = dot(sy[:, :n], jnp.where(pick, 1.0, 0.0), HI)
     sub = iota((ORDER, 128), 0)
+    base = iota((ORDER, 128), 1) // ORDER * ORDER
     return [
-        spread[:, 128 * b : 128 * (b + 1)] * lam + jnp.where(sub == b, RIDGE, 0.0)
+        jnp.take_along_axis(sy, base + b, axis=1, mode="promise_in_bounds") * lam
+        + jnp.where(sub == b, RIDGE, 0.0)
         for b in range(ORDER)
     ]
 
@@ -390,11 +393,10 @@
     return jnp.where(iota((ORDER, 128), 1) < vis * ORDER, out, 0.0)
 
 
-def block_diag_t(z, vis):
+def block_diag(z, vis):
     n = vis * ORDER
-    tiled = tile_rows(z, vis)
     keep = iota((n, 128), 0) // ORDER == iota((n, 128), 1) // ORDER
-    return jnp.where(keep, tiled, 0.0).T[:n]
+    return jnp.where(keep, tile_rows(z, vis), 0.0)
 
 
 def model_kernel(arr_ref, const_ref, mtw_ref, mw_ref, t_ref, sy_ref, pay_ref):
@@ -408,7 +410,8 @@
     sy_ref[...] = sy
     mom = unpack([total[i : i + 1] for i in range(rows)])
     z = solve(mom, sy, const_ref[LAM_LANE], vis)
-    diag = block_diag_t(z, vis)
+    square = block_diag(z, vis)
+    diag = square.T[:n]
     weights = diag[:ORDER]
     for v in range(1, vis):
         weights = weights + diag[v * ORDER : (v + 1) * ORDER]
@@ -416,9 +419,10 @@
     model = (
         dot(w_hi, mtw_ref[0:n]) + dot(w_lo, mtw_ref[0:n]) + dot(w_hi, mtw_ref[n : 2 * n])
     )
-    surface = lax.dot_general(
-        weights, const_ref[CXT], (((0,), (0,)), ((), ())), precision=HI, preferred_element_type=F32
-    )
+    z_hi, z_lo = split(square, 2)
+    c_hi, c_lo = split(tile_rows(const_ref[CXT], 128 // ORDER), 2)
+    surface = dot(jnp.concatenate([z_hi, z_lo], axis=0), c_hi)
+    surface = surface[:n] + surface[n:] + dot(z_hi, c_lo)
     s_hi, s_lo = split(surface, 2)
     surface = jnp.concatenate([s_hi, s_lo, s_hi, jnp.zeros((128 - 3 * n, 128), BF16)], axis=0)
     corrected = t_ref[...] - dot(mw_ref[...], surface)

time: 66.4 us -> 65.6 us (0.988)
  Pallas kernels: 13.2 us -> 12.5 us
    pallas_call x7, Pallas kernels: 13.2 us -> 12.5 us  [run(): fn(*(x if i in spec else pltpu.with_memory_space_constraint(x, pltpu.VMEM...]
where the time goes in v7:
time: 65.6 us; the launch traced here: 65.1 us
  blocking collectives  29.7 us (45%)
  Pallas kernels  12.5 us (19%)
  starting transfers between devices  11.9 us (18%)
  waiting for transfers between devices  10.4 us (16%)
  between operations  0.67 us (1%)
    all_to_all x2, blocking collectives, exchange(): return lax.all_to_all(x, axis, split_axis=0, concat_axis=0, tiled=True)  29.7 us
    pallas_call x7, Pallas kernels, run(): fn(*(x if i in spec else pltpu.with_memory_space_constraint(x, pltpu.VMEM...  12.5 us
    all_to_all x2, starting transfers between devices, exchange(): return lax.all_to_all(x, axis, split_axis=0, concat_axis=0, tiled=True)  11.9 us
    all_to_all x2, waiting for transfers between devices, exchange(): return lax.all_to_all(x, axis, split_axis=0, concat_axis=0, tiled=True)  10.4 us
  transfers between devices with their start and end apart: 2, of which 2 were waited for; matrix products, arithmetic and copies ran while one was open for 0% of the time, Pallas kernels for 9%

profile of v7, /device:TPU:1, one launch (start us, length us, event | category | flops | bytes accessed | tf_op | source)
XLA Modules:
  0.0 65.1 jit_solution(6627122120823439385)
XLA Ops:
  0.6 4.1 %shard_map.86 = (bf16[32,40,128]{2,1,0:T(8,128)(2,1)}, s32[32,128]{1,0:T(8,128)S(1)}, bf16[4,1024,128]{2,1,0:T(8,128)(2,1)S(1)}, bf16[4,128,128]{2,1,0:T(8,128)(...) custom-call(s32[32,128]{1,0:T(8,128)} %bitcast.6, ...), custom_call_target="tpu_custom_call" | custom-call | tf_op jit(solution)/shard_map/pallas_call | solution.py:493
  4.7 8.6 %all-to-all-start = ((bf16[32,40,128]{2,1,0:T(8,128)(2,1)}), bf16[32,40,128]{2,1,0:T(8,128)(2,1)S(1)}, u32[]{:S(2)}, u32[]{:S(2)}) async-start(bf16[32,40,128]{2,1,0:T(8,128)(2,1)} %get-tuple-element.22), calls=%async_computation | async-start | bytes 655360 | tf_op jit(solution)/shard_map/all_to_all | solution.py:512
  13.3 4.9 %shard_map.87 = (f32[512,128]{1,0:T(8,128)S(1)}, f32[8,128]{1,0:T(8,128)S(1)}, f32[8,128]{1,0:T(8,128)S(1)}, bf16[512,128]{1,0:T(8,128)(2,1)S(1)}, bf16[64,512]{1,0:T(8,128)(2,1)S(1)}) custom-call(s32[4096]{0:T(1024)} %bitcast.7, bf16[4,1024,128]{2,1,0:T(8,128)(2,1)S(1)} %get-tuple-element.23.raw_ref, bf16[4,128,128]{2,1,0:T(8,128)(2,1)S(1)} %get-tuple-element.24.res_ref, ...), custom_call_target="tpu_custom_call" | custom-call | tf_op jit(solution)/shard_map/pallas_call | solution.py:493
  18.2 4.7 %all-to-all-done.arr_ref = bf16[32,40,128]{2,1,0:T(8,128)(2,1)S(1)} async-done(((bf16[32,40,128]{2,1,0:T(8,128)(2,1)}), bf16[32,40,128]{2,1,0:T(8,128)(2,1)S(1)}, u32[]{:S(2)}, u32[]{:S(2)}) %all-to-all-start) | async-done | bytes 327712 | tf_op jit(solution)/shard_map/all_to_all | solution.py:512
  22.9 0.3 shard_map.88
  23.2 14.6 %all_to_all.20.arr_ref = f32[8,4,128]{2,1,0:T(4,128)S(1)} all-to-all(f32[8,4,128]{2,1,0:T(4,128)S(1)} %get-tuple-element.33), channel_id=1, replica_groups=mesh['visit'=32,'ccd'=8] {'ccd'}, dimensions={0} | all-to-all | bytes 32768 | tf_op jit(solution)/shard_map/all_to_all | solution.py:512
  37.8 0.7 %shard_map.89 = (f32[8,128]{1,0:T(8,128)S(1)}, bf16[32,48,128]{2,1,0:T(8,128)(2,1)S(1)}) custom-call(f32[8,4,128]{2,1,0:T(4,128)S(1)} %all_to_all.20.arr_ref, f32[32,128]{1,0:T(8,128)S(1)} %get-tuple-element.29.const_ref, bf16[64,512]{1,0:T(8,128)(2,1)S(1)} %get-tuple-element.30.mtw_ref, bf16[512,128]{1,0:T(8,128)(2,1)S(1)} %get-tuple-element.34.mw_ref, ...), custom_call_target="tpu_custom_call" | custom-call | tf_op jit(solution)/shard_map/pallas_call | solution.py:493
  38.5 15.1 %all_to_all.21.arr_ref = bf16[32,48,128]{2,1,0:T(8,128)(2,1)S(1)} all-to-all(bf16[32,48,128]{2,1,0:T(8,128)(2,1)S(1)} %get-tuple-element.36), channel_id=1, replica_groups=mesh['visit'=32,'ccd'=8] {'visit'}, dimensions={0} | all-to-all | bytes 786432 | tf_op jit(solution)/shard_map/all_to_all | solution.py:512
  53.6 0.9 %shard_map.90 = f32[8,2,128]{2,1,0:T(2,128)} custom-call(bf16[32,48,128]{2,1,0:T(8,128)(2,1)S(1)} %all_to_all.21.arr_ref, f32[8,512]{1,0:T(8,128)S(1)} %get-tuple-element.37.b_ref, f32[8,512]{1,0:T(8,128)S(1)} %get-tuple-element.38.den_ref, bf16[64,512]{1,0:T(8,128)(2,1)S(1)} %get-tuple-element.30.mtw_ref, f32[8,128]{1,0:T(8,128)S(1)} %get-tuple-element.31.qb_ref, ...), custom_call_target="tpu_custom_call" | custom-call | tf_op jit(solution)/shard_map/pallas_call | solution.py:493
  54.5 3.3 %all-to-all-start.3 = ((f32[8,2,128]{2,1,0:T(2,128)}), f32[8,2,128]{2,1,0:T(2,128)S(1)}, u32[]{:S(2)}, u32[]{:S(2)}) async-start(f32[8,2,128]{2,1,0:T(2,128)} %shard_map.90), calls=%async_computation.3 | async-start | bytes 16384 | tf_op jit(solution)/shard_map/all_to_all | solution.py:512
  57.9 0.9 %shard_map.91 = (f32[16,128]{1,0:T(8,128)}, f32[8,8,128]{2,1,0:T(8,128)S(1)}) custom-call(bf16[32,48,128]{2,1,0:T(8,128)(2,1)S(1)} %all_to_all.21.arr_ref, f32[8,512]{1,0:T(8,128)S(1)} %get-tuple-element.38.den_ref, f32[8,128]{1,0:T(8,128)S(1)} %get-tuple-element.39.sy_ref, f32[32,128]{1,0:T(8,128)S(1)} %get-tuple-element.29.const_ref), custom_call_target="tpu_custom_call" | custom-call | tf_op jit(solution)/shard_map/pallas_call | solution.py:493
  58.7 5.7 %all-to-all-done.3.arr_ref = f32[8,2,128]{2,1,0:T(2,128)S(1)} async-done(((f32[8,2,128]{2,1,0:T(2,128)}), f32[8,2,128]{2,1,0:T(2,128)S(1)}, u32[]{:S(2)}, u32[]{:S(2)}) %all-to-all-start.3) | async-done | bytes 8224 | tf_op jit(solution)/shard_map/all_to_all | solution.py:512
  64.4 0.7 %shard_map.92 = f32[4,64]{1,0:T(4,128)} custom-call(f32[8,2,128]{2,1,0:T(2,128)S(1)} %all-to-all-done.3.arr_ref, f32[8,8,128]{2,1,0:T(8,128)S(1)} %get-tuple-element.40.inv_ref, f32[32,128]{1,0:T(8,128)S(1)} %get-tuple-element.29.const_ref), custom_call_target="tpu_custom_call" | custom-call | tf_op jit(solution)/shard_map/pallas_call | solution.py:493
Async XLA Ops:
  4.7 18.2 %all-to-all-start = ((bf16[32,40,128]{2,1,0:T(8,128)(2,1)}), bf16[32,40,128]{2,1,0:T(8,128)(2,1)S(1)}, u32[]{:S(2)}, u32[]{:S(2)}) async-start(bf16[32,40,128]{2,1,0:T(8,128)(2,1)} %get-tuple-element.22), calls=%async_computation | async-start | bytes 655360 | tf_op jit(solution)/shard_map/all_to_all | solution.py:512
  54.5 9.8 %all-to-all-start.3 = ((f32[8,2,128]{2,1,0:T(2,128)}), f32[8,2,128]{2,1,0:T(2,128)S(1)}, u32[]{:S(2)}, u32[]{:S(2)}) async-start(f32[8,2,128]{2,1,0:T(2,128)} %shard_map.90), calls=%async_computation.3 | async-start | bytes 16384 | tf_op jit(solution)/shard_map/all_to_all | solution.py:512

commit v8 on v7

--- a/solution.py
+++ b/solution.py
@@ -13,6 +13,7 @@
 P_DEV = 16
 RIDGE = 1.0
 UNROLL = 8
+UNROLL_W = 2
 CXT, LAM_LANE, LAM_SUB, ROT = (slice(8 * i, 8 * (i + 1)) for i in range(4))
 HI = lax.Precision.HIGHEST
 F32 = jnp.float32
@@ -74,7 +75,7 @@
 def project_kernel(
     srow_hbm, raw_hbm, res_hbm, w_hbm, pid_hbm, live_hbm, const_hbm,
     pay_ref, srow_ref, raw_ref, res_ref, w_ref, pid_ref, live_ref, const_ref,
-    hi_sc, lo_sc, code_sc, acc_sc, sems,
+    hi_sc, lo_sc, code_sc, hot_sc, member_sc, acc_sc, sems,
 ):
     vis, rows, pix = raw_ref.shape
     owners, slots = srow_ref.shape
@@ -85,8 +86,11 @@
         (const_hbm, const_ref), (res_hbm, res_ref),
     )
     copies = [pltpu.make_async_copy(a, b, sems.at[n]) for n, (a, b) in enumerate(small)]
-    raw_copy = pltpu.make_async_copy(raw_hbm, raw_ref, sems.at[len(small)])
-    for copy in copies + [raw_copy]:
+    raw_copies = [
+        pltpu.make_async_copy(raw_hbm.at[v], raw_ref.at[v], sems.at[len(small) + v])
+        for v in range(vis)
+    ]
+    for copy in copies + raw_copies:
         copy.start()
     for copy in copies:
         copy.wait()
@@ -103,7 +107,26 @@
     for v in range(vis):
         both = dot_t(c_parts, res_ref[v])
         kernels.append(jnp.concatenate(split(both[:ORDER] + both[ORDER:], 2), axis=0))
-    raw_copy.wait()
+    rid = iota((wide, slots), 0).astype(F32).astype(BF16)
+    ids = rid[:128]
+    unit = jnp.ones((128, slots), BF16)
+    def operands(j):
+        low = lo_sc[pl.ds(j, 1), :]
+        one = jnp.zeros((wide, slots), BF16)
+        for t in range(TAPS):
+            hit = rid == (low + float(t)).astype(BF16)
+            one = jnp.where(hit, w_ref[t, pl.ds(j, 1), :].astype(BF16), one)
+        code = code_sc[pl.ds(j, 1), :].astype(BF16)
+        return one, jnp.where(ids == code, unit, jnp.zeros_like(unit))
+
+    def build(j, carry):
+        hot_sc[j], member_sc[j] = operands(j)
+        return carry
+
+    early = blocks // 2
+    lax.fori_loop(0, early * group, build, 0, unroll=UNROLL_W)
+    for copy in raw_copies:
+        copy.wait()
     pieces = []
     for v in range(vis):
         both = dot_t(kernels[v], raw_ref[v])
@@ -130,43 +153,33 @@
     if len(windows) % 2:
         windows.append(jnp.zeros((ORDER, wide), F32))
     left = jnp.concatenate(windows, axis=0).astype(BF16)
-    rid = iota((wide, slots), 0).astype(F32).astype(BF16)
-    ids = rid[:128]
     ones = jnp.ones((ORDER, slots), BF16)
-    unit = jnp.ones((128, slots), BF16)
-
-    def pair_sums(m):
-        taps, his = [], []
-        for h in range(2):
-            j = 2 * m + h
-            low = lo_sc[pl.ds(j, 1), :]
-            one = jnp.zeros((wide, slots), BF16)
-            for t in range(TAPS):
-                hit = rid == (low + float(t)).astype(BF16)
-                one = jnp.where(hit, w_ref[t, pl.ds(j, 1), :].astype(BF16), one)
-            taps.append(one)
-            his.append(jnp.broadcast_to(hi_sc[pl.ds(j, 1), :], (ORDER, slots)))
-        vals = dot(left, jnp.concatenate(taps, axis=1))
-        left_sums, members = [], []
-        for h in range(2):
+
+    def pair_sums(m, made):
+        both = [2 * m, 2 * m + 1]
+        pairs = [(hot_sc[j], member_sc[j]) if made else operands(j) for j in both]
+        vals = dot(left, jnp.concatenate([p[0] for p in pairs], axis=1))
+        left_sums = []
+        for h, j in enumerate(both):
+            high = jnp.broadcast_to(hi_sc[pl.ds(j, 1), :], (ORDER, slots))
             got = jnp.zeros((ORDER, slots), F32)
             for k in range(len(windows)):
                 part = vals[ORDER * k : ORDER * (k + 1), slots * h : slots * (h + 1)]
-                got = jnp.where(his[h] == float(k), part, got)
+                got = jnp.where(high == float(k), part, got)
             left_sums.append(jnp.concatenate(split(got, 2) + [ones, ones], axis=0))
-            code = code_sc[pl.ds(2 * m + h, 1), :].astype(BF16)
-            members.append(jnp.where(ids == code, unit, jnp.zeros_like(unit)))
-        return dot_t(jnp.concatenate(left_sums, axis=1), jnp.concatenate(members, axis=1))
-
-    def body(q, carry):
+        members = jnp.concatenate([p[1] for p in pairs], axis=1)
+        return dot_t(jnp.concatenate(left_sums, axis=1), members)
+
+    def body(made, q, carry):
         pairs = group // 2
-        total = pair_sums(q * pairs)
+        total = pair_sums(q * pairs, made)
         for m in range(1, pairs):
-            total = total + pair_sums(q * pairs + m)
+            total = total + pair_sums(q * pairs + m, made)
         acc_sc[q] = total
         return carry
 
-    lax.fori_loop(0, blocks, body, 0, unroll=2)
+    lax.fori_loop(0, early, functools.partial(body, True), 0, unroll=True)
+    lax.fori_loop(early, blocks, functools.partial(body, False), 0, unroll=True)
     sub = iota((8, 128), 0)
     tail = jnp.zeros((8, 128), F32)
     rows_out = []
@@ -548,8 +561,10 @@
             pltpu.VMEM((owners, slots), F32),
             pltpu.VMEM((owners, slots), F32),
             pltpu.VMEM((owners, slots), F32),
+            pltpu.VMEM((owners // 2, 256, slots), BF16),
+            pltpu.VMEM((owners // 2, 128, slots), BF16),
             pltpu.VMEM((blocks, 4 * ORDER, 128), F32),
-            pltpu.SemaphoreType.DMA((7,)),
+            pltpu.SemaphoreType.DMA((6 + vis,)),
         ),
         n_in=7,
         hbm=range(7),

time: 65.6 us -> 65.6 us (level)
  no operation moved by 1% of the time
where the time goes in v8:
time: 65.6 us; the launch traced here: 65.1 us
  blocking collectives  29.7 us (45%)
  Pallas kernels  12.4 us (19%)
  starting transfers between devices  11.9 us (18%)
  waiting for transfers between devices  10.4 us (16%)
  between operations  0.67 us (1%)
    all_to_all x2, blocking collectives, exchange(): return lax.all_to_all(x, axis, split_axis=0, concat_axis=0, tiled=True)  29.7 us
    pallas_call x7, Pallas kernels, run(): fn(*(x if i in spec else pltpu.with_memory_space_constraint(x, pltpu.VMEM...  12.4 us
    all_to_all x2, starting transfers between devices, exchange(): return lax.all_to_all(x, axis, split_axis=0, concat_axis=0, tiled=True)  11.9 us
    all_to_all x2, waiting for transfers between devices, exchange(): return lax.all_to_all(x, axis, split_axis=0, concat_axis=0, tiled=True)  10.4 us
  transfers between devices with their start and end apart: 2, of which 2 were waited for; matrix products, arithmetic and copies ran while one was open for 0% of the time, Pallas kernels for 9%

profile of v8, /device:TPU:1, one launch (start us, length us, event | category | flops | bytes accessed | tf_op | source)
XLA Modules:
  0.0 65.1 jit_solution(11976486566858761249)
XLA Ops:
  0.6 4.0 %shard_map.86 = (bf16[32,40,128]{2,1,0:T(8,128)(2,1)}, s32[32,128]{1,0:T(8,128)S(1)}, bf16[4,1024,128]{2,1,0:T(8,128)(2,1)S(1)}, bf16[4,128,128]{2,1,0:T(8,128)(...) custom-call(s32[32,128]{1,0:T(8,128)} %bitcast.6, ...), custom_call_target="tpu_custom_call" | custom-call | tf_op jit(solution)/shard_map/pallas_call | solution.py:506
  4.7 8.6 %all-to-all-start = ((bf16[32,40,128]{2,1,0:T(8,128)(2,1)}), bf16[32,40,128]{2,1,0:T(8,128)(2,1)S(1)}, u32[]{:S(2)}, u32[]{:S(2)}) async-start(bf16[32,40,128]{2,1,0:T(8,128)(2,1)} %get-tuple-element.22), calls=%async_computation | async-start | bytes 655360 | tf_op jit(solution)/shard_map/all_to_all | solution.py:525
  13.3 4.9 %shard_map.87 = (f32[512,128]{1,0:T(8,128)S(1)}, f32[8,128]{1,0:T(8,128)S(1)}, f32[8,128]{1,0:T(8,128)S(1)}, bf16[512,128]{1,0:T(8,128)(2,1)S(1)}, bf16[64,512]{1,0:T(8,128)(2,1)S(1)}) custom-call(s32[4096]{0:T(1024)} %bitcast.7, bf16[4,1024,128]{2,1,0:T(8,128)(2,1)S(1)} %get-tuple-element.23.raw_ref, bf16[4,128,128]{2,1,0:T(8,128)(2,1)S(1)} %get-tuple-element.24.res_ref, ...), custom_call_target="tpu_custom_call" | custom-call | tf_op jit(solution)/shard_map/pallas_call | solution.py:506
  18.2 4.7 %all-to-all-done.arr_ref = bf16[32,40,128]{2,1,0:T(8,128)(2,1)S(1)} async-done(((bf16[32,40,128]{2,1,0:T(8,128)(2,1)}), bf16[32,40,128]{2,1,0:T(8,128)(2,1)S(1)}, u32[]{:S(2)}, u32[]{:S(2)}) %all-to-all-start) | async-done | bytes 327712 | tf_op jit(solution)/shard_map/all_to_all | solution.py:525
  22.9 0.3 shard_map.88
  23.2 14.6 %all_to_all.20.arr_ref = f32[8,4,128]{2,1,0:T(4,128)S(1)} all-to-all(f32[8,4,128]{2,1,0:T(4,128)S(1)} %get-tuple-element.33), channel_id=1, replica_groups=mesh['visit'=32,'ccd'=8] {'ccd'}, dimensions={0} | all-to-all | bytes 32768 | tf_op jit(solution)/shard_map/all_to_all | solution.py:525
  37.8 0.7 %shard_map.89 = (f32[8,128]{1,0:T(8,128)S(1)}, bf16[32,48,128]{2,1,0:T(8,128)(2,1)S(1)}) custom-call(f32[8,4,128]{2,1,0:T(4,128)S(1)} %all_to_all.20.arr_ref, f32[32,128]{1,0:T(8,128)S(1)} %get-tuple-element.29.const_ref, bf16[64,512]{1,0:T(8,128)(2,1)S(1)} %get-tuple-element.30.mtw_ref, bf16[512,128]{1,0:T(8,128)(2,1)S(1)} %get-tuple-element.34.mw_ref, ...), custom_call_target="tpu_custom_call" | custom-call | tf_op jit(solution)/shard_map/pallas_call | solution.py:506
  38.5 15.1 %all_to_all.21.arr_ref = bf16[32,48,128]{2,1,0:T(8,128)(2,1)S(1)} all-to-all(bf16[32,48,128]{2,1,0:T(8,128)(2,1)S(1)} %get-tuple-element.36), channel_id=1, replica_groups=mesh['visit'=32,'ccd'=8] {'visit'}, dimensions={0} | all-to-all | bytes 786432 | tf_op jit(solution)/shard_map/all_to_all | solution.py:525
  53.6 0.9 %shard_map.90 = f32[8,2,128]{2,1,0:T(2,128)} custom-call(bf16[32,48,128]{2,1,0:T(8,128)(2,1)S(1)} %all_to_all.21.arr_ref, f32[8,512]{1,0:T(8,128)S(1)} %get-tuple-element.37.b_ref, f32[8,512]{1,0:T(8,128)S(1)} %get-tuple-element.38.den_ref, bf16[64,512]{1,0:T(8,128)(2,1)S(1)} %get-tuple-element.30.mtw_ref, f32[8,128]{1,0:T(8,128)S(1)} %get-tuple-element.31.qb_ref, ...), custom_call_target="tpu_custom_call" | custom-call | tf_op jit(solution)/shard_map/pallas_call | solution.py:506
  54.5 3.3 %all-to-all-start.3 = ((f32[8,2,128]{2,1,0:T(2,128)}), f32[8,2,128]{2,1,0:T(2,128)S(1)}, u32[]{:S(2)}, u32[]{:S(2)}) async-start(f32[8,2,128]{2,1,0:T(2,128)} %shard_map.90), calls=%async_computation.3 | async-start | bytes 16384 | tf_op jit(solution)/shard_map/all_to_all | solution.py:525
  57.8 0.9 %shard_map.91 = (f32[16,128]{1,0:T(8,128)}, f32[8,8,128]{2,1,0:T(8,128)S(1)}) custom-call(bf16[32,48,128]{2,1,0:T(8,128)(2,1)S(1)} %all_to_all.21.arr_ref, f32[8,512]{1,0:T(8,128)S(1)} %get-tuple-element.38.den_ref, f32[8,128]{1,0:T(8,128)S(1)} %get-tuple-element.39.sy_ref, f32[32,128]{1,0:T(8,128)S(1)} %get-tuple-element.29.const_ref), custom_call_target="tpu_custom_call" | custom-call | tf_op jit(solution)/shard_map/pallas_call | solution.py:506
  58.7 5.7 %all-to-all-done.3.arr_ref = f32[8,2,128]{2,1,0:T(2,128)S(1)} async-done(((f32[8,2,128]{2,1,0:T(2,128)}), f32[8,2,128]{2,1,0:T(2,128)S(1)}, u32[]{:S(2)}, u32[]{:S(2)}) %all-to-all-start.3) | async-done | bytes 8224 | tf_op jit(solution)/shard_map/all_to_all | solution.py:525
  64.3 0.7 %shard_map.92 = f32[4,64]{1,0:T(4,128)} custom-call(f32[8,2,128]{2,1,0:T(2,128)S(1)} %all-to-all-done.3.arr_ref, f32[8,8,128]{2,1,0:T(8,128)S(1)} %get-tuple-element.40.inv_ref, f32[32,128]{1,0:T(8,128)S(1)} %get-tuple-element.29.const_ref), custom_call_target="tpu_custom_call" | custom-call | tf_op jit(solution)/shard_map/pallas_call | solution.py:506
Async XLA Ops:
  4.7 18.2 %all-to-all-start = ((bf16[32,40,128]{2,1,0:T(8,128)(2,1)}), bf16[32,40,128]{2,1,0:T(8,128)(2,1)S(1)}, u32[]{:S(2)}, u32[]{:S(2)}) async-start(bf16[32,40,128]{2,1,0:T(8,128)(2,1)} %get-tuple-element.22), calls=%async_computation | async-start | bytes 655360 | tf_op jit(solution)/shard_map/all_to_all | solution.py:525
  54.5 9.8 %all-to-all-start.3 = ((f32[8,2,128]{2,1,0:T(2,128)}), f32[8,2,128]{2,1,0:T(2,128)S(1)}, u32[]{:S(2)}, u32[]{:S(2)}) async-start(f32[8,2,128]{2,1,0:T(2,128)} %shard_map.90), calls=%async_computation.3 | async-start | bytes 16384 | tf_op jit(solution)/shard_map/all_to_all | solution.py:525

commit v9 on v8

--- a/solution.py
+++ b/solution.py
@@ -449,7 +449,7 @@
         pay_ref[i, rows : rows + P_DEV] = corrected[P_DEV * i : P_DEV * (i + 1)].astype(BF16)
 
 
-def second_kernel(arr_ref, b_ref, den_ref, mtw_ref, qb_ref, const_ref, pay_ref):
+def second_kernel(arr_ref, b_ref, den_ref, mtw_ref, qb_ref, const_ref, pay_ref, lam_ref):
     blocks = b_ref.shape[1] // 128
     total = senders_sum(arr_ref, 0, ORDER * blocks)
     model = jnp.concatenate(
@@ -457,39 +457,34 @@
     )
     lam = const_ref[LAM_SUB][:, 0:1]
     mom = moments_block(mtw_ref, b_ref[...] - lam * model / den_ref[...], qb_ref[...])
+    lam_ref[...] = const_ref[LAM_LANE]
     block = stack(pack(mom))[: pay_ref.shape[1]]
     for i in range(pay_ref.shape[0]):
         pay_ref[i] = block
 
 
-def background_kernel(vis, arr_ref, den_ref, sy_ref, const_ref, out_ref, inv_ref):
-    rows = arr_ref.shape[1] - P_DEV
-    sums = senders_sum(arr_ref, rows, rows + P_DEV)
-    own = lax.axis_index("visit") * P_DEV
-    width = den_ref.shape[1]
-    pick = iota((P_DEV, width), 1) == iota((P_DEV, width), 0) + own
-    den = dot_t(jnp.where(pick, 1.0, 0.0), den_ref[...], HI)
-    out_ref[...] = sums / den[:, 0:1]
-    sub = iota((ORDER, 128), 0)
-    unit = [jnp.where(sub == b, 1.0, 0.0) for b in range(ORDER)]
-    inverse = eliminate(systems(sy_ref[...], const_ref[LAM_LANE], vis), unit)
-    for b in range(ORDER):
-        inv_ref[b] = inverse[b]
-
-
-def final_kernel(arr_ref, inv_ref, const_ref, out_ref):
+def final_kernel(
+    arr_ref, sums_ref, den_ref, sy_ref, const_ref, lam_ref, out_ref, back_ref
+):
     vis = out_ref.shape[0]
     n = vis * ORDER
     total = arr_ref[0]
     for i in range(1, arr_ref.shape[0]):
         total = total + arr_ref[i]
     mom = unpack([total[i : i + 1] for i in range(ORDER // 4)])
-    z = inv_ref[0] * mom[0]
-    for d in range(1, ORDER):
-        z = z + inv_ref[d] * mom[d]
+    z = solve(mom, sy_ref[...], lam_ref[...], vis)
     flat = tile_rows(z, ORDER).T[:n] * tile_rows(const_ref[ROT][:, : ORDER * ORDER], vis)
     for v in range(vis):
         out_ref[v : v + 1] = jnp.sum(flat[v * ORDER : (v + 1) * ORDER], axis=0, keepdims=True)
+    rows = sums_ref.shape[1] - P_DEV
+    sums = senders_sum(sums_ref, rows, rows + P_DEV)
+    own = lax.axis_index("visit") * P_DEV
+    width = den_ref.shape[1]
+    pick = iota((P_DEV, width), 1) == iota((P_DEV, width), 0) + own
+    d_hi, d_lo = split(den_ref[...], 2)
+    pick = jnp.where(pick, 1.0, 0.0).astype(BF16)
+    den = dot_t(pick, d_hi) + dot_t(pick, d_lo)
+    back_ref[...] = sums / den[:, 0:1]
 
 
 def call(kernel, out_shape, scratch=(), n_in=1, hbm=(), smem=()):
@@ -606,16 +601,15 @@
         n_in=5,
     )(arr2, const, mtw, mw, tsum)
     arr3 = exchange(pay3, "visit")
-    pay4 = call(second_kernel, shape((ccd_devs, ORDER // 4, 128)), n_in=6)(
+    pay4, lam = call(
+        second_kernel, (shape((ccd_devs, ORDER // 4, 128)), shape((ORDER, 128))), n_in=6
+    )(
         arr3, back, den, mtw, qb, const
     )
     arr4 = exchange(pay4, "ccd")
-    background, inverse = call(
-        functools.partial(background_kernel, vis),
-        (result((P_DEV, pix)), shape((ORDER, ORDER, 128))),
-        n_in=4,
-    )(arr3, den, sy_all, const)
-    offsets = call(final_kernel, result((vis, ORDER * ORDER)), n_in=3)(arr4, inverse, const)
+    offsets, background = call(
+        final_kernel, (result((vis, ORDER * ORDER)), result((P_DEV, pix))), n_in=6
+    )(arr4, arr3, den, sy_all, const, lam)
     return offsets, background
 
 

time: 65.6 us -> 64.1 us (0.977)
  blocking collectives: 29.7 us -> 38.7 us
  waiting for transfers between devices: 10.4 us -> 4.69 us
  starting transfers between devices: 11.9 us -> 8.59 us
  Pallas kernels: 12.4 us -> 11.1 us
    all_to_all x2 -> x3, blocking collectives: 29.7 us -> 38.7 us  [exchange(): return lax.all_to_all(x, axis, split_axis=0, concat_axis=0, tiled=True)]
    all_to_all x2 -> x1, waiting for transfers between devices: 10.4 us -> 4.69 us  [exchange(): return lax.all_to_all(x, axis, split_axis=0, concat_axis=0, tiled=True)]
    all_to_all x2 -> x1, starting transfers between devices: 11.9 us -> 8.59 us  [exchange(): return lax.all_to_all(x, axis, split_axis=0, concat_axis=0, tiled=True)]
    pallas_call x7 -> x6, Pallas kernels: 12.4 us -> 11.1 us  [run(): fn(*(x if i in spec else pltpu.with_memory_space_constraint(x, pltpu.VMEM...]
  transfers between devices with their start and end apart: 2 -> 1, of which waited for: 2 -> 1; matrix products, arithmetic and copies ran while one was open for 0% -> 0% of each run, Pallas kernels for 9% -> 8%
where the time goes in v9:
time: 64.1 us; the launch traced here: 63.7 us
  blocking collectives  38.7 us (60%)
  Pallas kernels  11.1 us (17%)
  starting transfers between devices  8.59 us (13%)
  waiting for transfers between devices  4.69 us (7%)
  between operations  0.66 us (1%)
    all_to_all x3, blocking collectives, exchange(): return lax.all_to_all(x, axis, split_axis=0, concat_axis=0, tiled=True)  38.7 us
    pallas_call x6, Pallas kernels, run(): fn(*(x if i in spec else pltpu.with_memory_space_constraint(x, pltpu.VMEM...  11.1 us
    all_to_all x1, starting transfers between devices, exchange(): return lax.all_to_all(x, axis, split_axis=0, concat_axis=0, tiled=True)  8.59 us
    all_to_all x1, waiting for transfers between devices, exchange(): return lax.all_to_all(x, axis, split_axis=0, concat_axis=0, tiled=True)  4.69 us
  transfers between devices with their start and end apart: 1, of which 1 were waited for; matrix products, arithmetic and copies ran while one was open for 0% of the time, Pallas kernels for 8%

profile of v9, /device:TPU:1, one launch (start us, length us, event | category | flops | bytes accessed | tf_op | source)
XLA Modules:
  0.0 63.7 jit_solution(7216787625985552778)
XLA Ops:
  0.6 4.0 %shard_map.86 = (bf16[32,40,128]{2,1,0:T(8,128)(2,1)}, s32[32,128]{1,0:T(8,128)S(1)}, bf16[4,1024,128]{2,1,0:T(8,128)(2,1)S(1)}, bf16[4,128,128]{2,1,0:T(8,128)(...) custom-call(s32[32,128]{1,0:T(8,128)} %bitcast.6, ...), custom_call_target="tpu_custom_call" | custom-call | tf_op jit(solution)/shard_map/pallas_call | solution.py:501
  4.7 8.6 %all-to-all-start = ((bf16[32,40,128]{2,1,0:T(8,128)(2,1)}), bf16[32,40,128]{2,1,0:T(8,128)(2,1)S(1)}, u32[]{:S(2)}, u32[]{:S(2)}) async-start(bf16[32,40,128]{2,1,0:T(8,128)(2,1)} %get-tuple-element.22), calls=%async_computation | async-start | bytes 655360 | tf_op jit(solution)/shard_map/all_to_all | solution.py:520
  13.3 4.9 %shard_map.87 = (f32[512,128]{1,0:T(8,128)S(1)}, f32[8,128]{1,0:T(8,128)S(1)}, f32[8,128]{1,0:T(8,128)S(1)}, bf16[512,128]{1,0:T(8,128)(2,1)S(1)}, bf16[64,512]{1,0:T(8,128)(2,1)S(1)}) custom-call(s32[4096]{0:T(1024)} %bitcast.7, bf16[4,1024,128]{2,1,0:T(8,128)(2,1)S(1)} %get-tuple-element.23.raw_ref, bf16[4,128,128]{2,1,0:T(8,128)(2,1)S(1)} %get-tuple-element.24.res_ref, ...), custom_call_target="tpu_custom_call" | custom-call | tf_op jit(solution)/shard_map/pallas_call | solution.py:501
  18.2 4.7 %all-to-all-done.arr_ref = bf16[32,40,128]{2,1,0:T(8,128)(2,1)S(1)} async-done(((bf16[32,40,128]{2,1,0:T(8,128)(2,1)}), bf16[32,40,128]{2,1,0:T(8,128)(2,1)S(1)}, u32[]{:S(2)}, u32[]{:S(2)}) %all-to-all-start) | async-done | bytes 327712 | tf_op jit(solution)/shard_map/all_to_all | solution.py:520
  22.9 0.3 shard_map.88
  23.2 14.6 %all_to_all.20.arr_ref = f32[8,4,128]{2,1,0:T(4,128)S(1)} all-to-all(f32[8,4,128]{2,1,0:T(4,128)S(1)} %get-tuple-element.33), channel_id=1, replica_groups=mesh['visit'=32,'ccd'=8] {'ccd'}, dimensions={0} | all-to-all | bytes 32768 | tf_op jit(solution)/shard_map/all_to_all | solution.py:520
  37.8 0.7 %shard_map.89 = (f32[8,128]{1,0:T(8,128)S(1)}, bf16[32,48,128]{2,1,0:T(8,128)(2,1)S(1)}) custom-call(f32[8,4,128]{2,1,0:T(4,128)S(1)} %all_to_all.20.arr_ref, f32[32,128]{1,0:T(8,128)S(1)} %get-tuple-element.29.const_ref, bf16[64,512]{1,0:T(8,128)(2,1)S(1)} %get-tuple-element.30.mtw_ref, bf16[512,128]{1,0:T(8,128)(2,1)S(1)} %get-tuple-element.34.mw_ref, ...), custom_call_target="tpu_custom_call" | custom-call | tf_op jit(solution)/shard_map/pallas_call | solution.py:501
  38.5 15.1 %all_to_all.21.arr_ref.sums_ref = bf16[32,48,128]{2,1,0:T(8,128)(2,1)S(1)} all-to-all(bf16[32,48,128]{2,1,0:T(8,128)(2,1)S(1)} %get-tuple-element.36), channel_id=1, replica_groups=mesh['visit'=32,'ccd'=8] {'visit'}, dimensions={0} | all-to-all | bytes 786432 | tf_op jit(solution)/shard_map/all_to_all | solution.py:520
  53.6 0.3 shard_map.90
  53.9 8.9 %all_to_all.22.arr_ref = f32[8,2,128]{2,1,0:T(2,128)S(1)} all-to-all(f32[8,2,128]{2,1,0:T(2,128)S(1)} %get-tuple-element.39), channel_id=1, replica_groups=mesh['visit'=32,'ccd'=8] {'ccd'}, dimensions={0} | all-to-all | bytes 16384 | tf_op jit(solution)/shard_map/all_to_all | solution.py:520
  62.8 0.8 %shard_map.91 = (f32[4,64]{1,0:T(4,128)}, f32[16,128]{1,0:T(8,128)}) custom-call(f32[8,2,128]{2,1,0:T(2,128)S(1)} %all_to_all.22.arr_ref, bf16[32,48,128]{2,1,0:T(8,128)(2,1)S(1)} %all_to_all.21.arr_ref.sums_ref, f32[8,512]{1,0:T(8,128)S(1)} %get-tuple-element.38.den_ref, f32[8,128]{1,0:T(8,128)S(1)} %get-tuple-element.40.sy_ref, ...), custom_call_target="tpu_custom_call" | custom-call | tf_op jit(solution)/shard_map/pallas_call | solution.py:501
Async XLA Ops:
  4.7 18.2 %all-to-all-start = ((bf16[32,40,128]{2,1,0:T(8,128)(2,1)}), bf16[32,40,128]{2,1,0:T(8,128)(2,1)S(1)}, u32[]{:S(2)}, u32[]{:S(2)}) async-start(bf16[32,40,128]{2,1,0:T(8,128)(2,1)} %get-tuple-element.22), calls=%async_computation | async-start | bytes 655360 | tf_op jit(solution)/shard_map/all_to_all | solution.py:520

commit v10 on v9

--- a/solution.py
+++ b/solution.py
@@ -123,7 +123,7 @@
         hot_sc[j], member_sc[j] = operands(j)
         return carry
 
-    early = blocks // 2
+    early = blocks // 4
     lax.fori_loop(0, early * group, build, 0, unroll=UNROLL_W)
     for copy in raw_copies:
         copy.wait()
@@ -556,8 +556,8 @@
             pltpu.VMEM((owners, slots), F32),
             pltpu.VMEM((owners, slots), F32),
             pltpu.VMEM((owners, slots), F32),
-            pltpu.VMEM((owners // 2, 256, slots), BF16),
-            pltpu.VMEM((owners // 2, 128, slots), BF16),
+            pltpu.VMEM((owners // 4, 256, slots), BF16),
+            pltpu.VMEM((owners // 4, 128, slots), BF16),
             pltpu.VMEM((blocks, 4 * ORDER, 128), F32),
             pltpu.SemaphoreType.DMA((6 + vis,)),
         ),

time: 64.1 us -> 64 us (level)
  no operation moved by 1% of the time
where the time goes in v10:
time: 64 us; the launch traced here: 63.5 us
  blocking collectives  38.7 us (60%)
  Pallas kernels  10.9 us (17%)
  starting transfers between devices  8.59 us (13%)
  waiting for transfers between devices  4.7 us (7%)
  between operations  0.66 us (1%)
    all_to_all x3, blocking collectives, exchange(): return lax.all_to_all(x, axis, split_axis=0, concat_axis=0, tiled=True)  38.7 us
    pallas_call x6, Pallas kernels, run(): fn(*(x if i in spec else pltpu.with_memory_space_constraint(x, pltpu.VMEM...  10.9 us
    all_to_all x1, starting transfers between devices, exchange(): return lax.all_to_all(x, axis, split_axis=0, concat_axis=0, tiled=True)  8.59 us
    all_to_all x1, waiting for transfers between devices, exchange(): return lax.all_to_all(x, axis, split_axis=0, concat_axis=0, tiled=True)  4.7 us
  transfers between devices with their start and end apart: 1, of which 1 were waited for; matrix products, arithmetic and copies ran while one was open for 0% of the time, Pallas kernels for 8%

profile of v10, /device:TPU:1, one launch (start us, length us, event | category | flops | bytes accessed | tf_op | source)
XLA Modules:
  0.0 63.5 jit_solution(13757454878526980186)
XLA Ops:
  0.6 3.8 %shard_map.86 = (bf16[32,40,128]{2,1,0:T(8,128)(2,1)}, s32[32,128]{1,0:T(8,128)S(1)}, bf16[4,1024,128]{2,1,0:T(8,128)(2,1)S(1)}, bf16[4,128,128]{2,1,0:T(8,128)(...) custom-call(s32[32,128]{1,0:T(8,128)} %bitcast.6, ...), custom_call_target="tpu_custom_call" | custom-call | tf_op jit(solution)/shard_map/pallas_call | solution.py:501
  4.5 8.6 %all-to-all-start = ((bf16[32,40,128]{2,1,0:T(8,128)(2,1)}), bf16[32,40,128]{2,1,0:T(8,128)(2,1)S(1)}, u32[]{:S(2)}, u32[]{:S(2)}) async-start(bf16[32,40,128]{2,1,0:T(8,128)(2,1)} %get-tuple-element.22), calls=%async_computation | async-start | bytes 655360 | tf_op jit(solution)/shard_map/all_to_all | solution.py:520
  13.1 4.9 %shard_map.87 = (f32[512,128]{1,0:T(8,128)S(1)}, f32[8,128]{1,0:T(8,128)S(1)}, f32[8,128]{1,0:T(8,128)S(1)}, bf16[512,128]{1,0:T(8,128)(2,1)S(1)}, bf16[64,512]{1,0:T(8,128)(2,1)S(1)}) custom-call(s32[4096]{0:T(1024)} %bitcast.7, bf16[4,1024,128]{2,1,0:T(8,128)(2,1)S(1)} %get-tuple-element.23.raw_ref, bf16[4,128,128]{2,1,0:T(8,128)(2,1)S(1)} %get-tuple-element.24.res_ref, ...), custom_call_target="tpu_custom_call" | custom-call | tf_op jit(solution)/shard_map/pallas_call | solution.py:501
  18.0 4.7 %all-to-all-done.arr_ref = bf16[32,40,128]{2,1,0:T(8,128)(2,1)S(1)} async-done(((bf16[32,40,128]{2,1,0:T(8,128)(2,1)}), bf16[32,40,128]{2,1,0:T(8,128)(2,1)S(1)}, u32[]{:S(2)}, u32[]{:S(2)}) %all-to-all-start) | async-done | bytes 327712 | tf_op jit(solution)/shard_map/all_to_all | solution.py:520
  22.7 0.3 shard_map.88
  23.0 14.6 %all_to_all.20.arr_ref = f32[8,4,128]{2,1,0:T(4,128)S(1)} all-to-all(f32[8,4,128]{2,1,0:T(4,128)S(1)} %get-tuple-element.33), channel_id=1, replica_groups=mesh['visit'=32,'ccd'=8] {'ccd'}, dimensions={0} | all-to-all | bytes 32768 | tf_op jit(solution)/shard_map/all_to_all | solution.py:520
  37.6 0.7 %shard_map.89 = (f32[8,128]{1,0:T(8,128)S(1)}, bf16[32,48,128]{2,1,0:T(8,128)(2,1)S(1)}) custom-call(f32[8,4,128]{2,1,0:T(4,128)S(1)} %all_to_all.20.arr_ref, f32[32,128]{1,0:T(8,128)S(1)} %get-tuple-element.29.const_ref, bf16[64,512]{1,0:T(8,128)(2,1)S(1)} %get-tuple-element.30.mtw_ref, bf16[512,128]{1,0:T(8,128)(2,1)S(1)} %get-tuple-element.34.mw_ref, ...), custom_call_target="tpu_custom_call" | custom-call | tf_op jit(solution)/shard_map/pallas_call | solution.py:501
  38.3 15.1 %all_to_all.21.arr_ref.sums_ref = bf16[32,48,128]{2,1,0:T(8,128)(2,1)S(1)} all-to-all(bf16[32,48,128]{2,1,0:T(8,128)(2,1)S(1)} %get-tuple-element.36), channel_id=1, replica_groups=mesh['visit'=32,'ccd'=8] {'visit'}, dimensions={0} | all-to-all | bytes 786432 | tf_op jit(solution)/shard_map/all_to_all | solution.py:520
  53.4 0.3 shard_map.90
  53.7 8.9 %all_to_all.22.arr_ref = f32[8,2,128]{2,1,0:T(2,128)S(1)} all-to-all(f32[8,2,128]{2,1,0:T(2,128)S(1)} %get-tuple-element.39), channel_id=1, replica_groups=mesh['visit'=32,'ccd'=8] {'ccd'}, dimensions={0} | all-to-all | bytes 16384 | tf_op jit(solution)/shard_map/all_to_all | solution.py:520
  62.6 0.8 %shard_map.91 = (f32[4,64]{1,0:T(4,128)}, f32[16,128]{1,0:T(8,128)}) custom-call(f32[8,2,128]{2,1,0:T(2,128)S(1)} %all_to_all.22.arr_ref, bf16[32,48,128]{2,1,0:T(8,128)(2,1)S(1)} %all_to_all.21.arr_ref.sums_ref, f32[8,512]{1,0:T(8,128)S(1)} %get-tuple-element.38.den_ref, f32[8,128]{1,0:T(8,128)S(1)} %get-tuple-element.40.sy_ref, ...), custom_call_target="tpu_custom_call" | custom-call | tf_op jit(solution)/shard_map/pallas_call | solution.py:501
Async XLA Ops:
  4.5 18.2 %all-to-all-start = ((bf16[32,40,128]{2,1,0:T(8,128)(2,1)}), bf16[32,40,128]{2,1,0:T(8,128)(2,1)S(1)}, u32[]{:S(2)}, u32[]{:S(2)}) async-start(bf16[32,40,128]{2,1,0:T(8,128)(2,1)} %get-tuple-element.22), calls=%async_computation | async-start | bytes 655360 | tf_op jit(solution)/shard_map/all_to_all | solution.py:520
